TPU v7x, 32 devices: a whole 2x2x4 slice. The times are simulated.
32 devices in a mesh: group: 2 (over y), seq: 4 (over z), head: 2 (over x), sub: 2 (over core).
Axes of the slice: x: 2, y: 2, z: 4, core: 2. Of those that a mesh axis runs over, the one named last changes fastest.
Arguments:
- query_rows: bfloat16 [4096, 2048], P(('group', 'seq', 'head', 'sub')), parts along dimension 0, may hold values from -6 to 6
- key_rows: bfloat16 [4096, 2048], P(('group', 'seq', 'head', 'sub')), parts along dimension 0, may hold values from -6 to 6
- value_rows: bfloat16 [4096, 2048], P(('group', 'seq', 'head', 'sub')), parts along dimension 0, may hold values from -6 to 6
- grad_out: bfloat16 [4096, 2048], P(('group', 'seq', 'head', 'sub')), parts along dimension 0, may hold values from -6 to 6
Outputs:
- normed_out: bfloat16 [4096, 2048], P(('group', 'seq', 'head', 'sub')), parts along dimension 0
- grad_query: bfloat16 [4096, 2048], P(('group', 'seq', 'head', 'sub')), parts along dimension 0
- grad_key: bfloat16 [4096, 2048], P(('group', 'seq', 'head', 'sub')), parts along dimension 0
- grad_value: bfloat16 [4096, 2048], P(('group', 'seq', 'head', 'sub')), parts along dimension 0
There are 2 independent parts, one for each index of `group`. A program takes and returns all parts, laid end to end along the dimension named above; each array names one. Nothing has to cross between parts.
All inputs are finite; a program needn't handle non-finite values.
Results may differ from a plain program's by a relative error of at most 0.0059.
Values may be sent and summed in bfloat16 or wider, within the bound.
No kernel may reach another device: no remote copies, remote signals or barrier semaphores. Data moves between devices by JAX's collectives and lax.ppermute only.
A program may use at most 64 MiB of HBM per device.

v0:
```python
import jax
import jax.numpy as jnp
from jax import lax
from jax.sharding import PartitionSpec as P

HEAD_DIM = 128
BLOCK = 128


EPSILON = 1e-05


def carried_in(value, axis, combine, identity, reverse):
    length, mine = (lax.axis_size(axis), lax.axis_index(axis))
    everything = lax.all_gather(value, axis)
    start = jnp.broadcast_to(jnp.asarray(identity, value.dtype), value.shape)

    def turn(k, before):
        at = length - 1 - k if reverse else k
        reached = at > mine if reverse else at < mine
        new = combine(before, everything[at])
        return jnp.where(reached, new, before)

    return lax.fori_loop(0, length, turn, start)


def add_tiles(earlier_part, later_part):
    return earlier_part + later_part


def chain_before(tiles):
    return carried_in(tiles, "seq", add_tiles, jnp.zeros_like(tiles), False)


def chain_after(tiles):
    return carried_in(tiles, "seq", add_tiles, jnp.zeros_like(tiles), True)


def on_device(query_rows, key_rows, value_rows, grad_out):
    queries, key_vals, value_vals, cotangent = (
        lax.all_to_all(query_rows, ("head", "sub"), split_axis=1, concat_axis=0, tiled=True),
        lax.all_to_all(key_rows, ("head", "sub"), split_axis=1, concat_axis=0, tiled=True),
        lax.all_to_all(value_rows, ("head", "sub"), split_axis=1, concat_axis=0, tiled=True),
        lax.all_to_all(grad_out, ("head", "sub"), split_axis=1, concat_axis=0, tiled=True),
    )
    rows = queries.shape[0]
    local_heads = queries.shape[1] // HEAD_DIM
    blocks = rows // BLOCK

    def split(array):
        return array.reshape(blocks, BLOCK, local_heads, HEAD_DIM)

    query_blk = split(queries)
    key_blk = split(key_vals)
    value_blk = split(value_vals)
    grad_blk = split(cotangent)
    causal = lax.iota(jnp.int32, BLOCK)[:, None] >= lax.iota(jnp.int32, BLOCK)[None, :]
    f32 = jnp.float32
    scores = jnp.einsum("nthe,nshe->nhts", query_blk, key_blk, preferred_element_type=f32)
    probs = jnp.where(causal, scores, 0.0).astype(jnp.bfloat16)
    block_kv = jnp.einsum("nshe,nshf->nhef", key_blk, value_blk, preferred_element_type=f32)
    own_total = jnp.sum(block_kv, axis=0)
    earlier = chain_before(own_total)
    inner_prefix = jnp.cumsum(
        jnp.concatenate([jnp.zeros_like(block_kv[:1]), block_kv[:-1]], axis=0), axis=0
    )
    state_low = (earlier[None] + inner_prefix).astype(jnp.bfloat16)
    unnormed = jnp.einsum("nhts,nshf->nthf", probs, value_blk, preferred_element_type=f32)
    unnormed = unnormed + jnp.einsum(
        "nthe,nhef->nthf", query_blk, state_low, preferred_element_type=f32
    )
    norm_scale = jnp.sqrt(jnp.mean(unnormed * unnormed, axis=-1, keepdims=True) + EPSILON)
    normed = unnormed / norm_scale
    grad_float = grad_blk.astype(f32)
    grad_raw = (
        (grad_float - normed * jnp.mean(grad_float * normed, axis=-1, keepdims=True)) / norm_scale
    ).astype(jnp.bfloat16)
    block_qd = jnp.einsum("nthe,nthf->nhef", query_blk, grad_raw, preferred_element_type=f32)
    own_grad = jnp.sum(block_qd, axis=0)
    later = chain_after(own_grad)
    shifted = jnp.concatenate([block_qd[1:], jnp.zeros_like(block_qd[:1])], axis=0)
    inner_suffix = jnp.cumsum(shifted[::-1], axis=0)[::-1]
    grad_state = (later[None] + inner_suffix).astype(jnp.bfloat16)
    grad_scores = jnp.einsum("nthf,nshf->nhts", grad_raw, value_blk, preferred_element_type=f32)
    grad_probs = jnp.where(causal, grad_scores, 0.0).astype(jnp.bfloat16)
    grad_q = jnp.einsum("nhts,nshe->nthe", grad_probs, key_blk, preferred_element_type=f32)
    grad_q = grad_q + jnp.einsum("nthf,nhef->nthe", grad_raw, state_low, preferred_element_type=f32)
    grad_k = jnp.einsum("nhts,nthe->nshe", grad_probs, query_blk, preferred_element_type=f32)
    grad_k = grad_k + jnp.einsum(
        "nshf,nhef->nshe", value_blk, grad_state, preferred_element_type=f32
    )
    grad_v = jnp.einsum("nhts,nthf->nshf", probs, grad_raw, preferred_element_type=f32)
    grad_v = grad_v + jnp.einsum("nshe,nhef->nshf", key_blk, grad_state, preferred_element_type=f32)

    def merge_rows(array):
        return array.astype(jnp.bfloat16).reshape(rows, local_heads * HEAD_DIM)

    results = (
        lax.all_to_all(
            merge_rows(normed), ("head", "sub"), split_axis=0, concat_axis=1, tiled=True
        ),
        lax.all_to_all(
            merge_rows(grad_q), ("head", "sub"), split_axis=0, concat_axis=1, tiled=True
        ),
        lax.all_to_all(
            merge_rows(grad_k), ("head", "sub"), split_axis=0, concat_axis=1, tiled=True
        ),
        lax.all_to_all(
            merge_rows(grad_v), ("head", "sub"), split_axis=0, concat_axis=1, tiled=True
        ),
    )
    return (results[0], results[1], results[2], results[3])


def solution(mesh):
    placed = (
        P(("group", "seq", "head", "sub"), None),
        P(("group", "seq", "head", "sub"), None),
        P(("group", "seq", "head", "sub"), None),
        P(("group", "seq", "head", "sub"), None),
    )
    return jax.shard_map(
        on_device,
        mesh=mesh,
        in_specs=placed,
        out_specs=(
            P(("group", "seq", "head", "sub"), None),
            P(("group", "seq", "head", "sub"), None),
            P(("group", "seq", "head", "sub"), None),
            P(("group", "seq", "head", "sub"), None),
        ),
        check_vma=False,
    )
```

profile of v0, /device:TPU:0, one launch (start us, length us, event | category | flops | bytes accessed | tf_op | source)
XLA Modules:
  0.0 152.5 jit_solution(3516820080660549750)
XLA Ops:
  7.2 2.0 %copy.47 = bf16[128,2048]{0,1:T(8,128)(2,1)} copy(bf16[128,2048]{1,0:T(8,128)(2,1)} %param.9) | data formatting | bytes 1048576 | tf_op args[1]
  9.2 4.3 %all-to-all-start.1 = ((bf16[128,4,512]{0,2,1:T(8,128)(2,1)}), bf16[128,4,512]{0,2,1:T(8,128)(2,1)S(1)}, u32[]{:S(2)}, u32[]{:S(2)}) async-start(bf16[128,4,512]{0,2,1:T(8,128)(2,1)} %bitcast.3), calls=%async_computation.1 | async-start | bytes 1048576 | tf_op jit(solution)/shard_map/all_to_all | solution.py:42
  13.8 8.6 %all-to-all-done.1 = bf16[128,4,512]{0,2,1:T(8,128)(2,1)S(1)} async-done(((bf16[128,4,512]{0,2,1:T(8,128)(2,1)}), bf16[128,4,512]{0,2,1:T(8,128)(2,1)S(1)}, u32[]{:S(2)}, u32[]{:S(2)}) %all-to-all-start.1) | async-done | bytes 524320 | tf_op jit(solution)/shard_map/all_to_all | solution.py:42
  22.4 11.2 %all_to_all.137 = bf16[128,4,512]{0,2,1:T(8,128)(2,1)S(1)} all-to-all(bf16[128,4,512]{0,2,1:T(8,128)(2,1)S(1)} %bitcast.112), channel_id=1, replica_groups=mesh['group'=2,'seq'=4,'head'=2,'sub'=2] {'head','sub'}, dimensions={1} | all-to-all | bytes 1048576 | tf_op jit(solution)/shard_map/all_to_all | solution.py:43
  35.8 3.5 %all-to-all-start = ((bf16[128,4,512]{0,2,1:T(8,128)(2,1)}), bf16[128,4,512]{0,2,1:T(8,128)(2,1)S(1)}, u32[]{:S(2)}, u32[]{:S(2)}) async-start(bf16[128,4,512]{0,2,1:T(8,128)(2,1)} %bitcast), calls=%async_computation | async-start | bytes 1048576 | tf_op jit(solution)/shard_map/all_to_all | solution.py:41
  39.3 2.0 %copy.82 = bf16[128,2048]{0,1:T(8,128)(2,1)} copy(bf16[128,2048]{1,0:T(8,128)(2,1)} %param.11) | data formatting | bytes 1048576 | tf_op jit(solution)/shard_map/all_to_all | solution.py:44
  41.4 6.7 %all-to-all-done = bf16[128,4,512]{0,2,1:T(8,128)(2,1)S(1)} async-done(((bf16[128,4,512]{0,2,1:T(8,128)(2,1)}), bf16[128,4,512]{0,2,1:T(8,128)(2,1)S(1)}, u32[]{:S(2)}, u32[]{:S(2)}) %all-to-all-start) | async-done | bytes 524320 | tf_op jit(solution)/shard_map/all_to_all | solution.py:41
  48.1 4.1 %all-to-all-start.4 = ((bf16[128,4,512]{0,2,1:T(8,128)(2,1)}), bf16[128,4,512]{0,2,1:T(8,128)(2,1)}, u32[]{:S(2)}, u32[]{:S(2)}) async-start(bf16[128,4,512]{0,2,1:T(8,128)(2,1)} %bitcast.108), calls=%async_computation.4 | async-start | bytes 1048576 | tf_op jit(solution)/shard_map/all_to_all | solution.py:44
  53.5 1.5 convolution_bitcast_fusion.6
  55.0 9.0 %all-gather.5.cloned.1.call-done = f32[16,128,128]{2,1,0:T(8,128)} async-done(((f32[4,128,128]{2,1,0:T(8,128)}), f32[16,128,128]{2,1,0:T(8,128)}) %all-gather.5.cloned.1.call-update) | async-done | bytes 1048592 | tf_op jit(solution)/shard_map/all_gather | solution.py:15
  63.9 4.2 %while.30 = (s32[]{:T(128)}, f32[4,128,128]{2,1,0:T(8,128)S(1)}, s32[]{:T(128)}, f32[4,4,128,128]{3,2,1,0:T(8,128)}, s32[]{:T(128)}, /*index=5*/s32[]{:T(128)}) while((s32[]{:T(128)}, f32[4,128,128]{2,1,0:T(8,128)S(1)}, s32[]{:T(128)}, f32[4,4,128,128]{3,2,1,0:T(8,128)}, s32[]{:T(128)}, /*index=5*/s32[]{:T(128)}) %tuple.86), condition=%wide.region_2.3_spmd.clone, body=%wide.region_1.2_spmd.clone.sunk | while | flops 196612 | bytes 786525 | solution.py:24
  71.4 2.1 %divide_convert_fusion = (bf16[4,128,4,128]{1,3,2,0:T(8,128)(2,1)S(1)}, bf16[4,128,4,128]{1,3,2,0:T(8,128)(2,1)}) fusion(f32[4,128,4]{1,2,0:T(4,128)S(1)} %broadcast_multiply_fusion, f32[4,128,4]{1,2,0:T(4,128)S(1)} %add_sqrt_fusion, bf16[128,4,512]{0,2,1:T(8,128)(2,1)} %all-to-all-done.4, f32[4,128,4,128]{1,3,2,0:T(8,128)S(1)} %get-tuple-element.246), kind=kLoop, calls=%fused_computation.23 | loop fusion | flops 1835008 | bytes 2637824 | tf_op jit(solution)/shard_map/convert_element_type | solution.py:77
  78.6 4.3 %all-to-all-start.5 = ((bf16[4,128,512]{1,2,0:T(8,128)(2,1)}), bf16[4,128,512]{1,2,0:T(8,128)(2,1)}, u32[]{:S(2)}, u32[]{:S(2)}) async-start(bf16[4,128,512]{1,2,0:T(8,128)(2,1)} %bitcast.107), calls=%async_computation.5 | async-start | bytes 1048576 | tf_op jit(solution)/shard_map/all_to_all | solution.py:102
  82.9 1.3 fusion.14
  85.3 17.2 %all-gather.7.cloned.1.call-done = f32[16,128,128]{2,1,0:T(8,128)} async-done(((f32[4,128,128]{2,1,0:T(8,128)}), f32[16,128,128]{2,1,0:T(8,128)}) %all-gather.7.cloned.1.call-update) | async-done | bytes 1048592 | tf_op jit(solution)/shard_map/all_gather | solution.py:15
  102.5 4.3 %while.31 = (s32[]{:T(128)}, f32[4,128,128]{2,1,0:T(8,128)S(1)}, s32[]{:T(128)}, f32[4,4,128,128]{3,2,1,0:T(8,128)}, s32[]{:T(128)}, /*index=5*/s32[]{:T(128)}, s32[]{:T(128)}, s32[]{:T(128)}) while((s32[]{:T(128)}, f32[4,128,128]{2,1,0:T(8,128)S(1)}, s32[]{:T(128)}, f32[4,4,128,128]{3,2,1,0:T(8,128)}, s32[]{:T(128)}, ...), condition=%wide.region_8.9_spmd.clone, body=%wide.region_7.8_spmd.clone.sunk | while | flops 196616 | bytes 786587 | solution.py:24
  107.6 3.6 %all-to-all-start.3 = ((bf16[4,128,512]{1,2,0:T(8,128)(2,1)}), bf16[4,128,512]{1,2,0:T(8,128)(2,1)S(1)}, u32[]{:S(2)}, u32[]{:S(2)}) async-start(bf16[4,128,512]{1,2,0:T(8,128)(2,1)} %bitcast.15), calls=%async_computation.3 | async-start | bytes 1048576 | tf_op jit(solution)/shard_map/all_to_all | solution.py:99
  111.2 1.4 add_convert_fusion
  113.9 6.2 %all-to-all-done.3 = bf16[4,128,512]{1,2,0:T(8,128)(2,1)S(1)} async-done(((bf16[4,128,512]{1,2,0:T(8,128)(2,1)}), bf16[4,128,512]{1,2,0:T(8,128)(2,1)S(1)}, u32[]{:S(2)}, u32[]{:S(2)}) %all-to-all-start.3) | async-done | bytes 524320 | tf_op jit(solution)/shard_map/all_to_all | solution.py:99
  120.0 3.5 %all-to-all-start.7 = ((bf16[4,128,512]{1,2,0:T(8,128)(2,1)}), bf16[4,128,512]{1,2,0:T(8,128)(2,1)S(1)}, u32[]{:S(2)}, u32[]{:S(2)}) async-start(bf16[4,128,512]{1,2,0:T(8,128)(2,1)} %bitcast.35), calls=%async_computation.7 | async-start | bytes 1048576 | tf_op jit(solution)/shard_map/all_to_all | solution.py:108
  125.0 7.4 %all-to-all-done.7 = bf16[4,128,512]{1,2,0:T(8,128)(2,1)S(1)} async-done(((bf16[4,128,512]{1,2,0:T(8,128)(2,1)}), bf16[4,128,512]{1,2,0:T(8,128)(2,1)S(1)}, u32[]{:S(2)}, u32[]{:S(2)}) %all-to-all-start.7) | async-done | bytes 524320 | tf_op jit(solution)/shard_map/all_to_all | solution.py:108
  132.3 3.5 %all-to-all-start.6 = ((bf16[4,128,512]{1,2,0:T(8,128)(2,1)}), bf16[4,128,512]{1,2,0:T(8,128)(2,1)S(1)}, u32[]{:S(2)}, u32[]{:S(2)}) async-start(bf16[4,128,512]{1,2,0:T(8,128)(2,1)} %bitcast.31), calls=%async_computation.6 | async-start | bytes 1048576 | tf_op jit(solution)/shard_map/all_to_all | solution.py:105
  135.8 2.0 %copy.83 = bf16[128,2048]{1,0:T(8,128)(2,1)} copy(bf16[128,2048]{0,1:T(8,128)(2,1)} %bitcast.26) | data formatting | bytes 1048576 | tf_op jit(solution)/shard_map/all_to_all | solution.py:102
  139.9 4.8 %all-to-all-done.6 = bf16[4,128,512]{1,2,0:T(8,128)(2,1)S(1)} async-done(((bf16[4,128,512]{1,2,0:T(8,128)(2,1)}), bf16[4,128,512]{1,2,0:T(8,128)(2,1)S(1)}, u32[]{:S(2)}, u32[]{:S(2)}) %all-to-all-start.6) | async-done | bytes 524320 | tf_op jit(solution)/shard_map/all_to_all | solution.py:105
  (62 shorter events, 27.8 us)
Async XLA Ops:
  9.2 4.3 %copy-start.8 = (bf16[128,2048]{1,0:T(8,128)(2,1)S(1)}, bf16[128,2048]{1,0:T(8,128)(2,1)}, u32[]{:S(2)}) copy-start(bf16[128,2048]{1,0:T(8,128)(2,1)} %param.10) | copy-start | bytes 1572868
  9.2 13.2 %all-to-all-start.1 = ((bf16[128,4,512]{0,2,1:T(8,128)(2,1)}), bf16[128,4,512]{0,2,1:T(8,128)(2,1)S(1)}, u32[]{:S(2)}, u32[]{:S(2)}) async-start(bf16[128,4,512]{0,2,1:T(8,128)(2,1)} %bitcast.3), calls=%async_computation.1 | async-start | bytes 1048576 | tf_op jit(solution)/shard_map/all_to_all | solution.py:42
  13.5 50.4 %all-gather.5.cloned.1.call-start = ((), (), s32[]{:S(2)}) async-start(), calls=%async_computation.8 | async-start | bytes 1310720 | tf_op jit(solution)/shard_map/all_gather | solution.py:15
  33.6 1.2 copy-start.9
  35.8 12.3 %all-to-all-start = ((bf16[128,4,512]{0,2,1:T(8,128)(2,1)}), bf16[128,4,512]{0,2,1:T(8,128)(2,1)S(1)}, u32[]{:S(2)}, u32[]{:S(2)}) async-start(bf16[128,4,512]{0,2,1:T(8,128)(2,1)} %bitcast), calls=%async_computation | async-start | bytes 1048576 | tf_op jit(solution)/shard_map/all_to_all | solution.py:41
  48.1 22.1 %all-to-all-start.4 = ((bf16[128,4,512]{0,2,1:T(8,128)(2,1)}), bf16[128,4,512]{0,2,1:T(8,128)(2,1)}, u32[]{:S(2)}, u32[]{:S(2)}) async-start(bf16[128,4,512]{0,2,1:T(8,128)(2,1)} %bitcast.108), calls=%async_computation.4 | async-start | bytes 1048576 | tf_op jit(solution)/shard_map/all_to_all | solution.py:44
  52.3 50.2 %all-gather.7.cloned.1.call-start = ((), (), s32[]{:S(2)}) async-start(), calls=%async_computation.9 | async-start | bytes 1310720 | tf_op jit(solution)/shard_map/all_gather | solution.py:15
  52.7 0.8 copy-start.2
  68.2 1.2 copy-start.4
  69.4 0.8 copy-start
  76.5 1.0 copy-start.1
  78.6 4.3 %copy-start.3 = (bf16[4,4,128,128]{3,2,1,0:T(8,128)(2,1)S(1)}, bf16[4,4,128,128]{3,2,1,0:T(8,128)(2,1)}, u32[]{:S(2)}) copy-start(bf16[4,4,128,128]{3,2,1,0:T(8,128)(2,1)} %copy-done.2) | copy-start | bytes 1572868
  78.6 29.0 %all-to-all-start.5 = ((bf16[4,128,512]{1,2,0:T(8,128)(2,1)}), bf16[4,128,512]{1,2,0:T(8,128)(2,1)}, u32[]{:S(2)}, u32[]{:S(2)}) async-start(bf16[4,128,512]{1,2,0:T(8,128)(2,1)} %bitcast.107), calls=%async_computation.5 | async-start | bytes 1048576 | tf_op jit(solution)/shard_map/all_to_all | solution.py:102
  82.9 1.3 copy-start.6
  107.6 3.6 %copy-start.7 = (f32[4,128,128]{1,2,0:T(8,128)S(1)}, f32[4,128,128]{1,2,0:T(8,128)}, u32[]{:S(2)}) copy-start(f32[4,128,128]{1,2,0:T(8,128)} %copy.62) | copy-start | bytes 786436
  107.6 12.4 %all-to-all-start.3 = ((bf16[4,128,512]{1,2,0:T(8,128)(2,1)}), bf16[4,128,512]{1,2,0:T(8,128)(2,1)S(1)}, u32[]{:S(2)}, u32[]{:S(2)}) async-start(bf16[4,128,512]{1,2,0:T(8,128)(2,1)} %bitcast.15), calls=%async_computation.3 | async-start | bytes 1048576 | tf_op jit(solution)/shard_map/all_to_all | solution.py:99
  111.2 1.5 %copy-start.5 = (f32[4,4,128,128]{3,2,1,0:T(8,128)S(1)}, f32[4,4,128,128]{3,2,1,0:T(8,128)}, u32[]{:S(2)}) copy-start(f32[4,4,128,128]{3,2,1,0:T(8,128)} %fusion.14) | copy-start | bytes 3145732
  120.0 12.3 %all-to-all-start.7 = ((bf16[4,128,512]{1,2,0:T(8,128)(2,1)}), bf16[4,128,512]{1,2,0:T(8,128)(2,1)S(1)}, u32[]{:S(2)}, u32[]{:S(2)}) async-start(bf16[4,128,512]{1,2,0:T(8,128)(2,1)} %bitcast.35), calls=%async_computation.7 | async-start | bytes 1048576 | tf_op jit(solution)/shard_map/all_to_all | solution.py:108
  132.3 12.3 %all-to-all-start.6 = ((bf16[4,128,512]{1,2,0:T(8,128)(2,1)}), bf16[4,128,512]{1,2,0:T(8,128)(2,1)S(1)}, u32[]{:S(2)}, u32[]{:S(2)}) async-start(bf16[4,128,512]{1,2,0:T(8,128)(2,1)} %bitcast.31), calls=%async_computation.6 | async-start | bytes 1048576 | tf_op jit(solution)/shard_map/all_to_all | solution.py:105
Sparse Core Ops, SparseCore 0:
  35.0 28.9 all-gather.4
  75.0 27.4 all-gather.6
where the time goes:
time: 154 us; the launch traced here: 152 us
  waiting for transfers between devices  59.8 us (39%)
  starting transfers between devices  26.8 us (17%)
  local copies, waits for them, and re-layouts  16.3 us (11%)
  other arithmetic  14.3 us (9%)
  between operations  14.3 us (9%)
  blocking collectives  11.2 us (7%)
  matrix products  9.59 us (6%)
    all_gather x2, waiting for transfers between devices, carried_in(): everything = lax.all_gather(value, axis)  26.2 us
    all_to_all x1, blocking collectives, on_device(): lax.all_to_all(value_rows, ('head', 'sub'), split_axis=1, concat_axis=0,...  11.2 us
    all_to_all x1, waiting for transfers between devices, on_device(): lax.all_to_all(key_rows, ('head', 'sub'), split_axis=1, concat_axis=0, ti...  8.57 us
    select_n x8, other arithmetic, turn(): return jnp.where(reached, new, before)  8.32 us
    all_to_all x1, waiting for transfers between devices, on_device(): lax.all_to_all(merge_rows(grad_v), ('head', 'sub'), split_axis=0, concat_...  7.36 us
    all_to_all x1, waiting for transfers between devices, on_device(): lax.all_to_all(query_rows, ('head', 'sub'), split_axis=1, concat_axis=0,...  6.73 us
    all_to_all x1, waiting for transfers between devices, on_device(): lax.all_to_all(merge_rows(normed), ('head', 'sub'), split_axis=0, concat_...  6.17 us
    unnamed x22, local copies, waits for them, and re-layouts  6.02 us
  transfers between devices with their start and end apart: 9, of which 7 were waited for; matrix products, arithmetic and copies ran while one was open for 19% of the time, Pallas kernels for 0%

commit v1 on v0

v1 whole, which is shorter than its diff:
```python
import functools

import jax
import jax.numpy as jnp
from jax import lax
from jax.experimental import pallas as pl
from jax.experimental.pallas import tpu as pltpu
from jax.sharding import PartitionSpec as P

HEAD_DIM = 128
BLOCK = 128
EPSILON = 1e-05
BF = jnp.bfloat16
F32 = jnp.float32
NN = (((1,), (0,)), ((), ()))
NT = (((1,), (1,)), ((), ()))
TN = (((0,), (0,)), ((), ()))


def dot(left, right, form):
    return lax.dot_general(left, right, form, preferred_element_type=F32)


def causal_mask():
    rows = lax.broadcasted_iota(jnp.int32, (BLOCK, BLOCK), 0)
    cols = lax.broadcasted_iota(jnp.int32, (BLOCK, BLOCK), 1)
    return rows >= cols


def columns(slot, flip_ref):
    head = lax.bitwise_xor(jnp.int32(slot), flip_ref[0])
    return pl.ds(pl.multiple_of(head * HEAD_DIM, HEAD_DIM), HEAD_DIM)


def key_value_body(heads, flip_ref, k_ref, v_ref, send_ref, keep_ref):
    half = heads // 2
    for slot in list(range(half, heads)) + list(range(half)):
        at = columns(slot, flip_ref)
        state = dot(k_ref[:, at], v_ref[:, at], TN)
        if slot >= half:
            send_ref[slot - half] = state.astype(BF)
        else:
            keep_ref[slot] = state


def inner_body(heads, q_ref, k_ref, v_ref, probs_ref, inner_ref):
    mask = causal_mask()
    for head in range(heads):
        at = pl.ds(head * HEAD_DIM, HEAD_DIM)
        probs = jnp.where(mask, dot(q_ref[:, at], k_ref[:, at], NT), 0.0).astype(BF)
        probs_ref[head] = probs
        inner_ref[:, at] = dot(probs, v_ref[:, at], NN)


def norm_body(
    heads, flip_ref, q_ref, g_ref, inner_ref, near_ref, far_ref, normed_ref, raw_ref, send_ref, keep_ref
):
    half = heads // 2
    for slot in list(range(half, heads)) + list(range(half)):
        at = columns(slot, flip_ref)
        query = q_ref[:, at]
        state = far_ref[slot - half] if slot >= half else near_ref[slot]
        unnormed = inner_ref[:, at] + dot(query, state, NN)
        inv = lax.rsqrt(jnp.mean(unnormed * unnormed, axis=-1, keepdims=True) + EPSILON)
        normed = unnormed * inv
        normed_ref[:, at] = normed.astype(BF)
        cot = g_ref[:, at].astype(F32)
        raw = (cot - normed * jnp.mean(cot * normed, axis=-1, keepdims=True)) * inv
        raw = raw.astype(BF)
        raw_ref[:, at] = raw
        grad = dot(query, raw, TN)
        if slot >= half:
            send_ref[slot - half] = grad.astype(BF)
        else:
            keep_ref[slot] = grad


def local_grads_body(
    heads, flip_ref, q_ref, k_ref, v_ref, raw_ref, probs_ref, near_ref, far_ref, gq_ref, gk_ref, gv_ref
):
    half = heads // 2
    mask = causal_mask()
    for slot in range(heads):
        at = columns(slot, flip_ref)
        head = lax.bitwise_xor(jnp.int32(slot), flip_ref[0])
        raw = raw_ref[:, at]
        state = far_ref[slot - half] if slot >= half else near_ref[slot]
        grad_probs = jnp.where(mask, dot(raw, v_ref[:, at], NT), 0.0).astype(BF)
        gq_ref[:, at] = (dot(grad_probs, k_ref[:, at], NN) + dot(raw, state, NT)).astype(BF)
        gk_ref[:, at] = dot(grad_probs, q_ref[:, at], TN)
        gv_ref[:, at] = dot(probs_ref[head], raw, TN)


def last_grads_body(
    heads, flip_ref, k_ref, v_ref, gk_in_ref, gv_in_ref, near_ref, far_ref, gk_ref, gv_ref
):
    half = heads // 2
    for slot in range(heads):
        at = columns(slot, flip_ref)
        state = far_ref[slot - half] if slot >= half else near_ref[slot]
        gk_ref[:, at] = (gk_in_ref[:, at] + dot(v_ref[:, at], state, NT)).astype(BF)
        gv_ref[:, at] = (gv_in_ref[:, at] + dot(k_ref[:, at], state, NN)).astype(BF)


def call(body, flip, arrays, outs, flops):
    in_specs = [pl.BlockSpec(memory_space=pltpu.VMEM)] * len(arrays)
    operands = list(arrays)
    if flip is not None:
        in_specs = [pl.BlockSpec(memory_space=pltpu.SMEM)] + in_specs
        operands = [flip] + operands
    size = sum(a.size * a.dtype.itemsize for a in arrays)
    size += sum(o.size * o.dtype.itemsize for o in outs)
    return pl.pallas_call(
        body,
        out_shape=outs,
        in_specs=in_specs,
        out_specs=[pl.BlockSpec(memory_space=pltpu.VMEM)] * len(outs),
        compiler_params=pltpu.CompilerParams(vmem_limit_bytes=24 * 1024 * 1024),
        cost_estimate=pl.CostEstimate(flops=flops, bytes_accessed=size, transcendentals=0),
    )(*operands)


def swap(value, axis, bit):
    pairs = [(i, i ^ bit) for i in range(lax.axis_size(axis))]
    return lax.ppermute(value, axis, pairs)


def bits_of(axis):
    return [1 << b for b in range(lax.axis_size(axis).bit_length() - 1)]


def has_bit(axis, bit):
    return (lax.axis_index(axis) & bit) != 0


def scan_states(send, keep, reverse):
    levels = [(axis, bit) for axis in ("sub", "head") for bit in bits_of(axis)]
    zero = jnp.zeros((), F32)
    total, saved = keep, []
    for number, (axis, bit) in enumerate(levels):
        if number:
            half = total.shape[0] // 2
            send, total = total[half:].astype(BF), total[:half]
        got = swap(send, axis, bit).astype(F32)
        saved.append((axis, bit, total, got))
        total = total + got
    carried = jnp.zeros_like(total)
    for bit in bits_of("seq"):
        got = swap(total.astype(BF), "seq", bit).astype(F32)
        counts = has_bit("seq", bit) != reverse
        carried = carried + jnp.where(counts, got, zero)
        total = total + got
    for number, (axis, bit, own, got) in reversed(list(enumerate(saved))):
        counts = has_bit(axis, bit) != reverse
        message = (carried + jnp.where(counts, zero, own)).astype(BF)
        near = carried + jnp.where(counts, got, zero)
        far = swap(message, axis, bit)
        if number:
            carried = jnp.concatenate([near, far.astype(F32)], axis=0)
    return near.astype(BF), far


def on_device(query, key, value, cot):
    rows, width = query.shape
    heads = width // HEAD_DIM
    half = heads // 2
    flip = jnp.zeros((), jnp.int32)
    weight = half
    for axis in ("sub", "head"):
        for bit in bits_of(axis):
            flip = flip + jnp.where(has_bit(axis, bit), weight, 0).astype(jnp.int32)
            weight //= 2
    flip = flip.reshape(1)
    state = (half, HEAD_DIM, HEAD_DIM)
    unit = 2 * BLOCK * HEAD_DIM * HEAD_DIM * heads

    def shape(dims, dtype):
        return jax.ShapeDtypeStruct(dims, dtype)

    send, keep = call(
        functools.partial(key_value_body, heads), flip, (key, value),
        [shape(state, BF), shape(state, F32)], unit,
    )
    probs, inner = call(
        functools.partial(inner_body, heads), None, (query, key, value),
        [shape((heads, BLOCK, BLOCK), BF), shape((rows, width), F32)], 2 * unit,
    )
    near, far = scan_states(send, keep, False)
    normed, raw, send, keep = call(
        functools.partial(norm_body, heads), flip, (query, cot, inner, near, far),
        [shape((rows, width), BF), shape((rows, width), BF), shape(state, BF), shape(state, F32)], 2 * unit,
    )
    grad_q, grad_k, grad_v = call(
        functools.partial(local_grads_body, heads), flip, (query, key, value, raw, probs, near, far),
        [shape((rows, width), BF), shape((rows, width), F32), shape((rows, width), F32)], 5 * unit,
    )
    near, far = scan_states(send, keep, True)
    grad_k, grad_v = call(
        functools.partial(last_grads_body, heads), flip, (key, value, grad_k, grad_v, near, far),
        [shape((rows, width), BF), shape((rows, width), BF)], 2 * unit,
    )
    return normed, grad_q, grad_k, grad_v


def solution(mesh):
    placed = P(("group", "seq", "head", "sub"), None)
    return jax.shard_map(
        on_device,
        mesh=mesh,
        in_specs=(placed,) * 4,
        out_specs=(placed,) * 4,
        check_vma=False,
    )
```

time: 154 us -> 69.8 us (0.45)
  waiting for transfers between devices: 59.8 us -> 37.7 us
  between operations: 14.3 us -> 0.84 us
  starting transfers between devices: 26.8 us -> 13.8 us
  local copies, waits for them, and re-layouts: 16.3 us -> 4.07 us
  blocking collectives: 11.2 us -> 0 us
  other arithmetic: 14.3 us -> 3.24 us
  Pallas kernels: 0 us -> 9.85 us
  matrix products: 9.59 us -> 0 us
    ppermute x0 -> x12, waiting for transfers between devices: none -> 37.7 us  [swap(): return lax.ppermute(value, axis, pairs)]
    all_to_all x7 -> x0, waiting for transfers between devices: 33.6 us -> none  [the longest x1 8.57 us: on_device(): lax.all_to_all(key_rows, ('head', 'sub'), split_axis=1, concat_axis=0, ti...]
    all_to_all x7 -> x0, starting transfers between devices: 26.8 us -> none  [the longest x1 4.34 us: on_device(): lax.all_to_all(key_rows, ('head', 'sub'), split_axis=1, concat_axis=0, ti...]
    all_gather x2 -> x0, waiting for transfers between devices: 26.2 us -> none  [carried_in(): everything = lax.all_gather(value, axis)]
    ppermute x0 -> x12, starting transfers between devices: none -> 13.8 us  [swap(): return lax.ppermute(value, axis, pairs)]
    all_to_all x1 -> x0, blocking collectives: 11.2 us -> none  [on_device(): lax.all_to_all(value_rows, ('head', 'sub'), split_axis=1, concat_axis=0,...]
    pallas_call x0 -> x5, Pallas kernels: none -> 9.85 us  [call(): pl.pallas_call(body, out_shape=outs, in_specs=in_specs, out_specs=[pl.Blo...]
    dot_general x12 -> x0, matrix products: 9.59 us -> none  [the longest x1 1.47 us: on_device(): jnp.einsum('nhts,nshf->nthf', probs, value_blk, preferred_element_type=f32)]
  transfers between devices with their start and end apart: 9 -> 12, of which waited for: 7 -> 10; matrix products, arithmetic and copies ran while one was open for 19% -> 0% of each run, Pallas kernels for 0% -> 9%
where the time goes in v1:
time: 69.8 us; the launch traced here: 69.5 us
  waiting for transfers between devices  37.7 us (54%)
  starting transfers between devices  13.8 us (20%)
  Pallas kernels  9.85 us (14%)
  local copies, waits for them, and re-layouts  4.07 us (6%)
  other arithmetic  3.24 us (5%)
  between operations  0.84 us (1%)
    ppermute x12, waiting for transfers between devices, swap(): return lax.ppermute(value, axis, pairs)  37.7 us
    ppermute x12, starting transfers between devices, swap(): return lax.ppermute(value, axis, pairs)  13.8 us
    pallas_call x5, Pallas kernels, call(): pl.pallas_call(body, out_shape=outs, in_specs=in_specs, out_specs=[pl.Blo...  9.85 us
    unnamed x22, local copies, waits for them, and re-layouts  4.02 us
    add x2, other arithmetic, scan_states(): near = carried + jnp.where(counts, got, zero)  2.01 us
  transfers between devices with their start and end apart: 12, of which 10 were waited for; matrix products, arithmetic and copies ran while one was open for 0% of the time, Pallas kernels for 9%

profile of v1, /device:TPU:0, one launch (start us, length us, event | category | flops | bytes accessed | tf_op | source)
XLA Modules:
  0.0 69.5 jit_solution(16968649231439368860)
XLA Ops:
  0.7 1.0 %copy-done = bf16[128,2048]{1,0:T(8,128)(2,1)S(1)} copy-done((bf16[128,2048]{1,0:T(8,128)(2,1)S(1)}, bf16[128,2048]{1,0:T(8,128)(2,1)}, u32[]{:S(2)}) %copy-start) | copy-done | bytes 524312
  1.7 1.0 %copy-done.2 = bf16[128,2048]{1,0:T(8,128)(2,1)S(1)} copy-done((bf16[128,2048]{1,0:T(8,128)(2,1)S(1)}, bf16[128,2048]{1,0:T(8,128)(2,1)}, u32[]{:S(2)}) %copy-start.2) | copy-done | bytes 524312
  3.7 1.2 %collective-permute-done = bf16[8,128,128]{2,1,0:T(8,128)(2,1)S(1)} collective-permute-done((bf16[8,128,128]{2,1,0:T(8,128)(2,1)S(1)}, bf16[8,128,128]{2,1,0:T(8,128)(2,1)S(1)}, u32[]{:S(2)}, u32[]{:S(2)}) %collective-permute-start) | collective-permute-done | bytes 262176 | tf_op jit(solution)/shard_map/ppermute | solution.py:125
  5.0 2.9 %collective-permute-start.1 = (bf16[4,128,128]{2,1,0:T(8,128)(2,1)S(1)}, bf16[4,128,128]{2,1,0:T(8,128)(2,1)S(1)}, u32[]{:S(2)}, u32[]{:S(2)}) collective-permute-start(bf16[4,128,128]{2,1,0:T(8,128)(2,1)S(1)} %slice.37), channel_id=1, source_target_pairs={{0,2},{2,0},{1,3},{3,1},{4,6},{6,4},{5,7},{7,5},{8,10},{10,8},{9,1... | collective-permute-start | bytes 393224 | tf_op jit(solution)/shard_map/ppermute | solution.py:125
  7.9 3.8 %collective-permute-done.1 = bf16[4,128,128]{2,1,0:T(8,128)(2,1)S(1)} collective-permute-done((bf16[4,128,128]{2,1,0:T(8,128)(2,1)S(1)}, bf16[4,128,128]{2,1,0:T(8,128)(2,1)S(1)}, u32[]{:S(2)}, u32[]{:S(2)}) %collective-permute-start.1) | collective-permute-done | bytes 131104 | tf_op jit(solution)/shard_map/ppermute | solution.py:125
  11.7 1.9 %collective-permute-start.2 = (bf16[4,128,128]{2,1,0:T(8,128)(2,1)S(1)}, bf16[4,128,128]{2,1,0:T(8,128)(2,1)S(1)}, u32[]{:S(2)}, u32[]{:S(2)}) collective-permute-start(bf16[4,128,128]{2,1,0:T(8,128)(2,1)S(1)} %fusion.10), channel_id=1, source_target_pairs={{0,4},{4,0},{8,12},{12,8},{1,5},{5,1},{9,13},{13,9},{2,6},{6,2},{1... | collective-permute-start | bytes 393224 | tf_op jit(solution)/shard_map/ppermute | solution.py:125
  13.6 3.2 %collective-permute-done.2 = bf16[4,128,128]{2,1,0:T(8,128)(2,1)S(1)} collective-permute-done((bf16[4,128,128]{2,1,0:T(8,128)(2,1)S(1)}, bf16[4,128,128]{2,1,0:T(8,128)(2,1)S(1)}, u32[]{:S(2)}, u32[]{:S(2)}) %collective-permute-start.2) | collective-permute-done | bytes 131104 | tf_op jit(solution)/shard_map/ppermute | solution.py:125
  16.9 2.8 %collective-permute-start.3 = (bf16[4,128,128]{2,1,0:T(8,128)(2,1)S(1)}, bf16[4,128,128]{2,1,0:T(8,128)(2,1)S(1)}, u32[]{:S(2)}, u32[]{:S(2)}) collective-permute-start(bf16[4,128,128]{2,1,0:T(8,128)(2,1)S(1)} %fusion.6), channel_id=1, source_target_pairs={{0,8},{4,12},{8,0},{12,4},{1,9},{5,13},{9,1},{13,5},{2,10},{6,14},... | collective-permute-start | bytes 393224 | tf_op jit(solution)/shard_map/ppermute | solution.py:125
  19.7 5.1 %collective-permute-done.3 = bf16[4,128,128]{2,1,0:T(8,128)(2,1)S(1)} collective-permute-done((bf16[4,128,128]{2,1,0:T(8,128)(2,1)S(1)}, bf16[4,128,128]{2,1,0:T(8,128)(2,1)S(1)}, u32[]{:S(2)}, u32[]{:S(2)}) %collective-permute-start.3) | collective-permute-done | bytes 131104 | tf_op jit(solution)/shard_map/ppermute | solution.py:125
  24.9 1.2 %collective-permute-start.4 = (bf16[4,128,128]{2,1,0:T(8,128)(2,1)S(1)}, bf16[4,128,128]{2,1,0:T(8,128)(2,1)S(1)}, u32[]{:S(2)}, u32[]{:S(2)}) collective-permute-start(bf16[4,128,128]{2,1,0:T(8,128)(2,1)S(1)} %get-tuple-element.37), channel_id=1, source_target_pairs={{0,2},{2,0},{1,3},{3,1},{4,6},{6,4},{5,7},{7,5},{8,10},{10,8},{9,1... | collective-permute-start | bytes 393224 | tf_op jit(solution)/shard_map/ppermute | solution.py:125
  26.1 3.9 %collective-permute-done.4 = bf16[4,128,128]{2,1,0:T(8,128)(2,1)S(1)} collective-permute-done((bf16[4,128,128]{2,1,0:T(8,128)(2,1)S(1)}, bf16[4,128,128]{2,1,0:T(8,128)(2,1)S(1)}, u32[]{:S(2)}, u32[]{:S(2)}) %collective-permute-start.4) | collective-permute-done | bytes 131104 | tf_op jit(solution)/shard_map/ppermute | solution.py:125
  31.3 2.6 %shard_map.75 = (bf16[16,128,128]{2,1,0:T(8,128)(2,1)S(1)}, f32[128,2048]{1,0:T(8,128)S(1)}) custom-call(bf16[128,2048]{1,0:T(8,128)(2,1)S(1)} %copy-done.4, bf16[128,2048]{1,0:T(8,128)(2,1)S(1)} %copy-done.1, bf16[128,2048]{1,0:T(8,128)(2,1)S(1)} %copy-done.3), custom_call_target="tpu_custom_call" | custom-call | flops 134217728 | bytes 3145728 | tf_op jit(solution)/shard_map/pallas_call | solution.py:113
  33.9 1.8 %shard_map.77 = (bf16[128,2048]{1,0:T(8,128)(2,1)}, bf16[128,2048]{1,0:T(8,128)(2,1)S(1)}, bf16[8,128,128]{2,1,0:T(8,128)(2,1)S(1)}, f32[8,128,128]{2,1,0:T(8,128)S(1)}) custom-call(s32[1]{0:T(128)} %bitcast.flip_ref, bf16[128,2048]{1,0:T(8,128)(2,1)S(1)} %copy-done.4, bf16[128,2048]{1,0:T(8,128)(2,1)S(1)} %copy-done.5, ...), custom_call_target="tpu_custom_call" | custom-call | flops 134217728 | bytes 4456448 | tf_op jit(solution)/shard_map/pallas_call | solution.py:113
  35.7 1.5 %collective-permute-done.6 = bf16[8,128,128]{2,1,0:T(8,128)(2,1)S(1)} collective-permute-done((bf16[8,128,128]{2,1,0:T(8,128)(2,1)S(1)}, bf16[8,128,128]{2,1,0:T(8,128)(2,1)S(1)}, u32[]{:S(2)}, u32[]{:S(2)}) %collective-permute-start.6) | collective-permute-done | bytes 262176 | tf_op jit(solution)/shard_map/ppermute | solution.py:125
  37.3 1.2 %collective-permute-start.7 = (bf16[4,128,128]{2,1,0:T(8,128)(2,1)S(1)}, bf16[4,128,128]{2,1,0:T(8,128)(2,1)S(1)}, u32[]{:S(2)}, u32[]{:S(2)}) collective-permute-start(bf16[4,128,128]{2,1,0:T(8,128)(2,1)S(1)} %slice.36), channel_id=1, source_target_pairs={{0,2},{2,0},{1,3},{3,1},{4,6},{6,4},{5,7},{7,5},{8,10},{10,8},{9,1... | collective-permute-start | bytes 393224 | tf_op jit(solution)/shard_map/ppermute | solution.py:125
  38.5 4.4 %collective-permute-done.7 = bf16[4,128,128]{2,1,0:T(8,128)(2,1)S(1)} collective-permute-done((bf16[4,128,128]{2,1,0:T(8,128)(2,1)S(1)}, bf16[4,128,128]{2,1,0:T(8,128)(2,1)S(1)}, u32[]{:S(2)}, u32[]{:S(2)}) %collective-permute-start.7) | collective-permute-done | bytes 131104 | tf_op jit(solution)/shard_map/ppermute | solution.py:125
  43.3 4.7 %collective-permute-done.8 = bf16[4,128,128]{2,1,0:T(8,128)(2,1)S(1)} collective-permute-done((bf16[4,128,128]{2,1,0:T(8,128)(2,1)S(1)}, bf16[4,128,128]{2,1,0:T(8,128)(2,1)S(1)}, u32[]{:S(2)}, u32[]{:S(2)}) %collective-permute-start.8) | collective-permute-done | bytes 131104 | tf_op jit(solution)/shard_map/ppermute | solution.py:125
  48.7 1.7 %collective-permute-start.9 = (bf16[4,128,128]{2,1,0:T(8,128)(2,1)}, bf16[4,128,128]{2,1,0:T(8,128)(2,1)}, u32[]{:S(2)}, u32[]{:S(2)}) collective-permute-start(bf16[4,128,128]{2,1,0:T(8,128)(2,1)} %fusion.9), channel_id=1, source_target_pairs={{0,8},{4,12},{8,0},{12,4},{1,9},{5,13},{9,1},{13,5},{2,10},{6,14},... | collective-permute-start | bytes 393224 | tf_op jit(solution)/shard_map/ppermute | solution.py:125
  50.4 5.9 %collective-permute-done.9 = bf16[4,128,128]{2,1,0:T(8,128)(2,1)} collective-permute-done((bf16[4,128,128]{2,1,0:T(8,128)(2,1)}, bf16[4,128,128]{2,1,0:T(8,128)(2,1)}, u32[]{:S(2)}, u32[]{:S(2)}) %collective-permute-start.9) | collective-permute-done | bytes 131104 | tf_op jit(solution)/shard_map/ppermute | solution.py:125
  56.3 1.9 %fusion.7 = (f32[4,128,128]{2,1,0:T(8,128)}, bf16[4,128,128]{2,1,0:T(8,128)(2,1)}) fusion(bf16[4,128,128]{2,1,0:T(8,128)(2,1)S(1)} %collective-permute-done.7, bf16[4,128,128]{2,1,0:T(8,128)(2,1)} %collective-permute-done.9, bf16[4,128,128]{2,1,0:T(8,128)(2,1)} %copy-done.10, pred[]{:T(512)S(6)} %ne.36, pred[]{:T(512)S(6)} %ne.35, pred[]{:T(512)S(6)} %ne.34, ...), kind=kLoop, calls=%fused_computation.23 | loop fusion | flops 720896 | bytes 1048579 | tf_op jit(solution)/shard_map/add | solution.py:156
  58.2 1.1 %collective-permute-start.10 = (bf16[4,128,128]{2,1,0:T(8,128)(2,1)}, bf16[4,128,128]{2,1,0:T(8,128)(2,1)S(1)}, u32[]{:S(2)}, u32[]{:S(2)}) collective-permute-start(bf16[4,128,128]{2,1,0:T(8,128)(2,1)} %get-tuple-element.35), channel_id=1, source_target_pairs={{0,2},{2,0},{1,3},{3,1},{4,6},{6,4},{5,7},{7,5},{8,10},{10,8},{9,1... | collective-permute-start | bytes 393224 | tf_op jit(solution)/shard_map/ppermute | solution.py:125
  59.4 4.1 %collective-permute-done.10 = bf16[4,128,128]{2,1,0:T(8,128)(2,1)S(1)} collective-permute-done((bf16[4,128,128]{2,1,0:T(8,128)(2,1)}, bf16[4,128,128]{2,1,0:T(8,128)(2,1)S(1)}, u32[]{:S(2)}, u32[]{:S(2)}) %collective-permute-start.10) | collective-permute-done | bytes 131104 | tf_op jit(solution)/shard_map/ppermute | solution.py:125
  64.5 3.4 %shard_map.78 = (bf16[128,2048]{1,0:T(8,128)(2,1)}, f32[128,2048]{1,0:T(8,128)S(1)}, f32[128,2048]{1,0:T(8,128)S(1)}) custom-call(s32[1]{0:T(128)} %bitcast.flip_ref, bf16[128,2048]{1,0:T(8,128)(2,1)S(1)} %copy-done.4, bf16[128,2048]{1,0:T(8,128)(2,1)S(1)} %copy-done.1, bf16[128,2048]{1,0:T(8,128)(2,1)S(1)} %copy-done.3, bf16[128,2048]{1,0:T(8,128)(2,1)S(1)} %copy-done.7, ...), custom_call_target="tpu_custom_call" | custom-call | flops 335544320 | bytes 5767168 | tf_op jit(solution)/shard_map/pallas_call | solution.py:113
  67.9 1.6 %shard_map.79 = (bf16[128,2048]{1,0:T(8,128)(2,1)}, bf16[128,2048]{1,0:T(8,128)(2,1)}) custom-call(s32[1]{0:T(128)} %bitcast.flip_ref, bf16[128,2048]{1,0:T(8,128)(2,1)S(1)} %copy-done.1, bf16[128,2048]{1,0:T(8,128)(2,1)S(1)} %copy-done.3, f32[128,2048]{1,0:T(8,128)S(1)} %get-tuple-element.24.gk_in_ref, f32[128,2048]{1,0:T(8,128)S(1)} %get-tuple-element.25.gv_in_ref, ...), custom_call_target="tpu_custom_call" | custom-call | flops 134217728 | bytes 4718592 | tf_op jit(solution)/shard_map/pallas_call | solution.py:113
  (41 shorter events, 4.8 us)
Async XLA Ops:
  0.6 1.0 %copy-start = (bf16[128,2048]{1,0:T(8,128)(2,1)S(1)}, bf16[128,2048]{1,0:T(8,128)(2,1)}, u32[]{:S(2)}) copy-start(bf16[128,2048]{1,0:T(8,128)(2,1)} %k_ref.7) | copy-start | bytes 1572868
  1.7 1.0 %copy-start.2 = (bf16[128,2048]{1,0:T(8,128)(2,1)S(1)}, bf16[128,2048]{1,0:T(8,128)(2,1)}, u32[]{:S(2)}) copy-start(bf16[128,2048]{1,0:T(8,128)(2,1)} %v_ref.7) | copy-start | bytes 1572868
  3.2 1.7 %collective-permute-start = (bf16[8,128,128]{2,1,0:T(8,128)(2,1)S(1)}, bf16[8,128,128]{2,1,0:T(8,128)(2,1)S(1)}, u32[]{:S(2)}, u32[]{:S(2)}) collective-permute-start(bf16[8,128,128]{2,1,0:T(8,128)(2,1)S(1)} %get-tuple-element.19), channel_id=1, source_target_pairs={{0,1},{1,0},{2,3},{3,2},{4,5},{5,4},{6,7},{7,6},{8,9},{9,8},{10,11... | collective-permute-start | bytes 786440 | tf_op jit(solution)/shard_map/ppermute | solution.py:125
  5.0 6.7 %collective-permute-start.1 = (bf16[4,128,128]{2,1,0:T(8,128)(2,1)S(1)}, bf16[4,128,128]{2,1,0:T(8,128)(2,1)S(1)}, u32[]{:S(2)}, u32[]{:S(2)}) collective-permute-start(bf16[4,128,128]{2,1,0:T(8,128)(2,1)S(1)} %slice.37), channel_id=1, source_target_pairs={{0,2},{2,0},{1,3},{3,1},{4,6},{6,4},{5,7},{7,5},{8,10},{10,8},{9,1... | collective-permute-start | bytes 393224 | tf_op jit(solution)/shard_map/ppermute | solution.py:125
  11.7 5.1 %collective-permute-start.2 = (bf16[4,128,128]{2,1,0:T(8,128)(2,1)S(1)}, bf16[4,128,128]{2,1,0:T(8,128)(2,1)S(1)}, u32[]{:S(2)}, u32[]{:S(2)}) collective-permute-start(bf16[4,128,128]{2,1,0:T(8,128)(2,1)S(1)} %fusion.10), channel_id=1, source_target_pairs={{0,4},{4,0},{8,12},{12,8},{1,5},{5,1},{9,13},{13,9},{2,6},{6,2},{1... | collective-permute-start | bytes 393224 | tf_op jit(solution)/shard_map/ppermute | solution.py:125
  16.9 7.9 %collective-permute-start.3 = (bf16[4,128,128]{2,1,0:T(8,128)(2,1)S(1)}, bf16[4,128,128]{2,1,0:T(8,128)(2,1)S(1)}, u32[]{:S(2)}, u32[]{:S(2)}) collective-permute-start(bf16[4,128,128]{2,1,0:T(8,128)(2,1)S(1)} %fusion.6), channel_id=1, source_target_pairs={{0,8},{4,12},{8,0},{12,4},{1,9},{5,13},{9,1},{13,5},{2,10},{6,14},... | collective-permute-start | bytes 393224 | tf_op jit(solution)/shard_map/ppermute | solution.py:125
  24.9 5.0 %collective-permute-start.4 = (bf16[4,128,128]{2,1,0:T(8,128)(2,1)S(1)}, bf16[4,128,128]{2,1,0:T(8,128)(2,1)S(1)}, u32[]{:S(2)}, u32[]{:S(2)}) collective-permute-start(bf16[4,128,128]{2,1,0:T(8,128)(2,1)S(1)} %get-tuple-element.37), channel_id=1, source_target_pairs={{0,2},{2,0},{1,3},{3,1},{4,6},{6,4},{5,7},{7,5},{8,10},{10,8},{9,1... | collective-permute-start | bytes 393224 | tf_op jit(solution)/shard_map/ppermute | solution.py:125
  29.9 1.0 %copy-start.1 = (bf16[128,2048]{1,0:T(8,128)(2,1)S(1)}, bf16[128,2048]{1,0:T(8,128)(2,1)}, u32[]{:S(2)}) copy-start(bf16[128,2048]{1,0:T(8,128)(2,1)} %k_ref.7) | copy-start | bytes 1572868
  29.9 1.2 %copy-start.3 = (bf16[128,2048]{1,0:T(8,128)(2,1)S(1)}, bf16[128,2048]{1,0:T(8,128)(2,1)}, u32[]{:S(2)}) copy-start(bf16[128,2048]{1,0:T(8,128)(2,1)} %v_ref.7) | copy-start | bytes 1572868
  30.0 1.3 %copy-start.4 = (bf16[128,2048]{1,0:T(8,128)(2,1)S(1)}, bf16[128,2048]{1,0:T(8,128)(2,1)}, u32[]{:S(2)}) copy-start(bf16[128,2048]{1,0:T(8,128)(2,1)} %q_ref.5) | copy-start | bytes 1572868
  30.1 3.8 %copy-start.5 = (bf16[128,2048]{1,0:T(8,128)(2,1)S(1)}, bf16[128,2048]{1,0:T(8,128)(2,1)}, u32[]{:S(2)}) copy-start(bf16[128,2048]{1,0:T(8,128)(2,1)} %g_ref.1) | copy-start | bytes 1572868
  30.1 3.7 %collective-permute-start.5 = (bf16[8,128,128]{2,1,0:T(8,128)(2,1)S(1)}, bf16[8,128,128]{2,1,0:T(8,128)(2,1)S(1)}, u32[]{:S(2)}, u32[]{:S(2)}) collective-permute-start(bf16[8,128,128]{2,1,0:T(8,128)(2,1)S(1)} %get-tuple-element.32), channel_id=1, source_target_pairs={{0,1},{1,0},{2,3},{3,2},{4,5},{5,4},{6,7},{7,6},{8,9},{9,8},{10,11... | collective-permute-start | bytes 786440 | tf_op jit(solution)/shard_map/ppermute | solution.py:125
  35.7 1.6 %copy-start.6 = (bf16[128,2048]{1,0:T(8,128)(2,1)}, bf16[128,2048]{1,0:T(8,128)(2,1)S(1)}, u32[]{:S(2)}) copy-start(bf16[128,2048]{1,0:T(8,128)(2,1)S(1)} %get-tuple-element.21.raw_ref) | copy-start | bytes 1572868
  35.7 1.5 %collective-permute-start.6 = (bf16[8,128,128]{2,1,0:T(8,128)(2,1)S(1)}, bf16[8,128,128]{2,1,0:T(8,128)(2,1)S(1)}, u32[]{:S(2)}, u32[]{:S(2)}) collective-permute-start(bf16[8,128,128]{2,1,0:T(8,128)(2,1)S(1)} %get-tuple-element.27), channel_id=1, source_target_pairs={{0,1},{1,0},{2,3},{3,2},{4,5},{5,4},{6,7},{7,6},{8,9},{9,8},{10,11... | collective-permute-start | bytes 786440 | tf_op jit(solution)/shard_map/ppermute | solution.py:125
  37.3 11.4 %copy-start.8 = (f32[8,128,128]{2,1,0:T(8,128)}, f32[8,128,128]{2,1,0:T(8,128)S(1)}, u32[]{:S(2)}) copy-start(f32[8,128,128]{2,1,0:T(8,128)S(1)} %convert_add_fusion) | copy-start | bytes 1572868
  37.3 5.6 %collective-permute-start.7 = (bf16[4,128,128]{2,1,0:T(8,128)(2,1)S(1)}, bf16[4,128,128]{2,1,0:T(8,128)(2,1)S(1)}, u32[]{:S(2)}, u32[]{:S(2)}) collective-permute-start(bf16[4,128,128]{2,1,0:T(8,128)(2,1)S(1)} %slice.36), channel_id=1, source_target_pairs={{0,2},{2,0},{1,3},{3,1},{4,6},{6,4},{5,7},{7,5},{8,10},{10,8},{9,1... | collective-permute-start | bytes 393224 | tf_op jit(solution)/shard_map/ppermute | solution.py:125
  43.0 5.0 %collective-permute-start.8 = (bf16[4,128,128]{2,1,0:T(8,128)(2,1)S(1)}, bf16[4,128,128]{2,1,0:T(8,128)(2,1)S(1)}, u32[]{:S(2)}, u32[]{:S(2)}) collective-permute-start(bf16[4,128,128]{2,1,0:T(8,128)(2,1)S(1)} %fusion.11), channel_id=1, source_target_pairs={{0,4},{4,0},{8,12},{12,8},{1,5},{5,1},{9,13},{13,9},{2,6},{6,2},{1... | collective-permute-start | bytes 393224 | tf_op jit(solution)/shard_map/ppermute | solution.py:125
  48.0 0.7 %copy-start.10 = (bf16[4,128,128]{2,1,0:T(8,128)(2,1)}, bf16[4,128,128]{2,1,0:T(8,128)(2,1)S(1)}, u32[]{:S(2)}) copy-start(bf16[4,128,128]{2,1,0:T(8,128)(2,1)S(1)} %collective-permute-done.8) | copy-start | bytes 393220
  48.7 7.6 %collective-permute-start.9 = (bf16[4,128,128]{2,1,0:T(8,128)(2,1)}, bf16[4,128,128]{2,1,0:T(8,128)(2,1)}, u32[]{:S(2)}, u32[]{:S(2)}) collective-permute-start(bf16[4,128,128]{2,1,0:T(8,128)(2,1)} %fusion.9), channel_id=1, source_target_pairs={{0,8},{4,12},{8,0},{12,4},{1,9},{5,13},{9,1},{13,5},{2,10},{6,14},... | collective-permute-start | bytes 393224 | tf_op jit(solution)/shard_map/ppermute | solution.py:125
  58.2 5.2 %collective-permute-start.10 = (bf16[4,128,128]{2,1,0:T(8,128)(2,1)}, bf16[4,128,128]{2,1,0:T(8,128)(2,1)S(1)}, u32[]{:S(2)}, u32[]{:S(2)}) collective-permute-start(bf16[4,128,128]{2,1,0:T(8,128)(2,1)} %get-tuple-element.35), channel_id=1, source_target_pairs={{0,2},{2,0},{1,3},{3,1},{4,6},{6,4},{5,7},{7,5},{8,10},{10,8},{9,1... | collective-permute-start | bytes 393224 | tf_op jit(solution)/shard_map/ppermute | solution.py:125
  59.4 4.1 %copy-start.9 = (f32[4,128,128]{2,1,0:T(8,128)S(1)}, f32[4,128,128]{2,1,0:T(8,128)}, u32[]{:S(2)}) copy-start(f32[4,128,128]{2,1,0:T(8,128)} %get-tuple-element.34) | copy-start | bytes 786436
  63.5 1.0 %copy-start.7 = (bf16[128,2048]{1,0:T(8,128)(2,1)S(1)}, bf16[128,2048]{1,0:T(8,128)(2,1)}, u32[]{:S(2)}) copy-start(bf16[128,2048]{1,0:T(8,128)(2,1)} %copy-done.6) | copy-start | bytes 1572868
  63.6 4.3 %collective-permute-start.11 = (bf16[8,128,128]{2,1,0:T(8,128)(2,1)S(1)}, bf16[8,128,128]{2,1,0:T(8,128)(2,1)S(1)}, u32[]{:S(2)}, u32[]{:S(2)}) collective-permute-start(bf16[8,128,128]{2,1,0:T(8,128)(2,1)S(1)} %get-tuple-element.30), channel_id=1, source_target_pairs={{0,1},{1,0},{2,3},{3,2},{4,5},{5,4},{6,7},{7,6},{8,9},{9,8},{10,11... | collective-permute-start | bytes 786440 | tf_op jit(solution)/shard_map/ppermute | solution.py:125

commit v2 on v1

v2 whole, which is shorter than its diff:
```python
import functools

import jax
import jax.numpy as jnp
from jax import lax
from jax.experimental import pallas as pl
from jax.experimental.pallas import tpu as pltpu
from jax.sharding import PartitionSpec as P

HEAD_DIM = 128
BLOCK = 128
EPSILON = 1e-05
STREAMS = 2
BF = jnp.bfloat16
F32 = jnp.float32
NN = (((1,), (0,)), ((), ()))
NT = (((1,), (1,)), ((), ()))
TN = (((0,), (0,)), ((), ()))


def dot(left, right, form):
    return lax.dot_general(left, right, form, preferred_element_type=F32)


def causal_mask():
    rows = lax.broadcasted_iota(jnp.int32, (BLOCK, BLOCK), 0)
    cols = lax.broadcasted_iota(jnp.int32, (BLOCK, BLOCK), 1)
    return rows >= cols


AXES = ("seq", "head", "sub")


def place_bit(level):
    place = lax.axis_index(AXES).astype(jnp.int32)
    return lax.bitwise_and(lax.shift_right_logical(place, jnp.int32(level)), jnp.int32(1))


class Stream:
    def __init__(self, number, heads, plane):
        self.number, self.slots = number, heads // STREAMS
        self.kept = heads // plane
        self.run = self.kept // STREAMS
        self.halvings = [heads >> (level + 1) for level in range(plane.bit_length() - 1)]

    def start(self, slot, width):
        position = (slot // self.run) * self.kept + self.number * self.run + slot % self.run
        head = jnp.int32(position)
        for level, weight in enumerate(self.halvings):
            head = lax.bitwise_xor(head, place_bit(level) * weight)
        return pl.ds(pl.multiple_of(head * HEAD_DIM, HEAD_DIM), width * HEAD_DIM)

    def columns(self, slot):
        return self.start(slot, 1)


def key_value_body(streams, k_ref, v_ref, *rest):
    *pairs, bits_ref, k_out, v_out, sems = rest
    half, run = streams[0].slots // 2, streams[0].run
    groups = streams[0].slots // run
    order = [
        (stream, group)
        for stream in streams
        for group in list(range(groups // 2, groups)) + list(range(groups // 2))
    ]
    copies = []
    for number, (stream, group) in enumerate(order):
        at = stream.start(group * run, run)
        copies.append([
            pltpu.make_async_copy(k_ref.at[:, at], k_out.at[:, at], sems.at[0, number]),
            pltpu.make_async_copy(v_ref.at[:, at], v_out.at[:, at], sems.at[1, number]),
        ])
        for copy in copies[-1]:
            copy.start()
    for level in range(bits_ref.shape[0]):
        bits_ref[level] = jnp.full(bits_ref.shape[1:], place_bit(level).astype(F32), F32)
    for (stream, group), pair in zip(order, copies):
        send_ref, keep_ref = pairs[2 * stream.number : 2 * stream.number + 2]
        for copy in pair:
            copy.wait()
        for slot in range(group * run, (group + 1) * run):
            at = stream.columns(slot)
            state = dot(k_out[:, at], v_out[:, at], TN)
            if slot >= half:
                send_ref[slot - half] = state.astype(BF)
            else:
                keep_ref[slot] = state


def inner_body(stream, q_ref, k_ref, v_ref, probs_ref, inner_ref):
    mask = causal_mask()
    for slot in range(stream.slots):
        at = stream.columns(slot)
        probs = jnp.where(mask, dot(q_ref[:, at], k_ref[:, at], NT), 0.0).astype(BF)
        probs_ref[slot] = probs
        inner_ref[slot] = dot(probs, v_ref[:, at], NN)


def norm_body(stream, base, q_ref, g_ref, inner_ref, state_ref, normed_ref, raw_ref, grad_ref):
    for number in range(state_ref.shape[0]):
        at = stream.columns(base + number)
        query = q_ref[:, at]
        unnormed = inner_ref[base + number] + dot(query, state_ref[number], NN)
        inv = lax.rsqrt(jnp.mean(unnormed * unnormed, axis=-1, keepdims=True) + EPSILON)
        normed = unnormed * inv
        normed_ref[number] = normed.astype(BF)
        cot = g_ref[:, at].astype(F32)
        raw = (cot - normed * jnp.mean(cot * normed, axis=-1, keepdims=True)) * inv
        raw = raw.astype(BF)
        raw_ref[number] = raw
        grad_ref[number] = dot(query, raw, TN).astype(grad_ref.dtype)


def local_grads_body(stream, q_ref, k_ref, v_ref, probs_ref, *rest):
    near_refs, far_refs, rest = rest[:3], rest[3:6], rest[6:]
    *_, gk_ref, gv_ref, normed_out, gq_out, gq_buf, sems = rest
    half = stream.slots // 2
    mask = causal_mask()
    copies = []
    held = [
        tuple(ref.at[slot % half] for ref in (near_refs, far_refs)[slot // half])
        for slot in range(stream.slots)
    ]
    for slot in range(stream.slots):
        at = stream.columns(slot)
        copies.append(
            pltpu.make_async_copy(held[slot][0], normed_out.at[:, at], sems.at[0, slot])
        )
        copies[-1].start()
    for slot in range(stream.slots):
        at = stream.columns(slot)
        raw, state = held[slot][1][...], held[slot][2][...]
        grad_probs = jnp.where(mask, dot(raw, v_ref[:, at], NT), 0.0).astype(BF)
        gq_buf[slot] = (dot(grad_probs, k_ref[:, at], NN) + dot(raw, state, NT)).astype(BF)
        copies.append(
            pltpu.make_async_copy(gq_buf.at[slot], gq_out.at[:, at], sems.at[1, slot])
        )
        copies[-1].start()
        gk_ref[slot] = dot(grad_probs, q_ref[:, at], TN)
        gv_ref[slot] = dot(probs_ref[slot], raw, TN)
    for copy in copies:
        copy.wait()


def last_grads_body(streams, base, k_ref, v_ref, *rest):
    parts = [rest[3 * s : 3 * s + 3] for s in range(len(streams))]
    *_, gk_out, gv_out, gk_buf, gv_buf, sems = rest
    copies = []
    for stream, (gk_ref, gv_ref, state_ref) in zip(streams, parts):
        for number in range(state_ref.shape[0]):
            slot, at = base + number, stream.columns(base + number)
            state, to = state_ref[number], (stream.number, number)
            gk_buf[to] = (gk_ref[slot] + dot(v_ref[:, at], state, NT)).astype(BF)
            copies.append(pltpu.make_async_copy(gk_buf.at[to], gk_out.at[:, at], sems.at[0, *to]))
            copies[-1].start()
            gv_buf[to] = (gv_ref[slot] + dot(k_ref[:, at], state, NN)).astype(BF)
            copies.append(pltpu.make_async_copy(gv_buf.at[to], gv_out.at[:, at], sems.at[1, *to]))
            copies[-1].start()
    for copy in copies:
        copy.wait()


def hbm(shape, dtype):
    return jax.ShapeDtypeStruct(shape, dtype)


def call(body, arrays, outs, flops, scratch=(), raw_in=False, partial=()):
    if raw_in:
        arrays = [pltpu.with_memory_space_constraint(a, pltpu.HBM) for a in arrays]
    vmem, anywhere = pl.BlockSpec(memory_space=pltpu.VMEM), pl.BlockSpec(memory_space=pl.ANY)
    operands = [*arrays, *partial]
    in_specs = [pl.BlockSpec(memory_space=pltpu.HBM) if raw_in else vmem] * len(arrays) + [anywhere] * len(partial)
    whole = [isinstance(out, jax.ShapeDtypeStruct) for out in outs]
    first = whole.index(True) if True in whole else 0
    aliases = {len(arrays) + i: first + i for i in range(len(partial))}
    size = sum(a.size * a.dtype.itemsize for a in arrays) * 2
    return pl.pallas_call(
        body,
        out_shape=outs,
        in_specs=in_specs,
        out_specs=[anywhere if w else vmem for w in whole],
        scratch_shapes=list(scratch),
        input_output_aliases=aliases,
        compiler_params=pltpu.CompilerParams(vmem_limit_bytes=8 * 1024 * 1024),
        cost_estimate=pl.CostEstimate(flops=flops, bytes_accessed=size, transcendentals=0),
    )(*operands)


def swap(value, axis, bit):
    pairs = [(i, i ^ bit) for i in range(lax.axis_size(axis))]
    return lax.ppermute(value, axis, pairs)


def bits_of(axis):
    return [1 << b for b in range(lax.axis_size(axis).bit_length() - 1)]


def gated(value, bits, level, wanted):
    return jnp.where(bits[level, :1][None] == wanted, value, 0.0)


def scan_states(sends, keeps, bits, reverse, asides):
    levels = [(axis, bit) for axis in ("sub", "head") for bit in bits_of(axis)]
    streams = range(len(sends))
    upper, lower = (0.0, 1.0) if reverse else (1.0, 0.0)
    sends, totals, saved = list(sends), list(keeps), []
    given = {}

    def exchange(value, axis, bit, at):
        if at not in asides:
            return swap(value, axis, bit).astype(F32)
        work, operands = asides[at]
        value, operands = lax.optimization_barrier((value, operands))
        got, given[at] = lax.optimization_barrier((swap(value, axis, bit), work(operands)))
        return got.astype(F32)

    for number, (axis, bit) in enumerate(levels):
        row = []
        for s in streams:
            if number:
                half = totals[s].shape[0] // 2
                sends[s], totals[s] = totals[s][half:].astype(BF), totals[s][:half]
            got = exchange(sends[s], axis, bit, (number, s))
            row.append((totals[s], got))
            totals[s] = totals[s] + got
        saved.append((axis, bit, row))
    carried = [jnp.zeros_like(total) for total in totals]
    for number, bit in enumerate(bits_of("seq"), len(levels)):
        for s in streams:
            got = exchange(totals[s].astype(BF), "seq", bit, (number, s))
            carried[s] = carried[s] + gated(got, bits, number, upper)
            totals[s] = totals[s] + got
    near, far = [None] * len(sends), [None] * len(sends)
    for number, (axis, bit, row) in reversed(list(enumerate(saved))):
        for s in streams:
            own, got = row[s]
            message = (carried[s] + gated(own, bits, number, lower)).astype(BF)
            known = carried[s] + gated(got, bits, number, upper)
            near[s], far[s] = known.astype(BF), swap(message, axis, bit)
            if number:
                carried[s] = jnp.concatenate([known, far[s].astype(F32)], axis=0)
    return near, far, given


def spread(streams):
    plane = len(bits_of("sub")) + len(bits_of("head"))
    return [(plane - 1 + stream.number, STREAMS - 1) for stream in streams]


def on_device(query, key, value, cot):
    rows, width = query.shape
    heads = width // HEAD_DIM
    plane = lax.axis_size("head") * lax.axis_size("sub")
    levels = lax.axis_size(AXES).bit_length() - 1
    streams = [Stream(s, heads, plane) for s in range(STREAMS)]
    count, slots, half = len(streams), streams[0].slots, streams[0].slots // 2
    half_state = (half, HEAD_DIM, HEAD_DIM)
    full_state = (slots, HEAD_DIM, HEAD_DIM)
    unit = 2 * BLOCK * HEAD_DIM * HEAD_DIM * slots
    vm, dma = pltpu.VMEM, pltpu.SemaphoreType.DMA

    *states, bits, key_vm, value_vm = call(
        functools.partial(key_value_body, streams), (key, value),
        [vm(half_state, BF), vm(half_state, F32)] * count
        + [vm((levels, 8, HEAD_DIM), F32), vm((rows, width), BF), vm((rows, width), BF)],
        unit * count, (dma((2, heads // streams[0].run)),), raw_in=True,
    )
    def inner_work(stream, operands):
        return call(
            functools.partial(inner_body, stream), operands,
            [vm(full_state, BF), vm(full_state, F32)], 2 * unit,
        )

    spots = spread(streams)
    near, far, inner = scan_states(
        states[0::2], states[1::2], bits, False,
        {
            spot: (functools.partial(inner_work, stream), (query, key_vm, value_vm))
            for spot, stream in zip(spots, streams)
        },
    )
    inner = [inner[spot] for spot in spots]

    def norm(s, base, state, dtype):
        return call(
            functools.partial(norm_body, streams[s], base), (query, cot, inner[s][1], state),
            [vm(half_state, BF), vm(half_state, BF), vm(half_state, dtype)], unit,
        )

    normed_near, normed_far = [], []
    for s in range(count):
        normed_near.append(norm(s, 0, near[s], F32))
        far[s], normed_near[s] = lax.optimization_barrier((far[s], normed_near[s]))
        normed_far.append(norm(s, half, far[s], BF))
    partials = ()

    def local_grads(stream, operands):
        nonlocal partials
        out = call(
            functools.partial(local_grads_body, stream), operands,
            [vm(full_state, F32), vm(full_state, F32), hbm((rows, width), BF), hbm((rows, width), BF)],
            5 * unit, (vm(full_state, BF), dma((2, slots))), partial=partials,
        )
        partials = out[2:]
        return out[:2]

    near, far, outs = scan_states(
        [n[2] for n in normed_far], [n[2] for n in normed_near], bits, True,
        {
            spot: (
                functools.partial(local_grads, stream),
                (query, key_vm, value_vm, inner[s][0], *normed_near[s][:2], near[s], *normed_far[s][:2], far[s]),
            )
            for s, (spot, stream) in enumerate(zip(spots, streams))
        },
    )
    outs = [outs[spot] for spot in spots]
    normed_out, grad_q = partials
    partials = ()
    for base in (0, half):
        found = far if base else near
        buf = vm((count, *half_state), BF)
        operands = [a for s in range(count) for a in (*outs[s], found[s])]
        partials = call(
            functools.partial(last_grads_body, streams, base), (key_vm, value_vm, *operands),
            [hbm((rows, width), BF), hbm((rows, width), BF)], 2 * unit,
            (buf, buf, dma((2, count, half))), partial=partials,
        )
        if base == 0:
            far, partials = lax.optimization_barrier((far, partials))
    grad_k, grad_v = partials
    return normed_out, grad_q, grad_k, grad_v


def solution(mesh):
    placed = P(("group", "seq", "head", "sub"), None)
    return jax.shard_map(
        on_device,
        mesh=mesh,
        in_specs=(placed,) * 4,
        out_specs=(placed,) * 4,
        check_vma=False,
    )
```

time: 69.8 us -> 60.2 us (0.86)
  waiting for transfers between devices: 37.7 us -> 18.8 us
  starting transfers between devices: 13.8 us -> 24.9 us
  Pallas kernels: 9.85 us -> 14.1 us
  local copies, waits for them, and re-layouts: 4.07 us -> 0.36 us
  other arithmetic: 3.24 us -> 0.82 us
    ppermute x12 -> x24, waiting for transfers between devices: 37.7 us -> 18.8 us  [swap(): return lax.ppermute(value, axis, pairs)]
    ppermute x12 -> x24, starting transfers between devices: 13.8 us -> 24.9 us  [swap(): return lax.ppermute(value, axis, pairs)]
    pallas_call x5 -> x11, Pallas kernels: 9.85 us -> 14.1 us  [call(): pl.pallas_call(body, out_shape=outs, in_specs=in_specs, out_specs=[anywhe...]
    unnamed x22 -> x4, local copies, waits for them, and re-layouts: 4.02 us -> 0.31 us
    add x4 -> x6, other arithmetic: 2.11 us -> 0.3 us  [the longest x2 0.2 us: scan_states(): known = carried[s] + gated(got, bits, number, upper)]
  transfers between devices with their start and end apart: 12 -> 24, of which waited for: 10 -> 13; matrix products, arithmetic and copies ran while one was open for 0% -> 1% of each run, Pallas kernels for 9% -> 17%
where the time goes in v2:
time: 60.2 us; the launch traced here: 60 us
  starting transfers between devices  24.9 us (41%)
  waiting for transfers between devices  18.8 us (31%)
  Pallas kernels  14.1 us (23%)
  between operations  0.91 us (2%)
  other arithmetic  0.82 us (1%)
    ppermute x24, starting transfers between devices, swap(): return lax.ppermute(value, axis, pairs)  24.9 us
    ppermute x24, waiting for transfers between devices, swap(): return lax.ppermute(value, axis, pairs)  18.8 us
    pallas_call x11, Pallas kernels, call(): pl.pallas_call(body, out_shape=outs, in_specs=in_specs, out_specs=[anywhe...  14.1 us
  transfers between devices with their start and end apart: 24, of which 13 were waited for; matrix products, arithmetic and copies ran while one was open for 1% of the time, Pallas kernels for 17%

profile of v2, /device:TPU:0, one launch (start us, length us, event | category | flops | bytes accessed | tf_op | source)
XLA Modules:
  0.0 60.0 jit_solution(11559583275625312428)
XLA Ops:
  0.6 2.7 %shard_map.75 = (bf16[4,128,128]{2,1,0:T(8,128)(2,1)S(1)}, f32[4,128,128]{2,1,0:T(8,128)S(1)}, bf16[4,128,128]{2,1,0:T(8,128)(2,1)S(1)}, f32[4,128,128]{2,1,0:T(...) custom-call(bf16[128,2048]{1,0:T(8,128)(2,1)} %k_ref.1, ...), custom_call_target="tpu_custom_call" | custom-call | flops 67108864 | bytes 2097152 | tf_op jit(solution)/shard_map/pallas_call | solution.py:177
  4.9 2.9 %collective-permute-start.1 = (bf16[2,128,128]{2,1,0:T(8,128)(2,1)S(1)}, bf16[2,128,128]{2,1,0:T(8,128)(2,1)S(1)}, u32[]{:S(2)}, u32[]{:S(2)}) collective-permute-start(bf16[2,128,128]{2,1,0:T(8,128)(2,1)S(1)} %slice.119), channel_id=1, source_target_pairs={{0,2},{2,0},{1,3},{3,1},{4,6},{6,4},{5,7},{7,5},{8,10},{10,8},{9,1... | collective-permute-start | bytes 196616 | tf_op jit(solution)/shard_map/ppermute | solution.py:191
  8.0 1.4 %shard_map.76 = (bf16[8,128,128]{2,1,0:T(8,128)(2,1)S(1)}, f32[8,128,128]{2,1,0:T(8,128)S(1)}) custom-call(bf16[128,2048]{1,0:T(8,128)(2,1)S(1)} %copy-done, bf16[128,2048]{1,0:T(8,128)(2,1)S(1)} %get-tuple-element.151.k_ref, bf16[128,2048]{1,0:T(8,128)(2,1)S(1)} %get-tuple-element.152.v_ref), custom_call_target="tpu_custom_call" | custom-call | flops 67108864 | bytes 3145728 | tf_op jit(solution)/shard_map/pallas_call | solution.py:177
  10.3 2.3 %collective-permute-start.2 = (bf16[2,128,128]{2,1,0:T(8,128)(2,1)S(1)}, bf16[2,128,128]{2,1,0:T(8,128)(2,1)S(1)}, u32[]{:S(2)}, u32[]{:S(2)}) collective-permute-start(bf16[2,128,128]{2,1,0:T(8,128)(2,1)S(1)} %fusion.20), channel_id=1, source_target_pairs={{0,4},{4,0},{8,12},{12,8},{1,5},{5,1},{9,13},{13,9},{2,6},{6,2},{1... | collective-permute-start | bytes 196616 | tf_op jit(solution)/shard_map/ppermute | solution.py:191
  12.6 1.3 %collective-permute-start.9 = (bf16[2,128,128]{2,1,0:T(8,128)(2,1)S(1)}, bf16[2,128,128]{2,1,0:T(8,128)(2,1)S(1)}, u32[]{:S(2)}, u32[]{:S(2)}) collective-permute-start(bf16[2,128,128]{2,1,0:T(8,128)(2,1)S(1)} %fusion.21), channel_id=1, source_target_pairs={{0,4},{4,0},{8,12},{12,8},{1,5},{5,1},{9,13},{13,9},{2,6},{6,2},{1... | collective-permute-start | bytes 196616 | tf_op jit(solution)/shard_map/ppermute | solution.py:191
  13.9 1.4 %shard_map.77 = (bf16[8,128,128]{2,1,0:T(8,128)(2,1)S(1)}, f32[8,128,128]{2,1,0:T(8,128)S(1)}) custom-call(bf16[128,2048]{1,0:T(8,128)(2,1)S(1)} %copy-done, bf16[128,2048]{1,0:T(8,128)(2,1)S(1)} %get-tuple-element.151.k_ref, bf16[128,2048]{1,0:T(8,128)(2,1)S(1)} %get-tuple-element.152.v_ref), custom_call_target="tpu_custom_call" | custom-call | flops 67108864 | bytes 3145728 | tf_op jit(solution)/shard_map/pallas_call | solution.py:177
  15.3 2.7 %collective-permute-start.3 = (bf16[2,128,128]{2,1,0:T(8,128)(2,1)S(1)}, bf16[2,128,128]{2,1,0:T(8,128)(2,1)S(1)}, u32[]{:S(2)}, u32[]{:S(2)}) collective-permute-start(bf16[2,128,128]{2,1,0:T(8,128)(2,1)S(1)} %fusion.10), channel_id=1, source_target_pairs={{0,8},{4,12},{8,0},{12,4},{1,9},{5,13},{9,1},{13,5},{2,10},{6,14},... | collective-permute-start | bytes 196616 | tf_op jit(solution)/shard_map/ppermute | solution.py:191
  18.0 1.6 %collective-permute-start.10 = (bf16[2,128,128]{2,1,0:T(8,128)(2,1)S(1)}, bf16[2,128,128]{2,1,0:T(8,128)(2,1)S(1)}, u32[]{:S(2)}, u32[]{:S(2)}) collective-permute-start(bf16[2,128,128]{2,1,0:T(8,128)(2,1)S(1)} %fusion.13), channel_id=1, source_target_pairs={{0,8},{4,12},{8,0},{12,4},{1,9},{5,13},{9,1},{13,5},{2,10},{6,14},... | collective-permute-start | bytes 196616 | tf_op jit(solution)/shard_map/ppermute | solution.py:191
  19.6 3.0 %collective-permute-done.3 = bf16[2,128,128]{2,1,0:T(8,128)(2,1)S(1)} collective-permute-done((bf16[2,128,128]{2,1,0:T(8,128)(2,1)S(1)}, bf16[2,128,128]{2,1,0:T(8,128)(2,1)S(1)}, u32[]{:S(2)}, u32[]{:S(2)}) %collective-permute-start.3) | collective-permute-done | bytes 65568 | tf_op jit(solution)/shard_map/ppermute | solution.py:191
  23.4 1.9 %collective-permute-start.4 = (bf16[2,128,128]{2,1,0:T(8,128)(2,1)S(1)}, bf16[2,128,128]{2,1,0:T(8,128)(2,1)S(1)}, u32[]{:S(2)}, u32[]{:S(2)}) collective-permute-start(bf16[2,128,128]{2,1,0:T(8,128)(2,1)S(1)} %get-tuple-element.197), channel_id=1, source_target_pairs={{0,2},{2,0},{1,3},{3,1},{4,6},{6,4},{5,7},{7,5},{8,10},{10,8},{9,1... | collective-permute-start | bytes 196616 | tf_op jit(solution)/shard_map/ppermute | solution.py:191
  25.5 2.6 %collective-permute-done.4 = bf16[2,128,128]{2,1,0:T(8,128)(2,1)S(1)} collective-permute-done((bf16[2,128,128]{2,1,0:T(8,128)(2,1)S(1)}, bf16[2,128,128]{2,1,0:T(8,128)(2,1)S(1)}, u32[]{:S(2)}, u32[]{:S(2)}) %collective-permute-start.4) | collective-permute-done | bytes 65568 | tf_op jit(solution)/shard_map/ppermute | solution.py:191
  28.2 1.4 %collective-permute-done.11 = bf16[2,128,128]{2,1,0:T(8,128)(2,1)S(1)} collective-permute-done((bf16[2,128,128]{2,1,0:T(8,128)(2,1)S(1)}, bf16[2,128,128]{2,1,0:T(8,128)(2,1)S(1)}, u32[]{:S(2)}, u32[]{:S(2)}) %collective-permute-start.11) | collective-permute-done | bytes 65568 | tf_op jit(solution)/shard_map/ppermute | solution.py:191
  34.5 1.2 %collective-permute-start.15 = (bf16[2,128,128]{2,1,0:T(8,128)(2,1)S(1)}, bf16[2,128,128]{2,1,0:T(8,128)(2,1)S(1)}, u32[]{:S(2)}, u32[]{:S(2)}) collective-permute-start(bf16[2,128,128]{2,1,0:T(8,128)(2,1)S(1)} %slice.116), channel_id=1, source_target_pairs={{0,2},{2,0},{1,3},{3,1},{4,6},{6,4},{5,7},{7,5},{8,10},{10,8},{9,1... | collective-permute-start | bytes 196616 | tf_op jit(solution)/shard_map/ppermute | solution.py:191
  35.7 2.1 %shard_map.82 = (f32[8,128,128]{2,1,0:T(8,128)S(1)}, f32[8,128,128]{2,1,0:T(8,128)S(1)}, bf16[128,2048]{1,0:T(8,128)(2,1)}, bf16[128,2048]{1,0:T(8,128)(2,1)}) custom-call(bf16[128,2048]{1,0:T(8,128)(2,1)S(1)} %copy-done, bf16[128,2048]{1,0:T(8,128)(2,1)S(1)} %get-tuple-element.151.k_ref, bf16[128,2048]{1,0:T(8,128)(2,1)S(1)} %get-tuple-element.152.v_ref, ...), custom_call_target="tpu_custom_call" | custom-call | flops 167772160 | bytes 5242880 | tf_op jit(solution)/shard_map/pallas_call | solution.py:177
  38.3 1.5 %collective-permute-start.20 = (bf16[2,128,128]{2,1,0:T(8,128)(2,1)S(1)}, bf16[2,128,128]{2,1,0:T(8,128)(2,1)S(1)}, u32[]{:S(2)}, u32[]{:S(2)}) collective-permute-start(bf16[2,128,128]{2,1,0:T(8,128)(2,1)S(1)} %fusion.22), channel_id=1, source_target_pairs={{0,4},{4,0},{8,12},{12,8},{1,5},{5,1},{9,13},{13,9},{2,6},{6,2},{1... | collective-permute-start | bytes 196616 | tf_op jit(solution)/shard_map/ppermute | solution.py:191
  40.7 2.1 %shard_map.83 = (f32[8,128,128]{2,1,0:T(8,128)S(1)}, f32[8,128,128]{2,1,0:T(8,128)S(1)}, bf16[128,2048]{1,0:T(8,128)(2,1)}, bf16[128,2048]{1,0:T(8,128)(2,1)}) custom-call(bf16[128,2048]{1,0:T(8,128)(2,1)S(1)} %copy-done, bf16[128,2048]{1,0:T(8,128)(2,1)S(1)} %get-tuple-element.151.k_ref, ...), custom_call_target="tpu_custom_call", output_to_operand_aliasing={{2}: (10, {}), {3}: (11, {})} | custom-call | flops 167772160 | bytes 5242880 | tf_op jit(solution)/shard_map/pallas_call | solution.py:177
  43.1 1.9 %collective-permute-start.21 = (bf16[2,128,128]{2,1,0:T(8,128)(2,1)S(1)}, bf16[2,128,128]{2,1,0:T(8,128)(2,1)S(1)}, u32[]{:S(2)}, u32[]{:S(2)}) collective-permute-start(bf16[2,128,128]{2,1,0:T(8,128)(2,1)S(1)} %fusion.19), channel_id=1, source_target_pairs={{0,8},{4,12},{8,0},{12,4},{1,9},{5,13},{9,1},{13,5},{2,10},{6,14},... | collective-permute-start | bytes 196616 | tf_op jit(solution)/shard_map/ppermute | solution.py:191
  45.0 1.2 %collective-permute-start.17 = (bf16[2,128,128]{2,1,0:T(8,128)(2,1)S(1)}, bf16[2,128,128]{2,1,0:T(8,128)(2,1)S(1)}, u32[]{:S(2)}, u32[]{:S(2)}) collective-permute-start(bf16[2,128,128]{2,1,0:T(8,128)(2,1)S(1)} %fusion.17), channel_id=1, source_target_pairs={{0,8},{4,12},{8,0},{12,4},{1,9},{5,13},{9,1},{13,5},{2,10},{6,14},... | collective-permute-start | bytes 196616 | tf_op jit(solution)/shard_map/ppermute | solution.py:191
  46.2 4.1 %collective-permute-done.21 = bf16[2,128,128]{2,1,0:T(8,128)(2,1)S(1)} collective-permute-done((bf16[2,128,128]{2,1,0:T(8,128)(2,1)S(1)}, bf16[2,128,128]{2,1,0:T(8,128)(2,1)S(1)}, u32[]{:S(2)}, u32[]{:S(2)}) %collective-permute-start.21) | collective-permute-done | bytes 65568 | tf_op jit(solution)/shard_map/ppermute | solution.py:191
  50.3 1.4 %collective-permute-done.17 = bf16[2,128,128]{2,1,0:T(8,128)(2,1)S(1)} collective-permute-done((bf16[2,128,128]{2,1,0:T(8,128)(2,1)S(1)}, bf16[2,128,128]{2,1,0:T(8,128)(2,1)S(1)}, u32[]{:S(2)}, u32[]{:S(2)}) %collective-permute-start.17) | collective-permute-done | bytes 65568 | tf_op jit(solution)/shard_map/ppermute | solution.py:191
  52.2 1.7 %collective-permute-start.22 = (bf16[2,128,128]{2,1,0:T(8,128)(2,1)S(1)}, bf16[2,128,128]{2,1,0:T(8,128)(2,1)S(1)}, u32[]{:S(2)}, u32[]{:S(2)}) collective-permute-start(bf16[2,128,128]{2,1,0:T(8,128)(2,1)S(1)} %get-tuple-element.208), channel_id=1, source_target_pairs={{0,2},{2,0},{1,3},{3,1},{4,6},{6,4},{5,7},{7,5},{8,10},{10,8},{9,1... | collective-permute-start | bytes 196616 | tf_op jit(solution)/shard_map/ppermute | solution.py:191
  54.0 2.2 %collective-permute-done.18 = bf16[2,128,128]{2,1,0:T(8,128)(2,1)S(1)} collective-permute-done((bf16[2,128,128]{2,1,0:T(8,128)(2,1)S(1)}, bf16[2,128,128]{2,1,0:T(8,128)(2,1)S(1)}, u32[]{:S(2)}, u32[]{:S(2)}) %collective-permute-start.18) | collective-permute-done | bytes 65568 | tf_op jit(solution)/shard_map/ppermute | solution.py:191
  57.6 1.1 %shard_map.84 = (bf16[128,2048]{1,0:T(8,128)(2,1)}, bf16[128,2048]{1,0:T(8,128)(2,1)}) custom-call(bf16[128,2048]{1,0:T(8,128)(2,1)S(1)} %get-tuple-element.151.k_ref, bf16[128,2048]{1,0:T(8,128)(2,1)S(1)} %get-tuple-element.152.v_ref, f32[8,128,128]{2,1,0:T(8,128)S(1)} %get-tuple-element.164.rest_0_, f32[8,128,128]{2,1,0:T(8,128)S(1)} %get-tuple-element.165.rest_1_, ...), custom_call_target="tpu_custom_call" | custom-call | flops 67108864 | bytes 6815744 | tf_op jit(solution)/shard_map/pallas_call | solution.py:177
  58.8 1.1 %shard_map.85 = (bf16[128,2048]{1,0:T(8,128)(2,1)}, bf16[128,2048]{1,0:T(8,128)(2,1)}) custom-call(bf16[128,2048]{1,0:T(8,128)(2,1)S(1)} %get-tuple-element.151.k_ref, bf16[128,2048]{1,0:T(8,128)(2,1)S(1)} %get-tuple-element.152.v_ref, f32[8,128,128]{2,1,0:T(8,128)S(1)} %get-tuple-element.164.rest_0_, ...), custom_call_target="tpu_custom_call", output_to_operand_aliasing={{0}: (8, {}), {1}: (9, {})} | custom-call | flops 67108864 | bytes 6815744 | tf_op jit(solution)/shard_map/pallas_call | solution.py:177
  (64 shorter events, 12.1 us)
Async XLA Ops:
  3.4 1.5 %collective-permute-start = (bf16[4,128,128]{2,1,0:T(8,128)(2,1)S(1)}, bf16[4,128,128]{2,1,0:T(8,128)(2,1)S(1)}, u32[]{:S(2)}, u32[]{:S(2)}) collective-permute-start(bf16[4,128,128]{2,1,0:T(8,128)(2,1)S(1)} %get-tuple-element.95), channel_id=1, source_target_pairs={{0,1},{1,0},{2,3},{3,2},{4,5},{5,4},{6,7},{7,6},{8,9},{9,8},{10,11... | collective-permute-start | bytes 393224 | tf_op jit(solution)/shard_map/ppermute | solution.py:191
  3.9 4.0 %collective-permute-start.7 = (bf16[4,128,128]{2,1,0:T(8,128)(2,1)S(1)}, bf16[4,128,128]{2,1,0:T(8,128)(2,1)S(1)}, u32[]{:S(2)}, u32[]{:S(2)}) collective-permute-start(bf16[4,128,128]{2,1,0:T(8,128)(2,1)S(1)} %get-tuple-element.121), channel_id=1, source_target_pairs={{0,1},{1,0},{2,3},{3,2},{4,5},{5,4},{6,7},{7,6},{8,9},{9,8},{10,11... | collective-permute-start | bytes 393224 | tf_op jit(solution)/shard_map/ppermute | solution.py:191
  4.9 5.3 %collective-permute-start.1 = (bf16[2,128,128]{2,1,0:T(8,128)(2,1)S(1)}, bf16[2,128,128]{2,1,0:T(8,128)(2,1)S(1)}, u32[]{:S(2)}, u32[]{:S(2)}) collective-permute-start(bf16[2,128,128]{2,1,0:T(8,128)(2,1)S(1)} %slice.119), channel_id=1, source_target_pairs={{0,2},{2,0},{1,3},{3,1},{4,6},{6,4},{5,7},{7,5},{8,10},{10,8},{9,1... | collective-permute-start | bytes 196616 | tf_op jit(solution)/shard_map/ppermute | solution.py:191
  7.9 4.7 %collective-permute-start.8 = (bf16[2,128,128]{2,1,0:T(8,128)(2,1)S(1)}, bf16[2,128,128]{2,1,0:T(8,128)(2,1)S(1)}, u32[]{:S(2)}, u32[]{:S(2)}) collective-permute-start(bf16[2,128,128]{2,1,0:T(8,128)(2,1)S(1)} %slice.117), channel_id=1, source_target_pairs={{0,2},{2,0},{1,3},{3,1},{4,6},{6,4},{5,7},{7,5},{8,10},{10,8},{9,1... | collective-permute-start | bytes 196616 | tf_op jit(solution)/shard_map/ppermute | solution.py:191
  10.3 5.0 %collective-permute-start.2 = (bf16[2,128,128]{2,1,0:T(8,128)(2,1)S(1)}, bf16[2,128,128]{2,1,0:T(8,128)(2,1)S(1)}, u32[]{:S(2)}, u32[]{:S(2)}) collective-permute-start(bf16[2,128,128]{2,1,0:T(8,128)(2,1)S(1)} %fusion.20), channel_id=1, source_target_pairs={{0,4},{4,0},{8,12},{12,8},{1,5},{5,1},{9,13},{13,9},{2,6},{6,2},{1... | collective-permute-start | bytes 196616 | tf_op jit(solution)/shard_map/ppermute | solution.py:191
  12.6 5.4 %collective-permute-start.9 = (bf16[2,128,128]{2,1,0:T(8,128)(2,1)S(1)}, bf16[2,128,128]{2,1,0:T(8,128)(2,1)S(1)}, u32[]{:S(2)}, u32[]{:S(2)}) collective-permute-start(bf16[2,128,128]{2,1,0:T(8,128)(2,1)S(1)} %fusion.21), channel_id=1, source_target_pairs={{0,4},{4,0},{8,12},{12,8},{1,5},{5,1},{9,13},{13,9},{2,6},{6,2},{1... | collective-permute-start | bytes 196616 | tf_op jit(solution)/shard_map/ppermute | solution.py:191
  15.3 7.3 %collective-permute-start.3 = (bf16[2,128,128]{2,1,0:T(8,128)(2,1)S(1)}, bf16[2,128,128]{2,1,0:T(8,128)(2,1)S(1)}, u32[]{:S(2)}, u32[]{:S(2)}) collective-permute-start(bf16[2,128,128]{2,1,0:T(8,128)(2,1)S(1)} %fusion.10), channel_id=1, source_target_pairs={{0,8},{4,12},{8,0},{12,4},{1,9},{5,13},{9,1},{13,5},{2,10},{6,14},... | collective-permute-start | bytes 196616 | tf_op jit(solution)/shard_map/ppermute | solution.py:191
  18.0 5.4 %collective-permute-start.10 = (bf16[2,128,128]{2,1,0:T(8,128)(2,1)S(1)}, bf16[2,128,128]{2,1,0:T(8,128)(2,1)S(1)}, u32[]{:S(2)}, u32[]{:S(2)}) collective-permute-start(bf16[2,128,128]{2,1,0:T(8,128)(2,1)S(1)} %fusion.13), channel_id=1, source_target_pairs={{0,8},{4,12},{8,0},{12,4},{1,9},{5,13},{9,1},{13,5},{2,10},{6,14},... | collective-permute-start | bytes 196616 | tf_op jit(solution)/shard_map/ppermute | solution.py:191
  23.4 4.7 %collective-permute-start.4 = (bf16[2,128,128]{2,1,0:T(8,128)(2,1)S(1)}, bf16[2,128,128]{2,1,0:T(8,128)(2,1)S(1)}, u32[]{:S(2)}, u32[]{:S(2)}) collective-permute-start(bf16[2,128,128]{2,1,0:T(8,128)(2,1)S(1)} %get-tuple-element.197), channel_id=1, source_target_pairs={{0,2},{2,0},{1,3},{3,1},{4,6},{6,4},{5,7},{7,5},{8,10},{10,8},{9,1... | collective-permute-start | bytes 196616 | tf_op jit(solution)/shard_map/ppermute | solution.py:191
  25.4 4.3 %collective-permute-start.11 = (bf16[2,128,128]{2,1,0:T(8,128)(2,1)S(1)}, bf16[2,128,128]{2,1,0:T(8,128)(2,1)S(1)}, u32[]{:S(2)}, u32[]{:S(2)}) collective-permute-start(bf16[2,128,128]{2,1,0:T(8,128)(2,1)S(1)} %get-tuple-element.206), channel_id=1, source_target_pairs={{0,2},{2,0},{1,3},{3,1},{4,6},{6,4},{5,7},{7,5},{8,10},{10,8},{9,1... | collective-permute-start | bytes 196616 | tf_op jit(solution)/shard_map/ppermute | solution.py:191
  29.8 1.4 %collective-permute-start.5 = (bf16[4,128,128]{2,1,0:T(8,128)(2,1)S(1)}, bf16[4,128,128]{2,1,0:T(8,128)(2,1)S(1)}, u32[]{:S(2)}, u32[]{:S(2)}) collective-permute-start(bf16[4,128,128]{2,1,0:T(8,128)(2,1)S(1)} %get-tuple-element.189), channel_id=1, source_target_pairs={{0,1},{1,0},{2,3},{3,2},{4,5},{5,4},{6,7},{7,6},{8,9},{9,8},{10,11... | collective-permute-start | bytes 393224 | tf_op jit(solution)/shard_map/ppermute | solution.py:191
  29.9 2.6 %collective-permute-start.12 = (bf16[4,128,128]{2,1,0:T(8,128)(2,1)S(1)}, bf16[4,128,128]{2,1,0:T(8,128)(2,1)S(1)}, u32[]{:S(2)}, u32[]{:S(2)}) collective-permute-start(bf16[4,128,128]{2,1,0:T(8,128)(2,1)S(1)} %get-tuple-element.210), channel_id=1, source_target_pairs={{0,1},{1,0},{2,3},{3,2},{4,5},{5,4},{6,7},{7,6},{8,9},{9,8},{10,11... | collective-permute-start | bytes 393224 | tf_op jit(solution)/shard_map/ppermute | solution.py:191
  31.8 1.7 %collective-permute-start.6 = (bf16[4,128,128]{2,1,0:T(8,128)(2,1)S(1)}, bf16[4,128,128]{2,1,0:T(8,128)(2,1)S(1)}, u32[]{:S(2)}, u32[]{:S(2)}) collective-permute-start(bf16[4,128,128]{2,1,0:T(8,128)(2,1)S(1)} %get-tuple-element.118), channel_id=1, source_target_pairs={{0,1},{1,0},{2,3},{3,2},{4,5},{5,4},{6,7},{7,6},{8,9},{9,8},{10,11... | collective-permute-start | bytes 393224 | tf_op jit(solution)/shard_map/ppermute | solution.py:191
  33.0 1.4 %collective-permute-start.14 = (bf16[4,128,128]{2,1,0:T(8,128)(2,1)S(1)}, bf16[4,128,128]{2,1,0:T(8,128)(2,1)S(1)}, u32[]{:S(2)}, u32[]{:S(2)}) collective-permute-start(bf16[4,128,128]{2,1,0:T(8,128)(2,1)S(1)} %get-tuple-element.167), channel_id=1, source_target_pairs={{0,1},{1,0},{2,3},{3,2},{4,5},{5,4},{6,7},{7,6},{8,9},{9,8},{10,11... | collective-permute-start | bytes 393224 | tf_op jit(solution)/shard_map/ppermute | solution.py:191
  33.5 4.7 %collective-permute-start.13 = (bf16[2,128,128]{2,1,0:T(8,128)(2,1)S(1)}, bf16[2,128,128]{2,1,0:T(8,128)(2,1)S(1)}, u32[]{:S(2)}, u32[]{:S(2)}) collective-permute-start(bf16[2,128,128]{2,1,0:T(8,128)(2,1)S(1)} %slice.118), channel_id=1, source_target_pairs={{0,2},{2,0},{1,3},{3,1},{4,6},{6,4},{5,7},{7,5},{8,10},{10,8},{9,1... | collective-permute-start | bytes 196616 | tf_op jit(solution)/shard_map/ppermute | solution.py:191
  34.5 5.2 %collective-permute-start.15 = (bf16[2,128,128]{2,1,0:T(8,128)(2,1)S(1)}, bf16[2,128,128]{2,1,0:T(8,128)(2,1)S(1)}, u32[]{:S(2)}, u32[]{:S(2)}) collective-permute-start(bf16[2,128,128]{2,1,0:T(8,128)(2,1)S(1)} %slice.116), channel_id=1, source_target_pairs={{0,2},{2,0},{1,3},{3,1},{4,6},{6,4},{5,7},{7,5},{8,10},{10,8},{9,1... | collective-permute-start | bytes 196616 | tf_op jit(solution)/shard_map/ppermute | solution.py:191
  38.3 4.8 %collective-permute-start.20 = (bf16[2,128,128]{2,1,0:T(8,128)(2,1)S(1)}, bf16[2,128,128]{2,1,0:T(8,128)(2,1)S(1)}, u32[]{:S(2)}, u32[]{:S(2)}) collective-permute-start(bf16[2,128,128]{2,1,0:T(8,128)(2,1)S(1)} %fusion.22), channel_id=1, source_target_pairs={{0,4},{4,0},{8,12},{12,8},{1,5},{5,1},{9,13},{13,9},{2,6},{6,2},{1... | collective-permute-start | bytes 196616 | tf_op jit(solution)/shard_map/ppermute | solution.py:191
  39.8 5.2 %collective-permute-start.16 = (bf16[2,128,128]{2,1,0:T(8,128)(2,1)S(1)}, bf16[2,128,128]{2,1,0:T(8,128)(2,1)S(1)}, u32[]{:S(2)}, u32[]{:S(2)}) collective-permute-start(bf16[2,128,128]{2,1,0:T(8,128)(2,1)S(1)} %fusion.23), channel_id=1, source_target_pairs={{0,4},{4,0},{8,12},{12,8},{1,5},{5,1},{9,13},{13,9},{2,6},{6,2},{1... | collective-permute-start | bytes 196616 | tf_op jit(solution)/shard_map/ppermute | solution.py:191
  43.1 7.3 %collective-permute-start.21 = (bf16[2,128,128]{2,1,0:T(8,128)(2,1)S(1)}, bf16[2,128,128]{2,1,0:T(8,128)(2,1)S(1)}, u32[]{:S(2)}, u32[]{:S(2)}) collective-permute-start(bf16[2,128,128]{2,1,0:T(8,128)(2,1)S(1)} %fusion.19), channel_id=1, source_target_pairs={{0,8},{4,12},{8,0},{12,4},{1,9},{5,13},{9,1},{13,5},{2,10},{6,14},... | collective-permute-start | bytes 196616 | tf_op jit(solution)/shard_map/ppermute | solution.py:191
  45.0 6.7 %collective-permute-start.17 = (bf16[2,128,128]{2,1,0:T(8,128)(2,1)S(1)}, bf16[2,128,128]{2,1,0:T(8,128)(2,1)S(1)}, u32[]{:S(2)}, u32[]{:S(2)}) collective-permute-start(bf16[2,128,128]{2,1,0:T(8,128)(2,1)S(1)} %fusion.17), channel_id=1, source_target_pairs={{0,8},{4,12},{8,0},{12,4},{1,9},{5,13},{9,1},{13,5},{2,10},{6,14},... | collective-permute-start | bytes 196616 | tf_op jit(solution)/shard_map/ppermute | solution.py:191
  51.9 4.3 %collective-permute-start.18 = (bf16[2,128,128]{2,1,0:T(8,128)(2,1)S(1)}, bf16[2,128,128]{2,1,0:T(8,128)(2,1)S(1)}, u32[]{:S(2)}, u32[]{:S(2)}) collective-permute-start(bf16[2,128,128]{2,1,0:T(8,128)(2,1)S(1)} %get-tuple-element.193), channel_id=1, source_target_pairs={{0,2},{2,0},{1,3},{3,1},{4,6},{6,4},{5,7},{7,5},{8,10},{10,8},{9,1... | collective-permute-start | bytes 196616 | tf_op jit(solution)/shard_map/ppermute | solution.py:191
  52.2 4.7 %collective-permute-start.22 = (bf16[2,128,128]{2,1,0:T(8,128)(2,1)S(1)}, bf16[2,128,128]{2,1,0:T(8,128)(2,1)S(1)}, u32[]{:S(2)}, u32[]{:S(2)}) collective-permute-start(bf16[2,128,128]{2,1,0:T(8,128)(2,1)S(1)} %get-tuple-element.208), channel_id=1, source_target_pairs={{0,2},{2,0},{1,3},{3,1},{4,6},{6,4},{5,7},{7,5},{8,10},{10,8},{9,1... | collective-permute-start | bytes 196616 | tf_op jit(solution)/shard_map/ppermute | solution.py:191
  57.1 1.7 %collective-permute-start.19 = (bf16[4,128,128]{2,1,0:T(8,128)(2,1)S(1)}, bf16[4,128,128]{2,1,0:T(8,128)(2,1)S(1)}, u32[]{:S(2)}, u32[]{:S(2)}) collective-permute-start(bf16[4,128,128]{2,1,0:T(8,128)(2,1)S(1)} %get-tuple-element.185), channel_id=1, source_target_pairs={{0,1},{1,0},{2,3},{3,2},{4,5},{5,4},{6,7},{7,6},{8,9},{9,8},{10,11... | collective-permute-start | bytes 393224 | tf_op jit(solution)/shard_map/ppermute | solution.py:191
  57.1 1.7 %collective-permute-start.23 = (bf16[4,128,128]{2,1,0:T(8,128)(2,1)S(1)}, bf16[4,128,128]{2,1,0:T(8,128)(2,1)S(1)}, u32[]{:S(2)}, u32[]{:S(2)}) collective-permute-start(bf16[4,128,128]{2,1,0:T(8,128)(2,1)S(1)} %get-tuple-element.212), channel_id=1, source_target_pairs={{0,1},{1,0},{2,3},{3,2},{4,5},{5,4},{6,7},{7,6},{8,9},{9,8},{10,11... | collective-permute-start | bytes 393224 | tf_op jit(solution)/shard_map/ppermute | solution.py:191
  (2 other events, 4.2 us)

commit v3 on v2

v3 whole, which is shorter than its diff:
```python
import functools

import jax
import jax.numpy as jnp
from jax import lax
from jax.experimental import pallas as pl
from jax.experimental.pallas import tpu as pltpu
from jax.sharding import PartitionSpec as P

HEAD_DIM = 128
BLOCK = 128
EPSILON = 1e-05
BF = jnp.bfloat16
F32 = jnp.float32
NN = (((1,), (0,)), ((), ()))
NT = (((1,), (1,)), ((), ()))
TN = (((0,), (0,)), ((), ()))
AXES = ("seq", "head", "sub")


def dot(left, right, form):
    return lax.dot_general(left, right, form, preferred_element_type=F32)


def causal_mask():
    rows = lax.broadcasted_iota(jnp.int32, (BLOCK, BLOCK), 0)
    cols = lax.broadcasted_iota(jnp.int32, (BLOCK, BLOCK), 1)
    return rows >= cols


def place_bit(level):
    place = lax.axis_index(AXES).astype(jnp.int32)
    return lax.bitwise_and(lax.shift_right_logical(place, jnp.int32(level)), jnp.int32(1))


def bits_in(axis):
    return lax.axis_size(axis).bit_length() - 1


class Plan:
    def __init__(self, heads):
        self.heads, self.half = heads, heads // 2
        self.steps = bits_in("head") + (bits_in("seq") > 0)
        self.groups = 1 << self.steps
        self.kept = self.half // self.groups
        self.part = self.half // 2

    def columns(self, slot, width=1):
        head = jnp.int32(slot)
        for level in range(self.steps + 1):
            head = lax.bitwise_xor(head, place_bit(level) * (self.heads >> (level + 1)))
        return pl.ds(pl.multiple_of(head * HEAD_DIM, HEAD_DIM), width * HEAD_DIM)

    def mask(self, group):
        return sum(((group >> (self.steps - 1 - j)) & 1) << j for j in range(self.steps))

    def base(self, part, far):
        return far * self.half + (1 - part) * self.part


def key_value_body(plan, k_ref, v_ref, *rest):
    *parts, bits_ref, k_out, v_out, sems = rest
    order = [(part, far) for far in (1, 0) for part in (0, 1)]
    copies = {}
    for part, far in order:
        for first in range(plan.base(part, far), plan.base(part, far) + plan.part, plan.kept):
            at, number = plan.columns(first, plan.kept), first // plan.kept
            copies[first] = [
                pltpu.make_async_copy(k_ref.at[:, at], k_out.at[:, at], sems.at[0, number]),
                pltpu.make_async_copy(v_ref.at[:, at], v_out.at[:, at], sems.at[1, number]),
            ]
            for copy in copies[first]:
                copy.start()
    for level in range(bits_ref.shape[0]):
        bits_ref[level] = jnp.full(bits_ref.shape[1:], place_bit(level).astype(F32), F32)
    for (part, far), out_ref in zip(order, parts):
        for number in range(plan.part):
            slot = plan.base(part, far) + number
            for copy in copies.get(slot, ()):
                copy.wait()
            at = plan.columns(slot)
            out_ref[number] = dot(k_out[:, at], v_out[:, at], TN).astype(out_ref.dtype)


def inner_body(plan, base, q_ref, k_ref, v_ref, probs_ref, inner_ref):
    mask = causal_mask()
    for number in range(plan.half):
        at = plan.columns(base + number)
        probs = jnp.where(mask, dot(q_ref[:, at], k_ref[:, at], NT), 0.0).astype(BF)
        probs_ref[number] = probs
        inner_ref[number] = dot(probs, v_ref[:, at], NN)


def norm_body(plan, base, q_ref, g_ref, inner_ref, state_ref, normed_ref, raw_ref, grad_ref):
    for number in range(plan.part):
        at = plan.columns(base + number)
        query = q_ref[:, at]
        unnormed = inner_ref[base % plan.half + number] + dot(query, state_ref[number], NN)
        inv = lax.rsqrt(jnp.mean(unnormed * unnormed, axis=-1, keepdims=True) + EPSILON)
        normed = unnormed * inv
        normed_ref[number] = normed.astype(BF)
        cot = g_ref[:, at].astype(F32)
        raw = (cot - normed * jnp.mean(cot * normed, axis=-1, keepdims=True)) * inv
        raw = raw.astype(BF)
        raw_ref[number] = raw
        grad_ref[number] = dot(query, raw, TN).astype(grad_ref.dtype)


def local_grads_body(plan, far, q_ref, k_ref, v_ref, probs_ref, *rest):
    upper, lower, rest = rest[:3], rest[3:6], rest[6:]
    *_, gk_ref, gv_ref, normed_out, gq_out, gq_buf, sems = rest
    mask = causal_mask()
    copies, held = [], {}
    for part, refs in enumerate((upper, lower)):
        for number in range(plan.part):
            slot = plan.base(part, far) + number
            held[slot] = [ref.at[number] for ref in refs]
    for slot, (normed_ref, _, _) in held.items():
        at, number = plan.columns(slot), slot % plan.half
        copies.append(pltpu.make_async_copy(normed_ref, normed_out.at[:, at], sems.at[0, number]))
        copies[-1].start()
    for slot, (_, raw_ref, state_ref) in held.items():
        at, number = plan.columns(slot), slot % plan.half
        raw, state = raw_ref[...], state_ref[...]
        grad_probs = jnp.where(mask, dot(raw, v_ref[:, at], NT), 0.0).astype(BF)
        gq_buf[number] = (dot(grad_probs, k_ref[:, at], NN) + dot(raw, state, NT)).astype(BF)
        copies.append(pltpu.make_async_copy(gq_buf.at[number], gq_out.at[:, at], sems.at[1, number]))
        copies[-1].start()
        gk_ref[number] = dot(grad_probs, q_ref[:, at], TN)
        gv_ref[number] = dot(probs_ref[number], raw, TN)
    for copy in copies:
        copy.wait()


def last_grads_body(plan, far, k_ref, v_ref, gk_ref, gv_ref, *rest):
    states = rest[:2]
    *_, gk_out, gv_out, gk_buf, gv_buf, sems = rest
    copies = []
    for part, state_ref in enumerate(states):
        for inside in range(plan.part):
            slot = plan.base(part, far) + inside
            at, number = plan.columns(slot), slot % plan.half
            state = state_ref[inside]
            gk_buf[number] = (gk_ref[number] + dot(v_ref[:, at], state, NT)).astype(BF)
            copies.append(
                pltpu.make_async_copy(gk_buf.at[number], gk_out.at[:, at], sems.at[0, number])
            )
            copies[-1].start()
            gv_buf[number] = (gv_ref[number] + dot(k_ref[:, at], state, NN)).astype(BF)
            copies.append(
                pltpu.make_async_copy(gv_buf.at[number], gv_out.at[:, at], sems.at[1, number])
            )
            copies[-1].start()
    for copy in copies:
        copy.wait()


def hbm(shape, dtype):
    return jax.ShapeDtypeStruct(shape, dtype)


def call(body, arrays, outs, flops, scratch=(), raw_in=False, partial=()):
    if raw_in:
        arrays = [pltpu.with_memory_space_constraint(a, pltpu.HBM) for a in arrays]
    vmem, anywhere = pl.BlockSpec(memory_space=pltpu.VMEM), pl.BlockSpec(memory_space=pl.ANY)
    operands = [*arrays, *partial]
    in_specs = [pl.BlockSpec(memory_space=pltpu.HBM) if raw_in else vmem] * len(arrays) + [anywhere] * len(partial)
    whole = [isinstance(out, jax.ShapeDtypeStruct) for out in outs]
    first = whole.index(True) if True in whole else 0
    aliases = {len(arrays) + i: first + i for i in range(len(partial))}
    size = sum(a.size * a.dtype.itemsize for a in arrays) * 2
    return pl.pallas_call(
        body,
        out_shape=outs,
        in_specs=in_specs,
        out_specs=[anywhere if w else vmem for w in whole],
        scratch_shapes=list(scratch),
        input_output_aliases=aliases,
        compiler_params=pltpu.CompilerParams(vmem_limit_bytes=8 * 1024 * 1024),
        cost_estimate=pl.CostEstimate(flops=flops, bytes_accessed=size, transcendentals=0),
    )(*operands)


def swap(value, axes, mask):
    pairs = [(i, i ^ mask) for i in range(lax.axis_size(axes))]
    return lax.ppermute(value, axes, pairs)


def gated(value, bits, level, wanted):
    return jnp.where(bits[level, :1][None] == wanted, value, 0.0)


def before(own, others, target, bits, reverse):
    total = None
    for mask, state in ((0, own), *others.items()):
        if mask != target:
            step = (mask ^ target).bit_length() - 1
            wanted = 1.0 - ((target >> step) & 1)
            term = gated(state, bits, step + 1, 1.0 - wanted if reverse else wanted)
            total = term if total is None else total + term
    return total


def scan_states(plan, sends, keeps, bits, reverse, asides):
    chips = ("seq", "head")
    upper, lower = (0.0, 1.0) if reverse else (1.0, 0.0)
    given = {}

    def beside(name, value, axes, mask):
        if name not in asides:
            return swap(value, axes, mask)
        work, operands = asides[name]
        value, operands = lax.optimization_barrier((value, operands))
        got, given[name] = lax.optimization_barrier((swap(value, axes, mask), work(operands)))
        return got

    share = plan.groups // 2
    members = [range(share, plan.groups), range(share)]
    own, near_got, pair = {}, {}, {}
    for part, (send, keep) in enumerate(zip(sends, keeps)):
        got = swap(send, "sub", 1)
        for number, group in enumerate(members[part]):
            rows = slice(number * plan.kept, (number + 1) * plan.kept)
            own[group], near_got[group] = keep[rows], got[rows].astype(F32)
            pair[group] = own[group] + near_got[group]
    order = [group for part in members for group in part if group]
    others = {}
    for group in order:
        name = "share" if group == order[-1] else ""
        got = beside(name, pair[group].astype(BF), chips, plan.mask(group))
        others[plan.mask(group)] = got.astype(F32)
    total = pair[0]
    for state in others.values():
        total = total + state
    carried = jnp.zeros_like(total)
    for level in range(plan.steps, bits_in(chips)):
        name = "total" if level == bits_in(chips) - 1 else ""
        got = beside(name, total.astype(BF), chips, 1 << level).astype(F32)
        carried = carried + gated(got, bits, level + 1, upper)
        total = total + got
    sums = {0: carried + before(pair[0], others, 0, bits, reverse)}
    for group in order:
        message = carried + before(pair[0], others, plan.mask(group), bits, reverse)
        sums[group] = swap(message.astype(BF), chips, plan.mask(group)).astype(F32)
    near, far = [], []
    for part in members:
        message = [sums[group] + gated(own[group], bits, 0, lower) for group in part]
        known = [sums[group] + gated(near_got[group], bits, 0, upper) for group in part]
        far.append(swap(jnp.concatenate(message).astype(BF), "sub", 1))
        near.append(jnp.concatenate(known).astype(BF))
    return near, far, given


def on_device(query, key, value, cot):
    rows, width = query.shape
    plan = Plan(width // HEAD_DIM)
    levels = bits_in(AXES)
    part_state = (plan.part, HEAD_DIM, HEAD_DIM)
    half_state = (plan.half, HEAD_DIM, HEAD_DIM)
    unit = 2 * BLOCK * HEAD_DIM * HEAD_DIM * plan.half
    vm, dma = pltpu.VMEM, pltpu.SemaphoreType.DMA
    whole = hbm((rows, width), BF)

    *states, bits, key_vm, value_vm = call(
        functools.partial(key_value_body, plan), (key, value),
        [vm(part_state, BF)] * 2 + [vm(part_state, F32)] * 2
        + [vm((levels, 8, HEAD_DIM), F32), vm((rows, width), BF), vm((rows, width), BF)],
        unit * 2, (dma((2, plan.heads // plan.kept)),), raw_in=True,
    )

    def inner_work(far, operands):
        return call(
            functools.partial(inner_body, plan, far * plan.half), operands,
            [vm(half_state, BF), vm(half_state, F32)], 2 * unit,
        )

    near, far, given = scan_states(
        plan, states[:2], states[2:], bits, False,
        {
            "share": (functools.partial(inner_work, 0), (query, key_vm, value_vm)),
            "total": (functools.partial(inner_work, 1), (query, key_vm, value_vm)),
        },
    )
    inner = [given["share"], given["total"]]

    def norm(part, is_far, state):
        return call(
            functools.partial(norm_body, plan, plan.base(part, is_far)),
            (query, cot, inner[is_far][1], state),
            [vm(part_state, BF), vm(part_state, BF), vm(part_state, BF if is_far else F32)], unit,
        )

    normed = [[], []]
    for part in range(2):
        normed[0].append(norm(part, 0, near[part]))
        far[part], normed[0][part] = lax.optimization_barrier((far[part], normed[0][part]))
    for part in range(2):
        normed[1].append(norm(part, 1, far[part]))
    partials = ()

    def local_grads(is_far, operands):
        nonlocal partials
        out = call(
            functools.partial(local_grads_body, plan, is_far), operands,
            [vm(half_state, F32), vm(half_state, F32), whole, whole],
            5 * unit, (vm(half_state, BF), dma((2, plan.half))), partial=partials,
        )
        partials = out[2:]
        return out[:2]

    def operands(is_far, found):
        parts = [a for part in range(2) for a in (*normed[is_far][part][:2], found[part])]
        return (query, key_vm, value_vm, inner[is_far][0], *parts)

    near, far, given = scan_states(
        plan, [n[2] for n in normed[1]], [n[2] for n in normed[0]], bits, True,
        {
            "share": (functools.partial(local_grads, 0), operands(0, near)),
            "total": (functools.partial(local_grads, 1), operands(1, far)),
        },
    )
    grads = [given["share"], given["total"]]
    normed_out, grad_q = partials
    partials = ()
    for is_far in range(2):
        found = far if is_far else near
        buf = vm(half_state, BF)
        partials = call(
            functools.partial(last_grads_body, plan, is_far), (key_vm, value_vm, *grads[is_far], *found),
            [whole, whole], 2 * unit, (buf, buf, dma((2, plan.half))), partial=partials,
        )
        if not is_far:
            far, partials = lax.optimization_barrier((far, partials))
    grad_k, grad_v = partials
    return normed_out, grad_q, grad_k, grad_v


def solution(mesh):
    placed = P(("group", "seq", "head", "sub"), None)
    return jax.shard_map(
        on_device,
        mesh=mesh,
        in_specs=(placed,) * 4,
        out_specs=(placed,) * 4,
        check_vma=False,
    )
```

time: 60.2 us -> 55.3 us (0.919)
  waiting for transfers between devices: 18.8 us -> 16.1 us
  starting transfers between devices: 24.9 us -> 22.8 us
    ppermute x24 -> x22, waiting for transfers between devices: 18.8 us -> 16.1 us  [swap(): return lax.ppermute(value, axes, pairs)]
    ppermute x24 -> x22, starting transfers between devices: 24.9 us -> 22.8 us  [swap(): return lax.ppermute(value, axes, pairs)]
  transfers between devices with their start and end apart: 24 -> 22, of which waited for: 13 -> 13; matrix products, arithmetic and copies ran while one was open for 1% -> 0% of each run, Pallas kernels for 17% -> 19%
where the time goes in v3:
time: 55.3 us; the launch traced here: 55.1 us
  starting transfers between devices  22.8 us (41%)
  waiting for transfers between devices  16.1 us (29%)
  Pallas kernels  14.1 us (25%)
  between operations  0.89 us (2%)
  other arithmetic  0.86 us (2%)
    ppermute x22, starting transfers between devices, swap(): return lax.ppermute(value, axes, pairs)  22.8 us
    ppermute x22, waiting for transfers between devices, swap(): return lax.ppermute(value, axes, pairs)  16.1 us
    pallas_call x11, Pallas kernels, call(): pl.pallas_call(body, out_shape=outs, in_specs=in_specs, out_specs=[anywhe...  14.1 us
  transfers between devices with their start and end apart: 22, of which 13 were waited for; matrix products, arithmetic and copies ran while one was open for 0% of the time, Pallas kernels for 19%

profile of v3, /device:TPU:0, one launch (start us, length us, event | category | flops | bytes accessed | tf_op | source)
XLA Modules:
  0.0 55.1 jit_solution(18205739112381366045)
XLA Ops:
  0.6 2.7 %shard_map.75 = (bf16[4,128,128]{2,1,0:T(8,128)(2,1)S(1)}, bf16[4,128,128]{2,1,0:T(8,128)(2,1)S(1)}, f32[4,128,128]{2,1,0:T(8,128)S(1)}, f32[4,128,128]{2,1,0:T(...) custom-call(bf16[128,2048]{1,0:T(8,128)(2,1)} %k_ref.1, ...), custom_call_target="tpu_custom_call" | custom-call | flops 67108864 | bytes 2097152 | tf_op jit(solution)/shard_map/pallas_call | solution.py:172
  4.0 0.9 %collective-permute-done = bf16[4,128,128]{2,1,0:T(8,128)(2,1)S(1)} collective-permute-done((bf16[4,128,128]{2,1,0:T(8,128)(2,1)S(1)}, bf16[4,128,128]{2,1,0:T(8,128)(2,1)S(1)}, u32[]{:S(2)}, u32[]{:S(2)}) %collective-permute-start) | collective-permute-done | bytes 131104 | tf_op jit(solution)/shard_map/ppermute | solution.py:186
  4.9 3.0 %collective-permute-start.4 = (bf16[2,128,128]{2,1,0:T(8,128)(2,1)S(1)}, bf16[2,128,128]{2,1,0:T(8,128)(2,1)S(1)}, u32[]{:S(2)}, u32[]{:S(2)}) collective-permute-start(bf16[2,128,128]{2,1,0:T(8,128)(2,1)S(1)} %fusion.18), channel_id=1, source_target_pairs={{0,4},{2,6},{4,0},{6,2},{8,12},{10,14},{12,8},{14,10},{1,5},{3,7},... | collective-permute-start | bytes 196616 | tf_op jit(solution)/shard_map/ppermute | solution.py:186
  7.9 1.6 %collective-permute-start.2 = (bf16[2,128,128]{2,1,0:T(8,128)(2,1)S(1)}, bf16[2,128,128]{2,1,0:T(8,128)(2,1)S(1)}, u32[]{:S(2)}, u32[]{:S(2)}) collective-permute-start(bf16[2,128,128]{2,1,0:T(8,128)(2,1)S(1)} %get-tuple-element.194), channel_id=1, source_target_pairs={{0,2},{2,0},{4,6},{6,4},{8,10},{10,8},{12,14},{14,12},{1,3},{3,1},... | collective-permute-start | bytes 196616 | tf_op jit(solution)/shard_map/ppermute | solution.py:186
  9.6 1.4 %shard_map.76 = (bf16[8,128,128]{2,1,0:T(8,128)(2,1)S(1)}, f32[8,128,128]{2,1,0:T(8,128)S(1)}) custom-call(bf16[128,2048]{1,0:T(8,128)(2,1)S(1)} %copy-done, bf16[128,2048]{1,0:T(8,128)(2,1)S(1)} %get-tuple-element.153.k_ref, bf16[128,2048]{1,0:T(8,128)(2,1)S(1)} %get-tuple-element.154.v_ref), custom_call_target="tpu_custom_call" | custom-call | flops 67108864 | bytes 3145728 | tf_op jit(solution)/shard_map/pallas_call | solution.py:172
  10.9 1.3 %collective-permute-done.2 = bf16[2,128,128]{2,1,0:T(8,128)(2,1)S(1)} collective-permute-done((bf16[2,128,128]{2,1,0:T(8,128)(2,1)S(1)}, bf16[2,128,128]{2,1,0:T(8,128)(2,1)S(1)}, u32[]{:S(2)}, u32[]{:S(2)}) %collective-permute-start.2) | collective-permute-done | bytes 65568 | tf_op jit(solution)/shard_map/ppermute | solution.py:186
  12.3 2.4 %collective-permute-done.3 = bf16[2,128,128]{2,1,0:T(8,128)(2,1)S(1)} collective-permute-done((bf16[2,128,128]{2,1,0:T(8,128)(2,1)S(1)}, bf16[2,128,128]{2,1,0:T(8,128)(2,1)S(1)}, u32[]{:S(2)}, u32[]{:S(2)}) %collective-permute-start.3) | collective-permute-done | bytes 65568 | tf_op jit(solution)/shard_map/ppermute | solution.py:186
  14.7 2.7 %collective-permute-start.5 = (bf16[2,128,128]{2,1,0:T(8,128)(2,1)S(1)}, bf16[2,128,128]{2,1,0:T(8,128)(2,1)S(1)}, u32[]{:S(2)}, u32[]{:S(2)}) collective-permute-start(bf16[2,128,128]{2,1,0:T(8,128)(2,1)S(1)} %fusion.40), channel_id=1, source_target_pairs={{0,8},{2,10},{4,12},{6,14},{8,0},{10,2},{12,4},{14,6},{1,9},{3,11}... | collective-permute-start | bytes 196616 | tf_op jit(solution)/shard_map/ppermute | solution.py:186
  17.4 1.4 %shard_map.77 = (bf16[8,128,128]{2,1,0:T(8,128)(2,1)S(1)}, f32[8,128,128]{2,1,0:T(8,128)S(1)}) custom-call(bf16[128,2048]{1,0:T(8,128)(2,1)S(1)} %copy-done, bf16[128,2048]{1,0:T(8,128)(2,1)S(1)} %get-tuple-element.153.k_ref, bf16[128,2048]{1,0:T(8,128)(2,1)S(1)} %get-tuple-element.154.v_ref), custom_call_target="tpu_custom_call" | custom-call | flops 67108864 | bytes 3145728 | tf_op jit(solution)/shard_map/pallas_call | solution.py:172
  18.8 1.8 %collective-permute-done.5 = bf16[2,128,128]{2,1,0:T(8,128)(2,1)S(1)} collective-permute-done((bf16[2,128,128]{2,1,0:T(8,128)(2,1)S(1)}, bf16[2,128,128]{2,1,0:T(8,128)(2,1)S(1)}, u32[]{:S(2)}, u32[]{:S(2)}) %collective-permute-start.5) | collective-permute-done | bytes 65568 | tf_op jit(solution)/shard_map/ppermute | solution.py:186
  21.3 0.9 %collective-permute-start.10 = (bf16[2,128,128]{2,1,0:T(8,128)(2,1)S(1)}, bf16[2,128,128]{2,1,0:T(8,128)(2,1)S(1)}, u32[]{:S(2)}, u32[]{:S(2)}) collective-permute-start(bf16[2,128,128]{2,1,0:T(8,128)(2,1)S(1)} %get-tuple-element.187), channel_id=1, source_target_pairs={{0,6},{2,4},{4,2},{6,0},{8,14},{10,12},{12,10},{14,8},{1,7},{3,5},... | collective-permute-start | bytes 196616 | tf_op jit(solution)/shard_map/ppermute | solution.py:186
  22.1 2.1 %collective-permute-start.6 = (bf16[2,128,128]{2,1,0:T(8,128)(2,1)S(1)}, bf16[2,128,128]{2,1,0:T(8,128)(2,1)S(1)}, u32[]{:S(2)}, u32[]{:S(2)}) collective-permute-start(bf16[2,128,128]{2,1,0:T(8,128)(2,1)S(1)} %get-tuple-element.188), channel_id=1, source_target_pairs={{0,4},{2,6},{4,0},{6,2},{8,12},{10,14},{12,8},{14,10},{1,5},{3,7},... | collective-permute-start | bytes 196616 | tf_op jit(solution)/shard_map/ppermute | solution.py:186
  25.0 1.4 %collective-permute-done.10 = bf16[2,128,128]{2,1,0:T(8,128)(2,1)S(1)} collective-permute-done((bf16[2,128,128]{2,1,0:T(8,128)(2,1)S(1)}, bf16[2,128,128]{2,1,0:T(8,128)(2,1)S(1)}, u32[]{:S(2)}, u32[]{:S(2)}) %collective-permute-start.10) | collective-permute-done | bytes 65568 | tf_op jit(solution)/shard_map/ppermute | solution.py:186
  31.2 1.4 %collective-permute-start.15 = (bf16[2,128,128]{2,1,0:T(8,128)(2,1)S(1)}, bf16[2,128,128]{2,1,0:T(8,128)(2,1)S(1)}, u32[]{:S(2)}, u32[]{:S(2)}) collective-permute-start(bf16[2,128,128]{2,1,0:T(8,128)(2,1)S(1)} %fusion.29), channel_id=1, source_target_pairs={{0,4},{2,6},{4,0},{6,2},{8,12},{10,14},{12,8},{14,10},{1,5},{3,7},... | collective-permute-start | bytes 196616 | tf_op jit(solution)/shard_map/ppermute | solution.py:186
  33.2 1.9 %collective-permute-start.14 = (bf16[2,128,128]{2,1,0:T(8,128)(2,1)S(1)}, bf16[2,128,128]{2,1,0:T(8,128)(2,1)S(1)}, u32[]{:S(2)}, u32[]{:S(2)}) collective-permute-start(bf16[2,128,128]{2,1,0:T(8,128)(2,1)S(1)} %get-tuple-element.193), channel_id=1, source_target_pairs={{0,6},{2,4},{4,2},{6,0},{8,14},{10,12},{12,10},{14,8},{1,7},{3,5},... | collective-permute-start | bytes 196616 | tf_op jit(solution)/shard_map/ppermute | solution.py:186
  35.1 2.1 %shard_map.82 = (f32[8,128,128]{2,1,0:T(8,128)S(1)}, f32[8,128,128]{2,1,0:T(8,128)S(1)}, bf16[128,2048]{1,0:T(8,128)(2,1)}, bf16[128,2048]{1,0:T(8,128)(2,1)}) custom-call(bf16[128,2048]{1,0:T(8,128)(2,1)S(1)} %copy-done, bf16[128,2048]{1,0:T(8,128)(2,1)S(1)} %get-tuple-element.153.k_ref, bf16[128,2048]{1,0:T(8,128)(2,1)S(1)} %get-tuple-element.154.v_ref, ...), custom_call_target="tpu_custom_call" | custom-call | flops 167772160 | bytes 5242880 | tf_op jit(solution)/shard_map/pallas_call | solution.py:172
  38.4 2.1 %collective-permute-start.16 = (bf16[2,128,128]{2,1,0:T(8,128)(2,1)S(1)}, bf16[2,128,128]{2,1,0:T(8,128)(2,1)S(1)}, u32[]{:S(2)}, u32[]{:S(2)}) collective-permute-start(bf16[2,128,128]{2,1,0:T(8,128)(2,1)S(1)} %fusion.48), channel_id=1, source_target_pairs={{0,8},{2,10},{4,12},{6,14},{8,0},{10,2},{12,4},{14,6},{1,9},{3,11}... | collective-permute-start | bytes 196616 | tf_op jit(solution)/shard_map/ppermute | solution.py:186
  40.5 2.1 %shard_map.83 = (f32[8,128,128]{2,1,0:T(8,128)S(1)}, f32[8,128,128]{2,1,0:T(8,128)S(1)}, bf16[128,2048]{1,0:T(8,128)(2,1)}, bf16[128,2048]{1,0:T(8,128)(2,1)}) custom-call(bf16[128,2048]{1,0:T(8,128)(2,1)S(1)} %copy-done, bf16[128,2048]{1,0:T(8,128)(2,1)S(1)} %get-tuple-element.153.k_ref, ...), custom_call_target="tpu_custom_call", output_to_operand_aliasing={{2}: (10, {}), {3}: (11, {})} | custom-call | flops 167772160 | bytes 5242880 | tf_op jit(solution)/shard_map/pallas_call | solution.py:172
  42.7 1.7 %collective-permute-done.16 = bf16[2,128,128]{2,1,0:T(8,128)(2,1)S(1)} collective-permute-done((bf16[2,128,128]{2,1,0:T(8,128)(2,1)S(1)}, bf16[2,128,128]{2,1,0:T(8,128)(2,1)S(1)}, u32[]{:S(2)}, u32[]{:S(2)}) %collective-permute-start.16) | collective-permute-done | bytes 65568 | tf_op jit(solution)/shard_map/ppermute | solution.py:186
  45.0 2.7 %collective-permute-start.18 = (bf16[2,128,128]{2,1,0:T(8,128)(2,1)S(1)}, bf16[2,128,128]{2,1,0:T(8,128)(2,1)S(1)}, u32[]{:S(2)}, u32[]{:S(2)}) collective-permute-start(bf16[2,128,128]{2,1,0:T(8,128)(2,1)S(1)} %get-tuple-element.183), channel_id=1, source_target_pairs={{0,6},{2,4},{4,2},{6,0},{8,14},{10,12},{12,10},{14,8},{1,7},{3,5},... | collective-permute-start | bytes 196616 | tf_op jit(solution)/shard_map/ppermute | solution.py:186
  48.8 1.8 %collective-permute-done.18 = bf16[2,128,128]{2,1,0:T(8,128)(2,1)S(1)} collective-permute-done((bf16[2,128,128]{2,1,0:T(8,128)(2,1)S(1)}, bf16[2,128,128]{2,1,0:T(8,128)(2,1)S(1)}, u32[]{:S(2)}, u32[]{:S(2)}) %collective-permute-start.18) | collective-permute-done | bytes 65568 | tf_op jit(solution)/shard_map/ppermute | solution.py:186
  50.6 1.3 %collective-permute-done.17 = bf16[2,128,128]{2,1,0:T(8,128)(2,1)S(1)} collective-permute-done((bf16[2,128,128]{2,1,0:T(8,128)(2,1)S(1)}, bf16[2,128,128]{2,1,0:T(8,128)(2,1)S(1)}, u32[]{:S(2)}, u32[]{:S(2)}) %collective-permute-start.17) | collective-permute-done | bytes 65568 | tf_op jit(solution)/shard_map/ppermute | solution.py:186
  52.8 1.1 %shard_map.84 = (bf16[128,2048]{1,0:T(8,128)(2,1)}, bf16[128,2048]{1,0:T(8,128)(2,1)}) custom-call(bf16[128,2048]{1,0:T(8,128)(2,1)S(1)} %get-tuple-element.153.k_ref, bf16[128,2048]{1,0:T(8,128)(2,1)S(1)} %get-tuple-element.154.v_ref, f32[8,128,128]{2,1,0:T(8,128)S(1)} %get-tuple-element.172.gk_ref, f32[8,128,128]{2,1,0:T(8,128)S(1)} %get-tuple-element.173.gv_ref, ...), custom_call_target="tpu_custom_call" | custom-call | flops 67108864 | bytes 4718592 | tf_op jit(solution)/shard_map/pallas_call | solution.py:172
  53.9 1.1 %shard_map.85 = (bf16[128,2048]{1,0:T(8,128)(2,1)}, bf16[128,2048]{1,0:T(8,128)(2,1)}) custom-call(bf16[128,2048]{1,0:T(8,128)(2,1)S(1)} %get-tuple-element.153.k_ref, bf16[128,2048]{1,0:T(8,128)(2,1)S(1)} %get-tuple-element.154.v_ref, f32[8,128,128]{2,1,0:T(8,128)S(1)} %get-tuple-element.169.gk_ref, ...), custom_call_target="tpu_custom_call", output_to_operand_aliasing={{0}: (6, {}), {1}: (7, {})} | custom-call | flops 67108864 | bytes 4718592 | tf_op jit(solution)/shard_map/pallas_call | solution.py:172
  (53 shorter events, 11.4 us)
Async XLA Ops:
  3.4 6.2 %copy-start = (bf16[128,2048]{1,0:T(8,128)(2,1)S(1)}, bf16[128,2048]{1,0:T(8,128)(2,1)}, u32[]{:S(2)}) copy-start(bf16[128,2048]{1,0:T(8,128)(2,1)} %q_ref.11) | copy-start | bytes 1572868
  3.4 1.5 %collective-permute-start = (bf16[4,128,128]{2,1,0:T(8,128)(2,1)S(1)}, bf16[4,128,128]{2,1,0:T(8,128)(2,1)S(1)}, u32[]{:S(2)}, u32[]{:S(2)}) collective-permute-start(bf16[4,128,128]{2,1,0:T(8,128)(2,1)S(1)} %get-tuple-element.95), channel_id=1, source_target_pairs={{0,1},{1,0},{2,3},{3,2},{4,5},{5,4},{6,7},{7,6},{8,9},{9,8},{10,11... | collective-permute-start | bytes 393224 | tf_op jit(solution)/shard_map/ppermute | solution.py:186
  3.9 4.0 %collective-permute-start.1 = (bf16[4,128,128]{2,1,0:T(8,128)(2,1)S(1)}, bf16[4,128,128]{2,1,0:T(8,128)(2,1)S(1)}, u32[]{:S(2)}, u32[]{:S(2)}) collective-permute-start(bf16[4,128,128]{2,1,0:T(8,128)(2,1)S(1)} %get-tuple-element.97), channel_id=1, source_target_pairs={{0,1},{1,0},{2,3},{3,2},{4,5},{5,4},{6,7},{7,6},{8,9},{9,8},{10,11... | collective-permute-start | bytes 393224 | tf_op jit(solution)/shard_map/ppermute | solution.py:186
  4.9 6.0 %collective-permute-start.4 = (bf16[2,128,128]{2,1,0:T(8,128)(2,1)S(1)}, bf16[2,128,128]{2,1,0:T(8,128)(2,1)S(1)}, u32[]{:S(2)}, u32[]{:S(2)}) collective-permute-start(bf16[2,128,128]{2,1,0:T(8,128)(2,1)S(1)} %fusion.18), channel_id=1, source_target_pairs={{0,4},{2,6},{4,0},{6,2},{8,12},{10,14},{12,8},{14,10},{1,5},{3,7},... | collective-permute-start | bytes 196616 | tf_op jit(solution)/shard_map/ppermute | solution.py:186
  7.9 4.3 %collective-permute-start.2 = (bf16[2,128,128]{2,1,0:T(8,128)(2,1)S(1)}, bf16[2,128,128]{2,1,0:T(8,128)(2,1)S(1)}, u32[]{:S(2)}, u32[]{:S(2)}) collective-permute-start(bf16[2,128,128]{2,1,0:T(8,128)(2,1)S(1)} %get-tuple-element.194), channel_id=1, source_target_pairs={{0,2},{2,0},{4,6},{6,4},{8,10},{10,8},{12,14},{14,12},{1,3},{3,1},... | collective-permute-start | bytes 196616 | tf_op jit(solution)/shard_map/ppermute | solution.py:186
  9.5 5.2 %collective-permute-start.3 = (bf16[2,128,128]{2,1,0:T(8,128)(2,1)S(1)}, bf16[2,128,128]{2,1,0:T(8,128)(2,1)S(1)}, u32[]{:S(2)}, u32[]{:S(2)}) collective-permute-start(bf16[2,128,128]{2,1,0:T(8,128)(2,1)S(1)} %get-tuple-element.195), channel_id=1, source_target_pairs={{0,6},{2,4},{4,2},{6,0},{8,14},{10,12},{12,10},{14,8},{1,7},{3,5},... | collective-permute-start | bytes 196616 | tf_op jit(solution)/shard_map/ppermute | solution.py:186
  14.7 5.8 %collective-permute-start.5 = (bf16[2,128,128]{2,1,0:T(8,128)(2,1)S(1)}, bf16[2,128,128]{2,1,0:T(8,128)(2,1)S(1)}, u32[]{:S(2)}, u32[]{:S(2)}) collective-permute-start(bf16[2,128,128]{2,1,0:T(8,128)(2,1)S(1)} %fusion.40), channel_id=1, source_target_pairs={{0,8},{2,10},{4,12},{6,14},{8,0},{10,2},{12,4},{14,6},{1,9},{3,11}... | collective-permute-start | bytes 196616 | tf_op jit(solution)/shard_map/ppermute | solution.py:186
  20.7 4.3 %collective-permute-start.9 = (bf16[2,128,128]{2,1,0:T(8,128)(2,1)S(1)}, bf16[2,128,128]{2,1,0:T(8,128)(2,1)S(1)}, u32[]{:S(2)}, u32[]{:S(2)}) collective-permute-start(bf16[2,128,128]{2,1,0:T(8,128)(2,1)S(1)} %get-tuple-element.186), channel_id=1, source_target_pairs={{0,2},{2,0},{4,6},{6,4},{8,10},{10,8},{12,14},{14,12},{1,3},{3,1},... | collective-permute-start | bytes 196616 | tf_op jit(solution)/shard_map/ppermute | solution.py:186
  21.3 5.2 %collective-permute-start.10 = (bf16[2,128,128]{2,1,0:T(8,128)(2,1)S(1)}, bf16[2,128,128]{2,1,0:T(8,128)(2,1)S(1)}, u32[]{:S(2)}, u32[]{:S(2)}) collective-permute-start(bf16[2,128,128]{2,1,0:T(8,128)(2,1)S(1)} %get-tuple-element.187), channel_id=1, source_target_pairs={{0,6},{2,4},{4,2},{6,0},{8,14},{10,12},{12,10},{14,8},{1,7},{3,5},... | collective-permute-start | bytes 196616 | tf_op jit(solution)/shard_map/ppermute | solution.py:186
  22.1 5.0 %collective-permute-start.6 = (bf16[2,128,128]{2,1,0:T(8,128)(2,1)S(1)}, bf16[2,128,128]{2,1,0:T(8,128)(2,1)S(1)}, u32[]{:S(2)}, u32[]{:S(2)}) collective-permute-start(bf16[2,128,128]{2,1,0:T(8,128)(2,1)S(1)} %get-tuple-element.188), channel_id=1, source_target_pairs={{0,4},{2,6},{4,0},{6,2},{8,12},{10,14},{12,8},{14,10},{1,5},{3,7},... | collective-permute-start | bytes 196616 | tf_op jit(solution)/shard_map/ppermute | solution.py:186
  27.3 1.0 %copy-start.1 = (bf16[128,2048]{1,0:T(8,128)(2,1)S(1)}, bf16[128,2048]{1,0:T(8,128)(2,1)}, u32[]{:S(2)}) copy-start(bf16[128,2048]{1,0:T(8,128)(2,1)} %g_ref.7) | copy-start | bytes 1572868
  27.4 1.5 %collective-permute-start.7 = (bf16[4,128,128]{2,1,0:T(8,128)(2,1)S(1)}, bf16[4,128,128]{2,1,0:T(8,128)(2,1)S(1)}, u32[]{:S(2)}, u32[]{:S(2)}) collective-permute-start(bf16[4,128,128]{2,1,0:T(8,128)(2,1)S(1)} %pad_maximum_fusion), channel_id=1, source_target_pairs={{0,1},{1,0},{2,3},{3,2},{4,5},{5,4},{6,7},{7,6},{8,9},{9,8},{10,11... | collective-permute-start | bytes 393224 | tf_op jit(solution)/shard_map/ppermute | solution.py:186
  27.5 2.6 %collective-permute-start.11 = (bf16[4,128,128]{2,1,0:T(8,128)(2,1)S(1)}, bf16[4,128,128]{2,1,0:T(8,128)(2,1)S(1)}, u32[]{:S(2)}, u32[]{:S(2)}) collective-permute-start(bf16[4,128,128]{2,1,0:T(8,128)(2,1)S(1)} %pad_maximum_fusion.2), channel_id=1, source_target_pairs={{0,1},{1,0},{2,3},{3,2},{4,5},{5,4},{6,7},{7,6},{8,9},{9,8},{10,11... | collective-permute-start | bytes 393224 | tf_op jit(solution)/shard_map/ppermute | solution.py:186
  29.4 1.7 %collective-permute-start.8 = (bf16[4,128,128]{2,1,0:T(8,128)(2,1)S(1)}, bf16[4,128,128]{2,1,0:T(8,128)(2,1)S(1)}, u32[]{:S(2)}, u32[]{:S(2)}) collective-permute-start(bf16[4,128,128]{2,1,0:T(8,128)(2,1)S(1)} %get-tuple-element.121), channel_id=1, source_target_pairs={{0,1},{1,0},{2,3},{3,2},{4,5},{5,4},{6,7},{7,6},{8,9},{9,8},{10,11... | collective-permute-start | bytes 393224 | tf_op jit(solution)/shard_map/ppermute | solution.py:186
  30.6 2.0 %collective-permute-start.12 = (bf16[4,128,128]{2,1,0:T(8,128)(2,1)S(1)}, bf16[4,128,128]{2,1,0:T(8,128)(2,1)S(1)}, u32[]{:S(2)}, u32[]{:S(2)}) collective-permute-start(bf16[4,128,128]{2,1,0:T(8,128)(2,1)S(1)} %get-tuple-element.127), channel_id=1, source_target_pairs={{0,1},{1,0},{2,3},{3,2},{4,5},{5,4},{6,7},{7,6},{8,9},{9,8},{10,11... | collective-permute-start | bytes 393224 | tf_op jit(solution)/shard_map/ppermute | solution.py:186
  31.2 6.0 %collective-permute-start.15 = (bf16[2,128,128]{2,1,0:T(8,128)(2,1)S(1)}, bf16[2,128,128]{2,1,0:T(8,128)(2,1)S(1)}, u32[]{:S(2)}, u32[]{:S(2)}) collective-permute-start(bf16[2,128,128]{2,1,0:T(8,128)(2,1)S(1)} %fusion.29), channel_id=1, source_target_pairs={{0,4},{2,6},{4,0},{6,2},{8,12},{10,14},{12,8},{14,10},{1,5},{3,7},... | collective-permute-start | bytes 196616 | tf_op jit(solution)/shard_map/ppermute | solution.py:186
  32.6 5.0 %collective-permute-start.13 = (bf16[2,128,128]{2,1,0:T(8,128)(2,1)S(1)}, bf16[2,128,128]{2,1,0:T(8,128)(2,1)S(1)}, u32[]{:S(2)}, u32[]{:S(2)}) collective-permute-start(bf16[2,128,128]{2,1,0:T(8,128)(2,1)S(1)} %get-tuple-element.192), channel_id=1, source_target_pairs={{0,2},{2,0},{4,6},{6,4},{8,10},{10,8},{12,14},{14,12},{1,3},{3,1},... | collective-permute-start | bytes 196616 | tf_op jit(solution)/shard_map/ppermute | solution.py:186
  33.2 5.2 %collective-permute-start.14 = (bf16[2,128,128]{2,1,0:T(8,128)(2,1)S(1)}, bf16[2,128,128]{2,1,0:T(8,128)(2,1)S(1)}, u32[]{:S(2)}, u32[]{:S(2)}) collective-permute-start(bf16[2,128,128]{2,1,0:T(8,128)(2,1)S(1)} %get-tuple-element.193), channel_id=1, source_target_pairs={{0,6},{2,4},{4,2},{6,0},{8,14},{10,12},{12,10},{14,8},{1,7},{3,5},... | collective-permute-start | bytes 196616 | tf_op jit(solution)/shard_map/ppermute | solution.py:186
  38.4 5.9 %collective-permute-start.16 = (bf16[2,128,128]{2,1,0:T(8,128)(2,1)S(1)}, bf16[2,128,128]{2,1,0:T(8,128)(2,1)S(1)}, u32[]{:S(2)}, u32[]{:S(2)}) collective-permute-start(bf16[2,128,128]{2,1,0:T(8,128)(2,1)S(1)} %fusion.48), channel_id=1, source_target_pairs={{0,8},{2,10},{4,12},{6,14},{8,0},{10,2},{12,4},{14,6},{1,9},{3,11}... | collective-permute-start | bytes 196616 | tf_op jit(solution)/shard_map/ppermute | solution.py:186
  44.5 4.3 %collective-permute-start.20 = (bf16[2,128,128]{2,1,0:T(8,128)(2,1)S(1)}, bf16[2,128,128]{2,1,0:T(8,128)(2,1)S(1)}, u32[]{:S(2)}, u32[]{:S(2)}) collective-permute-start(bf16[2,128,128]{2,1,0:T(8,128)(2,1)S(1)} %get-tuple-element.182), channel_id=1, source_target_pairs={{0,4},{2,6},{4,0},{6,2},{8,12},{10,14},{12,8},{14,10},{1,5},{3,7},... | collective-permute-start | bytes 196616 | tf_op jit(solution)/shard_map/ppermute | solution.py:186
  45.0 5.6 %collective-permute-start.18 = (bf16[2,128,128]{2,1,0:T(8,128)(2,1)S(1)}, bf16[2,128,128]{2,1,0:T(8,128)(2,1)S(1)}, u32[]{:S(2)}, u32[]{:S(2)}) collective-permute-start(bf16[2,128,128]{2,1,0:T(8,128)(2,1)S(1)} %get-tuple-element.183), channel_id=1, source_target_pairs={{0,6},{2,4},{4,2},{6,0},{8,14},{10,12},{12,10},{14,8},{1,7},{3,5},... | collective-permute-start | bytes 196616 | tf_op jit(solution)/shard_map/ppermute | solution.py:186
  47.7 4.3 %collective-permute-start.17 = (bf16[2,128,128]{2,1,0:T(8,128)(2,1)S(1)}, bf16[2,128,128]{2,1,0:T(8,128)(2,1)S(1)}, u32[]{:S(2)}, u32[]{:S(2)}) collective-permute-start(bf16[2,128,128]{2,1,0:T(8,128)(2,1)S(1)} %get-tuple-element.184), channel_id=1, source_target_pairs={{0,2},{2,0},{4,6},{6,4},{8,10},{10,8},{12,14},{14,12},{1,3},{3,1},... | collective-permute-start | bytes 196616 | tf_op jit(solution)/shard_map/ppermute | solution.py:186
  52.1 1.8 %collective-permute-start.19 = (bf16[4,128,128]{2,1,0:T(8,128)(2,1)S(1)}, bf16[4,128,128]{2,1,0:T(8,128)(2,1)S(1)}, u32[]{:S(2)}, u32[]{:S(2)}) collective-permute-start(bf16[4,128,128]{2,1,0:T(8,128)(2,1)S(1)} %pad_maximum_fusion.4), channel_id=1, source_target_pairs={{0,1},{1,0},{2,3},{3,2},{4,5},{5,4},{6,7},{7,6},{8,9},{9,8},{10,11... | collective-permute-start | bytes 393224 | tf_op jit(solution)/shard_map/ppermute | solution.py:186
  52.2 1.7 %collective-permute-start.21 = (bf16[4,128,128]{2,1,0:T(8,128)(2,1)S(1)}, bf16[4,128,128]{2,1,0:T(8,128)(2,1)S(1)}, u32[]{:S(2)}, u32[]{:S(2)}) collective-permute-start(bf16[4,128,128]{2,1,0:T(8,128)(2,1)S(1)} %pad_maximum_fusion.5), channel_id=1, source_target_pairs={{0,1},{1,0},{2,3},{3,2},{4,5},{5,4},{6,7},{7,6},{8,9},{9,8},{10,11... | collective-permute-start | bytes 393224 | tf_op jit(solution)/shard_map/ppermute | solution.py:186

commit v4 on v3

--- a/solution.py
+++ b/solution.py
@@ -55,34 +55,38 @@
         return sum(((group >> (self.steps - 1 - j)) & 1) << j for j in range(self.steps))
 
     def base(self, part, far):
-        return far * self.half + (1 - part) * self.part
+        return far * self.half + part * self.part
+
+    def side(self, far):
+        half = lax.bitwise_xor(jnp.int32(far), place_bit(0)) * (self.half * HEAD_DIM)
+        return pl.ds(pl.multiple_of(half, HEAD_DIM), self.half * HEAD_DIM)
 
 
 def key_value_body(plan, k_ref, v_ref, *rest):
     *parts, bits_ref, k_out, v_out, sems = rest
-    order = [(part, far) for far in (1, 0) for part in (0, 1)]
     copies = {}
-    for part, far in order:
-        for first in range(plan.base(part, far), plan.base(part, far) + plan.part, plan.kept):
-            at, number = plan.columns(first, plan.kept), first // plan.kept
-            copies[first] = [
-                pltpu.make_async_copy(k_ref.at[:, at], k_out.at[:, at], sems.at[0, number]),
-                pltpu.make_async_copy(v_ref.at[:, at], v_out.at[:, at], sems.at[1, number]),
-            ]
-            for copy in copies[first]:
-                copy.start()
+    for far in (1, 0):
+        at = plan.side(far)
+        copies[far] = [
+            pltpu.make_async_copy(k_ref.at[:, at], k_out.at[:, at], sems.at[0, far]),
+            pltpu.make_async_copy(v_ref.at[:, at], v_out.at[:, at], sems.at[1, far]),
+        ]
+        for copy in copies[far]:
+            copy.start()
     for level in range(bits_ref.shape[0]):
         bits_ref[level] = jnp.full(bits_ref.shape[1:], place_bit(level).astype(F32), F32)
-    for (part, far), out_ref in zip(order, parts):
-        for number in range(plan.part):
-            slot = plan.base(part, far) + number
-            for copy in copies.get(slot, ()):
-                copy.wait()
-            at = plan.columns(slot)
-            out_ref[number] = dot(k_out[:, at], v_out[:, at], TN).astype(out_ref.dtype)
-
-
-def inner_body(plan, base, q_ref, k_ref, v_ref, probs_ref, inner_ref):
+    for far in (1, 0):
+        for copy in copies[far]:
+            copy.wait()
+        for part in (0, 1):
+            out_ref = parts[2 * (1 - far) + part]
+            for number in range(plan.part):
+                at = plan.columns(plan.base(part, far) + number)
+                out_ref[number] = dot(k_out[:, at], v_out[:, at], TN).astype(out_ref.dtype)
+
+
+def inner_body(plan, base, q_ref, k_ref, v_ref, *rest):
+    *_, probs_ref, inner_ref = rest
     mask = causal_mask()
     for number in range(plan.half):
         at = plan.columns(base + number)
@@ -107,11 +111,11 @@
 
 
 def local_grads_body(plan, far, q_ref, k_ref, v_ref, probs_ref, *rest):
-    upper, lower, rest = rest[:3], rest[3:6], rest[6:]
+    first, second, rest = rest[:3], rest[3:6], rest[6:]
     *_, gk_ref, gv_ref, normed_out, gq_out, gq_buf, sems = rest
     mask = causal_mask()
     copies, held = [], {}
-    for part, refs in enumerate((upper, lower)):
+    for part, refs in enumerate((first, second)):
         for number in range(plan.part):
             slot = plan.base(part, far) + number
             held[slot] = [ref.at[number] for ref in refs]
@@ -132,11 +136,11 @@
         copy.wait()
 
 
-def last_grads_body(plan, far, k_ref, v_ref, gk_ref, gv_ref, *rest):
-    states = rest[:2]
+def last_grads_body(plan, pieces, k_ref, v_ref, gk_ref, gv_ref, *rest):
+    states = rest[: len(pieces)]
     *_, gk_out, gv_out, gk_buf, gv_buf, sems = rest
     copies = []
-    for part, state_ref in enumerate(states):
+    for (part, far), state_ref in zip(pieces, states):
         for inside in range(plan.part):
             slot = plan.base(part, far) + inside
             at, number = plan.columns(slot), slot % plan.half
@@ -215,7 +219,7 @@
         return got
 
     share = plan.groups // 2
-    members = [range(share, plan.groups), range(share)]
+    members = [range(share), range(share, plan.groups)]
     own, near_got, pair = {}, {}, {}
     for part, (send, keep) in enumerate(zip(sends, keeps)):
         got = swap(send, "sub", 1)
@@ -242,12 +246,17 @@
     for group in order:
         message = carried + before(pair[0], others, plan.mask(group), bits, reverse)
         sums[group] = swap(message.astype(BF), chips, plan.mask(group)).astype(F32)
-    near, far = [], []
+    near, far, message = [], [], None
     for part in members:
+        if message is not None:
+            for group in part:
+                sums[group], message = lax.optimization_barrier((sums[group], message))
+            far.append(swap(message, "sub", 1))
         message = [sums[group] + gated(own[group], bits, 0, lower) for group in part]
         known = [sums[group] + gated(near_got[group], bits, 0, upper) for group in part]
-        far.append(swap(jnp.concatenate(message).astype(BF), "sub", 1))
+        message = jnp.concatenate(message).astype(BF)
         near.append(jnp.concatenate(known).astype(BF))
+    far.append(swap(message, "sub", 1))
     return near, far, given
 
 
@@ -265,7 +274,7 @@
         functools.partial(key_value_body, plan), (key, value),
         [vm(part_state, BF)] * 2 + [vm(part_state, F32)] * 2
         + [vm((levels, 8, HEAD_DIM), F32), vm((rows, width), BF), vm((rows, width), BF)],
-        unit * 2, (dma((2, plan.heads // plan.kept)),), raw_in=True,
+        unit * 2, (dma((2, 2)),), raw_in=True,
     )
 
     def inner_work(far, operands):
@@ -277,7 +286,7 @@
     near, far, given = scan_states(
         plan, states[:2], states[2:], bits, False,
         {
-            "share": (functools.partial(inner_work, 0), (query, key_vm, value_vm)),
+            "share": (functools.partial(inner_work, 0), (query, key_vm, value_vm, cot)),
             "total": (functools.partial(inner_work, 1), (query, key_vm, value_vm)),
         },
     )
@@ -322,12 +331,13 @@
     grads = [given["share"], given["total"]]
     normed_out, grad_q = partials
     partials = ()
-    for is_far in range(2):
-        found = far if is_far else near
-        buf = vm(half_state, BF)
+    buf = vm(half_state, BF)
+    for pieces in (((0, 0), (1, 0)), ((0, 1), (1, 1))):
+        is_far = pieces[0][1]
+        found = [(far if is_far else near)[part] for part, _ in pieces]
         partials = call(
-            functools.partial(last_grads_body, plan, is_far), (key_vm, value_vm, *grads[is_far], *found),
-            [whole, whole], 2 * unit, (buf, buf, dma((2, plan.half))), partial=partials,
+            functools.partial(last_grads_body, plan, pieces), (key_vm, value_vm, *grads[is_far], *found),
+            [whole, whole], unit * len(pieces), (buf, buf, dma((2, plan.half))), partial=partials,
         )
         if not is_far:
             far, partials = lax.optimization_barrier((far, partials))

time: 55.3 us -> 52.8 us (0.955)
  waiting for transfers between devices: 16.1 us -> 14.1 us
  Pallas kernels: 14.1 us -> 13.1 us
  starting transfers between devices: 22.8 us -> 23.6 us
    ppermute x22, waiting for transfers between devices: 16.1 us -> 14.1 us  [swap(): return lax.ppermute(value, axes, pairs)]
    pallas_call x11, Pallas kernels: 14.1 us -> 13.1 us  [call(): pl.pallas_call(body, out_shape=outs, in_specs=in_specs, out_specs=[anywhe...]
    ppermute x22, starting transfers between devices: 22.8 us -> 23.6 us  [swap(): return lax.ppermute(value, axes, pairs)]
  transfers between devices with their start and end apart: 22 -> 22, of which waited for: 13 -> 12; matrix products, arithmetic and copies ran while one was open for 0% -> 1% of each run, Pallas kernels for 19% -> 19%
where the time goes in v4:
time: 52.8 us; the launch traced here: 52.6 us
  starting transfers between devices  23.6 us (45%)
  waiting for transfers between devices  14.1 us (27%)
  Pallas kernels  13.1 us (25%)
  between operations  0.91 us (2%)
  other arithmetic  0.88 us (2%)
    ppermute x22, starting transfers between devices, swap(): return lax.ppermute(value, axes, pairs)  23.6 us
    ppermute x22, waiting for transfers between devices, swap(): return lax.ppermute(value, axes, pairs)  14.1 us
    pallas_call x11, Pallas kernels, call(): pl.pallas_call(body, out_shape=outs, in_specs=in_specs, out_specs=[anywhe...  13.1 us
  transfers between devices with their start and end apart: 22, of which 12 were waited for; matrix products, arithmetic and copies ran while one was open for 1% of the time, Pallas kernels for 19%

profile of v4, /device:TPU:0, one launch (start us, length us, event | category | flops | bytes accessed | tf_op | source)
XLA Modules:
  0.0 52.6 jit_solution(6099884629117780585)
XLA Ops:
  0.6 1.7 %shard_map.75 = (bf16[4,128,128]{2,1,0:T(8,128)(2,1)S(1)}, bf16[4,128,128]{2,1,0:T(8,128)(2,1)S(1)}, f32[4,128,128]{2,1,0:T(8,128)S(1)}, f32[4,128,128]{2,1,0:T(...) custom-call(bf16[128,2048]{1,0:T(8,128)(2,1)} %k_ref.1, ...), custom_call_target="tpu_custom_call" | custom-call | flops 67108864 | bytes 2097152 | tf_op jit(solution)/shard_map/pallas_call | solution.py:176
  3.0 0.9 %collective-permute-done.2 = bf16[4,128,128]{2,1,0:T(8,128)(2,1)S(1)} collective-permute-done((bf16[4,128,128]{2,1,0:T(8,128)(2,1)S(1)}, bf16[4,128,128]{2,1,0:T(8,128)(2,1)S(1)}, u32[]{:S(2)}, u32[]{:S(2)}) %collective-permute-start.2) | collective-permute-done | bytes 131104 | tf_op jit(solution)/shard_map/ppermute | solution.py:190
  3.9 3.9 %collective-permute-start.4 = (bf16[2,128,128]{2,1,0:T(8,128)(2,1)S(1)}, bf16[2,128,128]{2,1,0:T(8,128)(2,1)S(1)}, u32[]{:S(2)}, u32[]{:S(2)}) collective-permute-start(bf16[2,128,128]{2,1,0:T(8,128)(2,1)S(1)} %get-tuple-element.109), channel_id=1, source_target_pairs={{0,6},{2,4},{4,2},{6,0},{8,14},{10,12},{12,10},{14,8},{1,7},{3,5},... | collective-permute-start | bytes 196616 | tf_op jit(solution)/shard_map/ppermute | solution.py:190
  8.6 1.4 %shard_map.76 = (bf16[8,128,128]{2,1,0:T(8,128)(2,1)S(1)}, f32[8,128,128]{2,1,0:T(8,128)S(1)}) custom-call(bf16[128,2048]{1,0:T(8,128)(2,1)S(1)} %copy-done, bf16[128,2048]{1,0:T(8,128)(2,1)S(1)} %get-tuple-element.167.k_ref, bf16[128,2048]{1,0:T(8,128)(2,1)S(1)} %get-tuple-element.168.v_ref, bf16[128,2048]{1,0:T(8,128)(2,1)S(1)} %copy-done.1), custom_call_target="tpu_custom_call" | custom-call | flops 67108864 | bytes 4194304 | tf_op jit(solution)/shard_map/pallas_call | solution.py:176
  10.3 1.9 %collective-permute-done.1 = bf16[2,128,128]{2,1,0:T(8,128)(2,1)S(1)} collective-permute-done((bf16[2,128,128]{2,1,0:T(8,128)(2,1)S(1)}, bf16[2,128,128]{2,1,0:T(8,128)(2,1)S(1)}, u32[]{:S(2)}, u32[]{:S(2)}) %collective-permute-start.1) | collective-permute-done | bytes 65568 | tf_op jit(solution)/shard_map/ppermute | solution.py:190
  12.7 2.7 %collective-permute-start.5 = (bf16[2,128,128]{2,1,0:T(8,128)(2,1)S(1)}, bf16[2,128,128]{2,1,0:T(8,128)(2,1)S(1)}, u32[]{:S(2)}, u32[]{:S(2)}) collective-permute-start(bf16[2,128,128]{2,1,0:T(8,128)(2,1)S(1)} %fusion.51), channel_id=1, source_target_pairs={{0,8},{2,10},{4,12},{6,14},{8,0},{10,2},{12,4},{14,6},{1,9},{3,11}... | collective-permute-start | bytes 196616 | tf_op jit(solution)/shard_map/ppermute | solution.py:190
  15.4 1.4 %shard_map.77 = (bf16[8,128,128]{2,1,0:T(8,128)(2,1)S(1)}, f32[8,128,128]{2,1,0:T(8,128)S(1)}) custom-call(bf16[128,2048]{1,0:T(8,128)(2,1)S(1)} %copy-done, bf16[128,2048]{1,0:T(8,128)(2,1)S(1)} %get-tuple-element.167.k_ref, bf16[128,2048]{1,0:T(8,128)(2,1)S(1)} %get-tuple-element.168.v_ref), custom_call_target="tpu_custom_call" | custom-call | flops 67108864 | bytes 3145728 | tf_op jit(solution)/shard_map/pallas_call | solution.py:176
  16.7 1.2 %collective-permute-done.5 = bf16[2,128,128]{2,1,0:T(8,128)(2,1)S(1)} collective-permute-done((bf16[2,128,128]{2,1,0:T(8,128)(2,1)S(1)}, bf16[2,128,128]{2,1,0:T(8,128)(2,1)S(1)}, u32[]{:S(2)}, u32[]{:S(2)}) %collective-permute-start.5) | collective-permute-done | bytes 65568 | tf_op jit(solution)/shard_map/ppermute | solution.py:190
  18.1 1.6 %collective-permute-start.8 = (bf16[2,128,128]{2,1,0:T(8,128)(2,1)S(1)}, bf16[2,128,128]{2,1,0:T(8,128)(2,1)S(1)}, u32[]{:S(2)}, u32[]{:S(2)}) collective-permute-start(bf16[2,128,128]{2,1,0:T(8,128)(2,1)S(1)} %get-tuple-element.204), channel_id=1, source_target_pairs={{0,4},{2,6},{4,0},{6,2},{8,12},{10,14},{12,8},{14,10},{1,5},{3,7},... | collective-permute-start | bytes 196616 | tf_op jit(solution)/shard_map/ppermute | solution.py:190
  19.7 0.9 %collective-permute-start.6 = (bf16[2,128,128]{2,1,0:T(8,128)(2,1)S(1)}, bf16[2,128,128]{2,1,0:T(8,128)(2,1)S(1)}, u32[]{:S(2)}, u32[]{:S(2)}) collective-permute-start(bf16[2,128,128]{2,1,0:T(8,128)(2,1)S(1)} %get-tuple-element.205), channel_id=1, source_target_pairs={{0,6},{2,4},{4,2},{6,0},{8,14},{10,12},{12,10},{14,8},{1,7},{3,5},... | collective-permute-start | bytes 196616 | tf_op jit(solution)/shard_map/ppermute | solution.py:190
  20.6 1.0 %collective-permute-start.7 = (bf16[2,128,128]{2,1,0:T(8,128)(2,1)S(1)}, bf16[2,128,128]{2,1,0:T(8,128)(2,1)S(1)}, u32[]{:S(2)}, u32[]{:S(2)}) collective-permute-start(bf16[2,128,128]{2,1,0:T(8,128)(2,1)S(1)} %get-tuple-element.206), channel_id=1, source_target_pairs={{0,2},{2,0},{4,6},{6,4},{8,10},{10,8},{12,14},{14,12},{1,3},{3,1},... | collective-permute-start | bytes 196616 | tf_op jit(solution)/shard_map/ppermute | solution.py:190
  21.7 0.8 %collective-permute-done.8 = bf16[2,128,128]{2,1,0:T(8,128)(2,1)S(1)} collective-permute-done((bf16[2,128,128]{2,1,0:T(8,128)(2,1)S(1)}, bf16[2,128,128]{2,1,0:T(8,128)(2,1)S(1)}, u32[]{:S(2)}, u32[]{:S(2)}) %collective-permute-start.8) | collective-permute-done | bytes 65568 | tf_op jit(solution)/shard_map/ppermute | solution.py:190
  22.5 3.1 %collective-permute-done.7 = bf16[2,128,128]{2,1,0:T(8,128)(2,1)S(1)} collective-permute-done((bf16[2,128,128]{2,1,0:T(8,128)(2,1)S(1)}, bf16[2,128,128]{2,1,0:T(8,128)(2,1)S(1)}, u32[]{:S(2)}, u32[]{:S(2)}) %collective-permute-start.7) | collective-permute-done | bytes 65568 | tf_op jit(solution)/shard_map/ppermute | solution.py:190
  29.5 1.4 %collective-permute-start.15 = (bf16[2,128,128]{2,1,0:T(8,128)(2,1)S(1)}, bf16[2,128,128]{2,1,0:T(8,128)(2,1)S(1)}, u32[]{:S(2)}, u32[]{:S(2)}) collective-permute-start(bf16[2,128,128]{2,1,0:T(8,128)(2,1)S(1)} %get-tuple-element.147), channel_id=1, source_target_pairs={{0,6},{2,4},{4,2},{6,0},{8,14},{10,12},{12,10},{14,8},{1,7},{3,5},... | collective-permute-start | bytes 196616 | tf_op jit(solution)/shard_map/ppermute | solution.py:190
  31.6 1.5 %collective-permute-start.11 = (bf16[2,128,128]{2,1,0:T(8,128)(2,1)S(1)}, bf16[2,128,128]{2,1,0:T(8,128)(2,1)S(1)}, u32[]{:S(2)}, u32[]{:S(2)}) collective-permute-start(bf16[2,128,128]{2,1,0:T(8,128)(2,1)S(1)} %fusion.41), channel_id=1, source_target_pairs={{0,4},{2,6},{4,0},{6,2},{8,12},{10,14},{12,8},{14,10},{1,5},{3,7},... | collective-permute-start | bytes 196616 | tf_op jit(solution)/shard_map/ppermute | solution.py:190
  33.1 2.1 %shard_map.82 = (f32[8,128,128]{2,1,0:T(8,128)S(1)}, f32[8,128,128]{2,1,0:T(8,128)S(1)}, bf16[128,2048]{1,0:T(8,128)(2,1)}, bf16[128,2048]{1,0:T(8,128)(2,1)}) custom-call(bf16[128,2048]{1,0:T(8,128)(2,1)S(1)} %copy-done, bf16[128,2048]{1,0:T(8,128)(2,1)S(1)} %get-tuple-element.167.k_ref, bf16[128,2048]{1,0:T(8,128)(2,1)S(1)} %get-tuple-element.168.v_ref, ...), custom_call_target="tpu_custom_call" | custom-call | flops 167772160 | bytes 5242880 | tf_op jit(solution)/shard_map/pallas_call | solution.py:176
  36.0 3.2 %collective-permute-start.16 = (bf16[2,128,128]{2,1,0:T(8,128)(2,1)S(1)}, bf16[2,128,128]{2,1,0:T(8,128)(2,1)S(1)}, u32[]{:S(2)}, u32[]{:S(2)}) collective-permute-start(bf16[2,128,128]{2,1,0:T(8,128)(2,1)S(1)} %fusion.53), channel_id=1, source_target_pairs={{0,8},{2,10},{4,12},{6,14},{8,0},{10,2},{12,4},{14,6},{1,9},{3,11}... | collective-permute-start | bytes 196616 | tf_op jit(solution)/shard_map/ppermute | solution.py:190
  39.2 2.1 %shard_map.83 = (f32[8,128,128]{2,1,0:T(8,128)S(1)}, f32[8,128,128]{2,1,0:T(8,128)S(1)}, bf16[128,2048]{1,0:T(8,128)(2,1)}, bf16[128,2048]{1,0:T(8,128)(2,1)}) custom-call(bf16[128,2048]{1,0:T(8,128)(2,1)S(1)} %copy-done, bf16[128,2048]{1,0:T(8,128)(2,1)S(1)} %get-tuple-element.167.k_ref, ...), custom_call_target="tpu_custom_call", output_to_operand_aliasing={{2}: (10, {}), {3}: (11, {})} | custom-call | flops 167772160 | bytes 5242880 | tf_op jit(solution)/shard_map/pallas_call | solution.py:176
  41.4 1.0 %collective-permute-done.16 = bf16[2,128,128]{2,1,0:T(8,128)(2,1)S(1)} collective-permute-done((bf16[2,128,128]{2,1,0:T(8,128)(2,1)S(1)}, bf16[2,128,128]{2,1,0:T(8,128)(2,1)S(1)}, u32[]{:S(2)}, u32[]{:S(2)}) %collective-permute-start.16) | collective-permute-done | bytes 65568 | tf_op jit(solution)/shard_map/ppermute | solution.py:190
  43.0 2.3 %collective-permute-start.17 = (bf16[2,128,128]{2,1,0:T(8,128)(2,1)S(1)}, bf16[2,128,128]{2,1,0:T(8,128)(2,1)S(1)}, u32[]{:S(2)}, u32[]{:S(2)}) collective-permute-start(bf16[2,128,128]{2,1,0:T(8,128)(2,1)S(1)} %get-tuple-element.201), channel_id=1, source_target_pairs={{0,6},{2,4},{4,2},{6,0},{8,14},{10,12},{12,10},{14,8},{1,7},{3,5},... | collective-permute-start | bytes 196616 | tf_op jit(solution)/shard_map/ppermute | solution.py:190
  45.3 0.8 %collective-permute-start.18 = (bf16[2,128,128]{2,1,0:T(8,128)(2,1)S(1)}, bf16[2,128,128]{2,1,0:T(8,128)(2,1)S(1)}, u32[]{:S(2)}, u32[]{:S(2)}) collective-permute-start(bf16[2,128,128]{2,1,0:T(8,128)(2,1)S(1)} %get-tuple-element.202), channel_id=1, source_target_pairs={{0,2},{2,0},{4,6},{6,4},{8,10},{10,8},{12,14},{14,12},{1,3},{3,1},... | collective-permute-start | bytes 196616 | tf_op jit(solution)/shard_map/ppermute | solution.py:190
  46.9 2.6 %collective-permute-done.18 = bf16[2,128,128]{2,1,0:T(8,128)(2,1)S(1)} collective-permute-done((bf16[2,128,128]{2,1,0:T(8,128)(2,1)S(1)}, bf16[2,128,128]{2,1,0:T(8,128)(2,1)S(1)}, u32[]{:S(2)}, u32[]{:S(2)}) %collective-permute-start.18) | collective-permute-done | bytes 65568 | tf_op jit(solution)/shard_map/ppermute | solution.py:190
  50.3 1.1 %shard_map.84 = (bf16[128,2048]{1,0:T(8,128)(2,1)}, bf16[128,2048]{1,0:T(8,128)(2,1)}) custom-call(bf16[128,2048]{1,0:T(8,128)(2,1)S(1)} %get-tuple-element.167.k_ref, bf16[128,2048]{1,0:T(8,128)(2,1)S(1)} %get-tuple-element.168.v_ref, f32[8,128,128]{2,1,0:T(8,128)S(1)} %get-tuple-element.190.gk_ref, f32[8,128,128]{2,1,0:T(8,128)S(1)} %get-tuple-element.191.gv_ref, ...), custom_call_target="tpu_custom_call" | custom-call | flops 67108864 | bytes 4718592 | tf_op jit(solution)/shard_map/pallas_call | solution.py:176
  51.5 1.1 %shard_map.85 = (bf16[128,2048]{1,0:T(8,128)(2,1)}, bf16[128,2048]{1,0:T(8,128)(2,1)}) custom-call(bf16[128,2048]{1,0:T(8,128)(2,1)S(1)} %get-tuple-element.167.k_ref, bf16[128,2048]{1,0:T(8,128)(2,1)S(1)} %get-tuple-element.168.v_ref, f32[8,128,128]{2,1,0:T(8,128)S(1)} %get-tuple-element.183.gk_ref, ...), custom_call_target="tpu_custom_call", output_to_operand_aliasing={{0}: (6, {}), {1}: (7, {})} | custom-call | flops 67108864 | bytes 4718592 | tf_op jit(solution)/shard_map/pallas_call | solution.py:176
  (59 shorter events, 9.8 us)
Async XLA Ops:
  0.6 8.0 %copy-start.1 = (bf16[128,2048]{1,0:T(8,128)(2,1)S(1)}, bf16[128,2048]{1,0:T(8,128)(2,1)}, u32[]{:S(2)}) copy-start(bf16[128,2048]{1,0:T(8,128)(2,1)} %g_ref.7) | copy-start | bytes 1572868
  2.4 6.2 %copy-start = (bf16[128,2048]{1,0:T(8,128)(2,1)S(1)}, bf16[128,2048]{1,0:T(8,128)(2,1)}, u32[]{:S(2)}) copy-start(bf16[128,2048]{1,0:T(8,128)(2,1)} %q_ref.11) | copy-start | bytes 1572868
  2.4 1.5 %collective-permute-start.2 = (bf16[4,128,128]{2,1,0:T(8,128)(2,1)S(1)}, bf16[4,128,128]{2,1,0:T(8,128)(2,1)S(1)}, u32[]{:S(2)}, u32[]{:S(2)}) collective-permute-start(bf16[4,128,128]{2,1,0:T(8,128)(2,1)S(1)} %get-tuple-element.106), channel_id=1, source_target_pairs={{0,1},{1,0},{2,3},{3,2},{4,5},{5,4},{6,7},{7,6},{8,9},{9,8},{10,11... | collective-permute-start | bytes 393224 | tf_op jit(solution)/shard_map/ppermute | solution.py:190
  2.9 4.9 %collective-permute-start = (bf16[4,128,128]{2,1,0:T(8,128)(2,1)S(1)}, bf16[4,128,128]{2,1,0:T(8,128)(2,1)S(1)}, u32[]{:S(2)}, u32[]{:S(2)}) collective-permute-start(bf16[4,128,128]{2,1,0:T(8,128)(2,1)S(1)} %get-tuple-element.104), channel_id=1, source_target_pairs={{0,1},{1,0},{2,3},{3,2},{4,5},{5,4},{6,7},{7,6},{8,9},{9,8},{10,11... | collective-permute-start | bytes 393224 | tf_op jit(solution)/shard_map/ppermute | solution.py:190
  3.9 6.3 %collective-permute-start.4 = (bf16[2,128,128]{2,1,0:T(8,128)(2,1)S(1)}, bf16[2,128,128]{2,1,0:T(8,128)(2,1)S(1)}, u32[]{:S(2)}, u32[]{:S(2)}) collective-permute-start(bf16[2,128,128]{2,1,0:T(8,128)(2,1)S(1)} %get-tuple-element.109), channel_id=1, source_target_pairs={{0,6},{2,4},{4,2},{6,0},{8,14},{10,12},{12,10},{14,8},{1,7},{3,5},... | collective-permute-start | bytes 196616 | tf_op jit(solution)/shard_map/ppermute | solution.py:190
  7.9 4.3 %collective-permute-start.1 = (bf16[2,128,128]{2,1,0:T(8,128)(2,1)S(1)}, bf16[2,128,128]{2,1,0:T(8,128)(2,1)S(1)}, u32[]{:S(2)}, u32[]{:S(2)}) collective-permute-start(bf16[2,128,128]{2,1,0:T(8,128)(2,1)S(1)} %fusion.30), channel_id=1, source_target_pairs={{0,4},{2,6},{4,0},{6,2},{8,12},{10,14},{12,8},{14,10},{1,5},{3,7},... | collective-permute-start | bytes 196616 | tf_op jit(solution)/shard_map/ppermute | solution.py:190
  8.4 4.3 %collective-permute-start.3 = (bf16[2,128,128]{2,1,0:T(8,128)(2,1)S(1)}, bf16[2,128,128]{2,1,0:T(8,128)(2,1)S(1)}, u32[]{:S(2)}, u32[]{:S(2)}) collective-permute-start(bf16[2,128,128]{2,1,0:T(8,128)(2,1)S(1)} %get-tuple-element.213), channel_id=1, source_target_pairs={{0,2},{2,0},{4,6},{6,4},{8,10},{10,8},{12,14},{14,12},{1,3},{3,1},... | collective-permute-start | bytes 196616 | tf_op jit(solution)/shard_map/ppermute | solution.py:190
  12.7 5.2 %collective-permute-start.5 = (bf16[2,128,128]{2,1,0:T(8,128)(2,1)S(1)}, bf16[2,128,128]{2,1,0:T(8,128)(2,1)S(1)}, u32[]{:S(2)}, u32[]{:S(2)}) collective-permute-start(bf16[2,128,128]{2,1,0:T(8,128)(2,1)S(1)} %fusion.51), channel_id=1, source_target_pairs={{0,8},{2,10},{4,12},{6,14},{8,0},{10,2},{12,4},{14,6},{1,9},{3,11}... | collective-permute-start | bytes 196616 | tf_op jit(solution)/shard_map/ppermute | solution.py:190
  18.1 4.3 %collective-permute-start.8 = (bf16[2,128,128]{2,1,0:T(8,128)(2,1)S(1)}, bf16[2,128,128]{2,1,0:T(8,128)(2,1)S(1)}, u32[]{:S(2)}, u32[]{:S(2)}) collective-permute-start(bf16[2,128,128]{2,1,0:T(8,128)(2,1)S(1)} %get-tuple-element.204), channel_id=1, source_target_pairs={{0,4},{2,6},{4,0},{6,2},{8,12},{10,14},{12,8},{14,10},{1,5},{3,7},... | collective-permute-start | bytes 196616 | tf_op jit(solution)/shard_map/ppermute | solution.py:190
  19.7 5.9 %collective-permute-start.6 = (bf16[2,128,128]{2,1,0:T(8,128)(2,1)S(1)}, bf16[2,128,128]{2,1,0:T(8,128)(2,1)S(1)}, u32[]{:S(2)}, u32[]{:S(2)}) collective-permute-start(bf16[2,128,128]{2,1,0:T(8,128)(2,1)S(1)} %get-tuple-element.205), channel_id=1, source_target_pairs={{0,6},{2,4},{4,2},{6,0},{8,14},{10,12},{12,10},{14,8},{1,7},{3,5},... | collective-permute-start | bytes 196616 | tf_op jit(solution)/shard_map/ppermute | solution.py:190
  20.6 5.0 %collective-permute-start.7 = (bf16[2,128,128]{2,1,0:T(8,128)(2,1)S(1)}, bf16[2,128,128]{2,1,0:T(8,128)(2,1)S(1)}, u32[]{:S(2)}, u32[]{:S(2)}) collective-permute-start(bf16[2,128,128]{2,1,0:T(8,128)(2,1)S(1)} %get-tuple-element.206), channel_id=1, source_target_pairs={{0,2},{2,0},{4,6},{6,4},{8,10},{10,8},{12,14},{14,12},{1,3},{3,1},... | collective-permute-start | bytes 196616 | tf_op jit(solution)/shard_map/ppermute | solution.py:190
  25.7 1.4 %collective-permute-start.12 = (bf16[4,128,128]{2,1,0:T(8,128)(2,1)S(1)}, bf16[4,128,128]{2,1,0:T(8,128)(2,1)S(1)}, u32[]{:S(2)}, u32[]{:S(2)}) collective-permute-start(bf16[4,128,128]{2,1,0:T(8,128)(2,1)S(1)} %pad_maximum_fusion.2), channel_id=1, source_target_pairs={{0,1},{1,0},{2,3},{3,2},{4,5},{5,4},{6,7},{7,6},{8,9},{9,8},{10,11... | collective-permute-start | bytes 393224 | tf_op jit(solution)/shard_map/ppermute | solution.py:190
  25.8 2.6 %collective-permute-start.9 = (bf16[4,128,128]{2,1,0:T(8,128)(2,1)S(1)}, bf16[4,128,128]{2,1,0:T(8,128)(2,1)S(1)}, u32[]{:S(2)}, u32[]{:S(2)}) collective-permute-start(bf16[4,128,128]{2,1,0:T(8,128)(2,1)S(1)} %pad_maximum_fusion), channel_id=1, source_target_pairs={{0,1},{1,0},{2,3},{3,2},{4,5},{5,4},{6,7},{7,6},{8,9},{9,8},{10,11... | collective-permute-start | bytes 393224 | tf_op jit(solution)/shard_map/ppermute | solution.py:190
  27.7 1.7 %collective-permute-start.13 = (bf16[4,128,128]{2,1,0:T(8,128)(2,1)S(1)}, bf16[4,128,128]{2,1,0:T(8,128)(2,1)S(1)}, u32[]{:S(2)}, u32[]{:S(2)}) collective-permute-start(bf16[4,128,128]{2,1,0:T(8,128)(2,1)S(1)} %get-tuple-element.141), channel_id=1, source_target_pairs={{0,1},{1,0},{2,3},{3,2},{4,5},{5,4},{6,7},{7,6},{8,9},{9,8},{10,11... | collective-permute-start | bytes 393224 | tf_op jit(solution)/shard_map/ppermute | solution.py:190
  29.0 2.5 %collective-permute-start.10 = (bf16[4,128,128]{2,1,0:T(8,128)(2,1)S(1)}, bf16[4,128,128]{2,1,0:T(8,128)(2,1)S(1)}, u32[]{:S(2)}, u32[]{:S(2)}) collective-permute-start(bf16[4,128,128]{2,1,0:T(8,128)(2,1)S(1)} %get-tuple-element.133), channel_id=1, source_target_pairs={{0,1},{1,0},{2,3},{3,2},{4,5},{5,4},{6,7},{7,6},{8,9},{9,8},{10,11... | collective-permute-start | bytes 393224 | tf_op jit(solution)/shard_map/ppermute | solution.py:190
  29.5 5.8 %collective-permute-start.15 = (bf16[2,128,128]{2,1,0:T(8,128)(2,1)S(1)}, bf16[2,128,128]{2,1,0:T(8,128)(2,1)S(1)}, u32[]{:S(2)}, u32[]{:S(2)}) collective-permute-start(bf16[2,128,128]{2,1,0:T(8,128)(2,1)S(1)} %get-tuple-element.147), channel_id=1, source_target_pairs={{0,6},{2,4},{4,2},{6,0},{8,14},{10,12},{12,10},{14,8},{1,7},{3,5},... | collective-permute-start | bytes 196616 | tf_op jit(solution)/shard_map/ppermute | solution.py:190
  30.9 5.1 %collective-permute-start.14 = (bf16[2,128,128]{2,1,0:T(8,128)(2,1)S(1)}, bf16[2,128,128]{2,1,0:T(8,128)(2,1)S(1)}, u32[]{:S(2)}, u32[]{:S(2)}) collective-permute-start(bf16[2,128,128]{2,1,0:T(8,128)(2,1)S(1)} %get-tuple-element.210), channel_id=1, source_target_pairs={{0,2},{2,0},{4,6},{6,4},{8,10},{10,8},{12,14},{14,12},{1,3},{3,1},... | collective-permute-start | bytes 196616 | tf_op jit(solution)/shard_map/ppermute | solution.py:190
  31.6 4.4 %collective-permute-start.11 = (bf16[2,128,128]{2,1,0:T(8,128)(2,1)S(1)}, bf16[2,128,128]{2,1,0:T(8,128)(2,1)S(1)}, u32[]{:S(2)}, u32[]{:S(2)}) collective-permute-start(bf16[2,128,128]{2,1,0:T(8,128)(2,1)S(1)} %fusion.41), channel_id=1, source_target_pairs={{0,4},{2,6},{4,0},{6,2},{8,12},{10,14},{12,8},{14,10},{1,5},{3,7},... | collective-permute-start | bytes 196616 | tf_op jit(solution)/shard_map/ppermute | solution.py:190
  36.0 6.3 %collective-permute-start.16 = (bf16[2,128,128]{2,1,0:T(8,128)(2,1)S(1)}, bf16[2,128,128]{2,1,0:T(8,128)(2,1)S(1)}, u32[]{:S(2)}, u32[]{:S(2)}) collective-permute-start(bf16[2,128,128]{2,1,0:T(8,128)(2,1)S(1)} %fusion.53), channel_id=1, source_target_pairs={{0,8},{2,10},{4,12},{6,14},{8,0},{10,2},{12,4},{14,6},{1,9},{3,11}... | collective-permute-start | bytes 196616 | tf_op jit(solution)/shard_map/ppermute | solution.py:190
  42.5 4.3 %collective-permute-start.19 = (bf16[2,128,128]{2,1,0:T(8,128)(2,1)S(1)}, bf16[2,128,128]{2,1,0:T(8,128)(2,1)S(1)}, u32[]{:S(2)}, u32[]{:S(2)}) collective-permute-start(bf16[2,128,128]{2,1,0:T(8,128)(2,1)S(1)} %get-tuple-element.200), channel_id=1, source_target_pairs={{0,4},{2,6},{4,0},{6,2},{8,12},{10,14},{12,8},{14,10},{1,5},{3,7},... | collective-permute-start | bytes 196616 | tf_op jit(solution)/shard_map/ppermute | solution.py:190
  43.0 6.6 %collective-permute-start.17 = (bf16[2,128,128]{2,1,0:T(8,128)(2,1)S(1)}, bf16[2,128,128]{2,1,0:T(8,128)(2,1)S(1)}, u32[]{:S(2)}, u32[]{:S(2)}) collective-permute-start(bf16[2,128,128]{2,1,0:T(8,128)(2,1)S(1)} %get-tuple-element.201), channel_id=1, source_target_pairs={{0,6},{2,4},{4,2},{6,0},{8,14},{10,12},{12,10},{14,8},{1,7},{3,5},... | collective-permute-start | bytes 196616 | tf_op jit(solution)/shard_map/ppermute | solution.py:190
  45.3 4.3 %collective-permute-start.18 = (bf16[2,128,128]{2,1,0:T(8,128)(2,1)S(1)}, bf16[2,128,128]{2,1,0:T(8,128)(2,1)S(1)}, u32[]{:S(2)}, u32[]{:S(2)}) collective-permute-start(bf16[2,128,128]{2,1,0:T(8,128)(2,1)S(1)} %get-tuple-element.202), channel_id=1, source_target_pairs={{0,2},{2,0},{4,6},{6,4},{8,10},{10,8},{12,14},{14,12},{1,3},{3,1},... | collective-permute-start | bytes 196616 | tf_op jit(solution)/shard_map/ppermute | solution.py:190
  49.7 1.7 %collective-permute-start.21 = (bf16[4,128,128]{2,1,0:T(8,128)(2,1)S(1)}, bf16[4,128,128]{2,1,0:T(8,128)(2,1)S(1)}, u32[]{:S(2)}, u32[]{:S(2)}) collective-permute-start(bf16[4,128,128]{2,1,0:T(8,128)(2,1)S(1)} %pad_maximum_fusion.5), channel_id=1, source_target_pairs={{0,1},{1,0},{2,3},{3,2},{4,5},{5,4},{6,7},{7,6},{8,9},{9,8},{10,11... | collective-permute-start | bytes 393224 | tf_op jit(solution)/shard_map/ppermute | solution.py:190
  49.8 1.7 %collective-permute-start.20 = (bf16[4,128,128]{2,1,0:T(8,128)(2,1)S(1)}, bf16[4,128,128]{2,1,0:T(8,128)(2,1)S(1)}, u32[]{:S(2)}, u32[]{:S(2)}) collective-permute-start(bf16[4,128,128]{2,1,0:T(8,128)(2,1)S(1)} %get-tuple-element.187), channel_id=1, source_target_pairs={{0,1},{1,0},{2,3},{3,2},{4,5},{5,4},{6,7},{7,6},{8,9},{9,8},{10,11... | collective-permute-start | bytes 393224 | tf_op jit(solution)/shard_map/ppermute | solution.py:190

commit v5 on v4

--- a/solution.py
+++ b/solution.py
@@ -45,11 +45,23 @@
         self.kept = self.half // self.groups
         self.part = self.half // 2
 
-    def columns(self, slot, width=1):
+    def head(self, slot, levels):
         head = jnp.int32(slot)
-        for level in range(self.steps + 1):
+        for level in levels:
             head = lax.bitwise_xor(head, place_bit(level) * (self.heads >> (level + 1)))
-        return pl.ds(pl.multiple_of(head * HEAD_DIM, HEAD_DIM), width * HEAD_DIM)
+        return head
+
+    def columns(self, slot):
+        head = self.head(slot, range(self.steps + 1))
+        return pl.ds(pl.multiple_of(head * HEAD_DIM, HEAD_DIM), HEAD_DIM)
+
+    def block(self, part, far):
+        head = self.head(self.base(part, far), range(2))
+        return pl.ds(pl.multiple_of(head * HEAD_DIM, HEAD_DIM), self.part * HEAD_DIM)
+
+    def inside(self, number):
+        head = self.head(number, range(2, self.steps + 1))
+        return pl.ds(pl.multiple_of(head * HEAD_DIM, HEAD_DIM), HEAD_DIM)
 
     def mask(self, group):
         return sum(((group >> (self.steps - 1 - j)) & 1) << j for j in range(self.steps))
@@ -111,50 +123,64 @@
 
 
 def local_grads_body(plan, far, q_ref, k_ref, v_ref, probs_ref, *rest):
-    first, second, rest = rest[:3], rest[3:6], rest[6:]
-    *_, gk_ref, gv_ref, normed_out, gq_out, gq_buf, sems = rest
+    found, rest = (rest[:3], rest[3:6]), rest[6:]
+    *_, gk_ref, gv_ref, normed_out, gq_out, normed_buf, gq_buf, sems = rest
     mask = causal_mask()
-    copies, held = [], {}
-    for part, refs in enumerate((first, second)):
+    copies = []
+    for part, (normed_ref, raw_ref, state_ref) in enumerate(found):
         for number in range(plan.part):
-            slot = plan.base(part, far) + number
-            held[slot] = [ref.at[number] for ref in refs]
-    for slot, (normed_ref, _, _) in held.items():
-        at, number = plan.columns(slot), slot % plan.half
-        copies.append(pltpu.make_async_copy(normed_ref, normed_out.at[:, at], sems.at[0, number]))
+            normed_buf[part, :, plan.inside(number)] = normed_ref[number]
+        to = plan.block(part, far)
+        copies.append(pltpu.make_async_copy(normed_buf.at[part], normed_out.at[:, to], sems.at[0, part]))
         copies[-1].start()
-    for slot, (_, raw_ref, state_ref) in held.items():
-        at, number = plan.columns(slot), slot % plan.half
-        raw, state = raw_ref[...], state_ref[...]
-        grad_probs = jnp.where(mask, dot(raw, v_ref[:, at], NT), 0.0).astype(BF)
-        gq_buf[number] = (dot(grad_probs, k_ref[:, at], NN) + dot(raw, state, NT)).astype(BF)
-        copies.append(pltpu.make_async_copy(gq_buf.at[number], gq_out.at[:, at], sems.at[1, number]))
+    for part, (normed_ref, raw_ref, state_ref) in enumerate(found):
+        for number in range(plan.part):
+            slot = part * plan.part + number
+            at = plan.columns(far * plan.half + slot)
+            raw, state = raw_ref[number], state_ref[number]
+            grad_probs = jnp.where(mask, dot(raw, v_ref[:, at], NT), 0.0).astype(BF)
+            grad_query = dot(grad_probs, k_ref[:, at], NN) + dot(raw, state, NT)
+            gq_buf[part, :, plan.inside(number)] = grad_query.astype(BF)
+            gk_ref[slot] = dot(grad_probs, q_ref[:, at], TN)
+            gv_ref[slot] = dot(probs_ref[slot], raw, TN)
+        to = plan.block(part, far)
+        copies.append(pltpu.make_async_copy(gq_buf.at[part], gq_out.at[:, to], sems.at[1, part]))
         copies[-1].start()
-        gk_ref[number] = dot(grad_probs, q_ref[:, at], TN)
-        gv_ref[number] = dot(probs_ref[number], raw, TN)
     for copy in copies:
         copy.wait()
 
 
-def last_grads_body(plan, pieces, k_ref, v_ref, gk_ref, gv_ref, *rest):
-    states = rest[: len(pieces)]
-    *_, gk_out, gv_out, gk_buf, gv_buf, sems = rest
+def last_grads(plan, part, far, k_ref, v_ref, gk_ref, gv_ref, state_ref, gk_to, gv_to):
+    for number in range(plan.part):
+        slot = part * plan.part + number
+        at, to = plan.columns(far * plan.half + slot), plan.inside(number)
+        state = state_ref[number]
+        gk_to[part, :, to] = (gk_ref[slot] + dot(v_ref[:, at], state, NT)).astype(BF)
+        gv_to[part, :, to] = (gv_ref[slot] + dot(k_ref[:, at], state, NN)).astype(BF)
+
+
+def near_grads_body(plan, k_ref, v_ref, gk_ref, gv_ref, *rest):
+    *states, gk_out, gv_out = rest
+    for part, state_ref in enumerate(states):
+        last_grads(plan, part, 0, k_ref, v_ref, gk_ref, gv_ref, state_ref, gk_out, gv_out)
+
+
+def far_grads_body(plan, k_ref, v_ref, gk_ref, gv_ref, *rest):
+    *states, gk_near, gv_near, gk_out, gv_out, gk_buf, gv_buf, sems = rest
     copies = []
-    for (part, far), state_ref in zip(pieces, states):
-        for inside in range(plan.part):
-            slot = plan.base(part, far) + inside
-            at, number = plan.columns(slot), slot % plan.half
-            state = state_ref[inside]
-            gk_buf[number] = (gk_ref[number] + dot(v_ref[:, at], state, NT)).astype(BF)
-            copies.append(
-                pltpu.make_async_copy(gk_buf.at[number], gk_out.at[:, at], sems.at[0, number])
-            )
+
+    def leave(part, far, pair):
+        to = plan.block(part, far)
+        for number, (ref, out) in enumerate(zip(pair, (gk_out, gv_out))):
+            sem = sems.at[number, far, part]
+            copies.append(pltpu.make_async_copy(ref.at[part], out.at[:, to], sem))
             copies[-1].start()
-            gv_buf[number] = (gv_ref[number] + dot(k_ref[:, at], state, NN)).astype(BF)
-            copies.append(
-                pltpu.make_async_copy(gv_buf.at[number], gv_out.at[:, at], sems.at[1, number])
-            )
-            copies[-1].start()
+
+    for part in range(2):
+        leave(part, 0, (gk_near, gv_near))
+    for part, state_ref in enumerate(states):
+        last_grads(plan, part, 1, k_ref, v_ref, gk_ref, gv_ref, state_ref, gk_buf, gv_buf)
+        leave(part, 1, (gk_buf, gv_buf))
     for copy in copies:
         copy.wait()
 
@@ -269,6 +295,7 @@
     unit = 2 * BLOCK * HEAD_DIM * HEAD_DIM * plan.half
     vm, dma = pltpu.VMEM, pltpu.SemaphoreType.DMA
     whole = hbm((rows, width), BF)
+    buf = vm((2, rows, plan.part * HEAD_DIM), BF)
 
     *states, bits, key_vm, value_vm = call(
         functools.partial(key_value_body, plan), (key, value),
@@ -299,12 +326,13 @@
             [vm(part_state, BF), vm(part_state, BF), vm(part_state, BF if is_far else F32)], unit,
         )
 
-    normed = [[], []]
-    for part in range(2):
-        normed[0].append(norm(part, 0, near[part]))
-        far[part], normed[0][part] = lax.optimization_barrier((far[part], normed[0][part]))
+    normed = [[None, None], []]
+    normed[0][0] = norm(0, 0, near[0])
+    far[0], normed[0][0] = lax.optimization_barrier((far[0], normed[0][0]))
     for part in range(2):
         normed[1].append(norm(part, 1, far[part]))
+    near[1], normed[1] = lax.optimization_barrier((near[1], normed[1]))
+    normed[0][1] = norm(1, 0, near[1])
     partials = ()
 
     def local_grads(is_far, operands):
@@ -312,7 +340,7 @@
         out = call(
             functools.partial(local_grads_body, plan, is_far), operands,
             [vm(half_state, F32), vm(half_state, F32), whole, whole],
-            5 * unit, (vm(half_state, BF), dma((2, plan.half))), partial=partials,
+            5 * unit, (buf, buf, dma((2, 2))), partial=partials,
         )
         partials = out[2:]
         return out[:2]
@@ -330,18 +358,15 @@
     )
     grads = [given["share"], given["total"]]
     normed_out, grad_q = partials
-    partials = ()
-    buf = vm(half_state, BF)
-    for pieces in (((0, 0), (1, 0)), ((0, 1), (1, 1))):
-        is_far = pieces[0][1]
-        found = [(far if is_far else near)[part] for part, _ in pieces]
-        partials = call(
-            functools.partial(last_grads_body, plan, pieces), (key_vm, value_vm, *grads[is_far], *found),
-            [whole, whole], unit * len(pieces), (buf, buf, dma((2, plan.half))), partial=partials,
-        )
-        if not is_far:
-            far, partials = lax.optimization_barrier((far, partials))
-    grad_k, grad_v = partials
+    near_grads = call(
+        functools.partial(near_grads_body, plan), (key_vm, value_vm, *grads[0], *near),
+        [buf, buf], 2 * unit,
+    )
+    far, near_grads = lax.optimization_barrier((far, near_grads))
+    grad_k, grad_v = call(
+        functools.partial(far_grads_body, plan), (key_vm, value_vm, *grads[1], *far, *near_grads),
+        [whole, whole], 2 * unit, (buf, buf, dma((2, 2, 2))),
+    )
     return normed_out, grad_q, grad_k, grad_v
 
 

time: 52.8 us -> 52.6 us (level)
  Pallas kernels: 13.1 us -> 12.3 us
  waiting for transfers between devices: 14.1 us -> 14.8 us
    pallas_call x11, Pallas kernels: 13.1 us -> 12.3 us  [call(): pl.pallas_call(body, out_shape=outs, in_specs=in_specs, out_specs=[anywhe...]
    ppermute x22, waiting for transfers between devices: 14.1 us -> 14.8 us  [swap(): return lax.ppermute(value, axes, pairs)]
  transfers between devices with their start and end apart: 22 -> 22, of which waited for: 12 -> 16; matrix products, arithmetic and copies ran while one was open for 1% -> 1% of each run, Pallas kernels for 19% -> 17%
where the time goes in v5:
time: 52.6 us; the launch traced here: 52.4 us
  starting transfers between devices  23.6 us (45%)
  waiting for transfers between devices  14.8 us (28%)
  Pallas kernels  12.3 us (23%)
  between operations  0.9 us (2%)
  other arithmetic  0.89 us (2%)
    ppermute x22, starting transfers between devices, swap(): return lax.ppermute(value, axes, pairs)  23.6 us
    ppermute x22, waiting for transfers between devices, swap(): return lax.ppermute(value, axes, pairs)  14.8 us
    pallas_call x11, Pallas kernels, call(): pl.pallas_call(body, out_shape=outs, in_specs=in_specs, out_specs=[anywhe...  12.3 us
  transfers between devices with their start and end apart: 22, of which 16 were waited for; matrix products, arithmetic and copies ran while one was open for 1% of the time, Pallas kernels for 17%

profile of v5, /device:TPU:0, one launch (start us, length us, event | category | flops | bytes accessed | tf_op | source)
XLA Modules:
  0.0 52.4 jit_solution(6771788306460067618)
XLA Ops:
  0.6 1.7 %shard_map.75 = (bf16[4,128,128]{2,1,0:T(8,128)(2,1)S(1)}, bf16[4,128,128]{2,1,0:T(8,128)(2,1)S(1)}, f32[4,128,128]{2,1,0:T(8,128)S(1)}, f32[4,128,128]{2,1,0:T(...) custom-call(bf16[128,2048]{1,0:T(8,128)(2,1)} %k_ref.1, ...), custom_call_target="tpu_custom_call" | custom-call | flops 67108864 | bytes 2097152 | tf_op jit(solution)/shard_map/pallas_call | solution.py:202
  3.0 0.9 %collective-permute-done.2 = bf16[4,128,128]{2,1,0:T(8,128)(2,1)S(1)} collective-permute-done((bf16[4,128,128]{2,1,0:T(8,128)(2,1)S(1)}, bf16[4,128,128]{2,1,0:T(8,128)(2,1)S(1)}, u32[]{:S(2)}, u32[]{:S(2)}) %collective-permute-start.2) | collective-permute-done | bytes 131104 | tf_op jit(solution)/shard_map/ppermute | solution.py:216
  3.9 3.9 %collective-permute-start.4 = (bf16[2,128,128]{2,1,0:T(8,128)(2,1)S(1)}, bf16[2,128,128]{2,1,0:T(8,128)(2,1)S(1)}, u32[]{:S(2)}, u32[]{:S(2)}) collective-permute-start(bf16[2,128,128]{2,1,0:T(8,128)(2,1)S(1)} %get-tuple-element.112), channel_id=1, source_target_pairs={{0,6},{2,4},{4,2},{6,0},{8,14},{10,12},{12,10},{14,8},{1,7},{3,5},... | collective-permute-start | bytes 196616 | tf_op jit(solution)/shard_map/ppermute | solution.py:216
  8.6 1.4 %shard_map.76 = (bf16[8,128,128]{2,1,0:T(8,128)(2,1)S(1)}, f32[8,128,128]{2,1,0:T(8,128)S(1)}) custom-call(bf16[128,2048]{1,0:T(8,128)(2,1)S(1)} %copy-done, bf16[128,2048]{1,0:T(8,128)(2,1)S(1)} %get-tuple-element.173.k_ref, bf16[128,2048]{1,0:T(8,128)(2,1)S(1)} %get-tuple-element.174.v_ref, bf16[128,2048]{1,0:T(8,128)(2,1)S(1)} %copy-done.1), custom_call_target="tpu_custom_call" | custom-call | flops 67108864 | bytes 4194304 | tf_op jit(solution)/shard_map/pallas_call | solution.py:202
  10.3 1.9 %collective-permute-done.1 = bf16[2,128,128]{2,1,0:T(8,128)(2,1)S(1)} collective-permute-done((bf16[2,128,128]{2,1,0:T(8,128)(2,1)S(1)}, bf16[2,128,128]{2,1,0:T(8,128)(2,1)S(1)}, u32[]{:S(2)}, u32[]{:S(2)}) %collective-permute-start.1) | collective-permute-done | bytes 65568 | tf_op jit(solution)/shard_map/ppermute | solution.py:216
  12.7 2.7 %collective-permute-start.5 = (bf16[2,128,128]{2,1,0:T(8,128)(2,1)S(1)}, bf16[2,128,128]{2,1,0:T(8,128)(2,1)S(1)}, u32[]{:S(2)}, u32[]{:S(2)}) collective-permute-start(bf16[2,128,128]{2,1,0:T(8,128)(2,1)S(1)} %fusion.51), channel_id=1, source_target_pairs={{0,8},{2,10},{4,12},{6,14},{8,0},{10,2},{12,4},{14,6},{1,9},{3,11}... | collective-permute-start | bytes 196616 | tf_op jit(solution)/shard_map/ppermute | solution.py:216
  15.4 1.4 %shard_map.77 = (bf16[8,128,128]{2,1,0:T(8,128)(2,1)S(1)}, f32[8,128,128]{2,1,0:T(8,128)S(1)}) custom-call(bf16[128,2048]{1,0:T(8,128)(2,1)S(1)} %copy-done, bf16[128,2048]{1,0:T(8,128)(2,1)S(1)} %get-tuple-element.173.k_ref, bf16[128,2048]{1,0:T(8,128)(2,1)S(1)} %get-tuple-element.174.v_ref), custom_call_target="tpu_custom_call" | custom-call | flops 67108864 | bytes 3145728 | tf_op jit(solution)/shard_map/pallas_call | solution.py:202
  16.7 1.2 %collective-permute-done.5 = bf16[2,128,128]{2,1,0:T(8,128)(2,1)S(1)} collective-permute-done((bf16[2,128,128]{2,1,0:T(8,128)(2,1)S(1)}, bf16[2,128,128]{2,1,0:T(8,128)(2,1)S(1)}, u32[]{:S(2)}, u32[]{:S(2)}) %collective-permute-start.5) | collective-permute-done | bytes 65568 | tf_op jit(solution)/shard_map/ppermute | solution.py:216
  18.1 1.6 %collective-permute-start.8 = (bf16[2,128,128]{2,1,0:T(8,128)(2,1)S(1)}, bf16[2,128,128]{2,1,0:T(8,128)(2,1)S(1)}, u32[]{:S(2)}, u32[]{:S(2)}) collective-permute-start(bf16[2,128,128]{2,1,0:T(8,128)(2,1)S(1)} %get-tuple-element.210), channel_id=1, source_target_pairs={{0,4},{2,6},{4,0},{6,2},{8,12},{10,14},{12,8},{14,10},{1,5},{3,7},... | collective-permute-start | bytes 196616 | tf_op jit(solution)/shard_map/ppermute | solution.py:216
  19.7 0.9 %collective-permute-start.6 = (bf16[2,128,128]{2,1,0:T(8,128)(2,1)S(1)}, bf16[2,128,128]{2,1,0:T(8,128)(2,1)S(1)}, u32[]{:S(2)}, u32[]{:S(2)}) collective-permute-start(bf16[2,128,128]{2,1,0:T(8,128)(2,1)S(1)} %get-tuple-element.211), channel_id=1, source_target_pairs={{0,6},{2,4},{4,2},{6,0},{8,14},{10,12},{12,10},{14,8},{1,7},{3,5},... | collective-permute-start | bytes 196616 | tf_op jit(solution)/shard_map/ppermute | solution.py:216
  20.6 1.0 %collective-permute-start.7 = (bf16[2,128,128]{2,1,0:T(8,128)(2,1)S(1)}, bf16[2,128,128]{2,1,0:T(8,128)(2,1)S(1)}, u32[]{:S(2)}, u32[]{:S(2)}) collective-permute-start(bf16[2,128,128]{2,1,0:T(8,128)(2,1)S(1)} %get-tuple-element.212), channel_id=1, source_target_pairs={{0,2},{2,0},{4,6},{6,4},{8,10},{10,8},{12,14},{14,12},{1,3},{3,1},... | collective-permute-start | bytes 196616 | tf_op jit(solution)/shard_map/ppermute | solution.py:216
  21.7 0.8 %collective-permute-done.8 = bf16[2,128,128]{2,1,0:T(8,128)(2,1)S(1)} collective-permute-done((bf16[2,128,128]{2,1,0:T(8,128)(2,1)S(1)}, bf16[2,128,128]{2,1,0:T(8,128)(2,1)S(1)}, u32[]{:S(2)}, u32[]{:S(2)}) %collective-permute-start.8) | collective-permute-done | bytes 65568 | tf_op jit(solution)/shard_map/ppermute | solution.py:216
  22.5 3.1 %collective-permute-done.7 = bf16[2,128,128]{2,1,0:T(8,128)(2,1)S(1)} collective-permute-done((bf16[2,128,128]{2,1,0:T(8,128)(2,1)S(1)}, bf16[2,128,128]{2,1,0:T(8,128)(2,1)S(1)}, u32[]{:S(2)}, u32[]{:S(2)}) %collective-permute-start.7) | collective-permute-done | bytes 65568 | tf_op jit(solution)/shard_map/ppermute | solution.py:216
  29.6 1.4 %collective-permute-start.15 = (bf16[2,128,128]{2,1,0:T(8,128)(2,1)S(1)}, bf16[2,128,128]{2,1,0:T(8,128)(2,1)S(1)}, u32[]{:S(2)}, u32[]{:S(2)}) collective-permute-start(bf16[2,128,128]{2,1,0:T(8,128)(2,1)S(1)} %get-tuple-element.153), channel_id=1, source_target_pairs={{0,6},{2,4},{4,2},{6,0},{8,14},{10,12},{12,10},{14,8},{1,7},{3,5},... | collective-permute-start | bytes 196616 | tf_op jit(solution)/shard_map/ppermute | solution.py:216
  31.0 0.9 %collective-permute-start.12 = (bf16[2,128,128]{2,1,0:T(8,128)(2,1)S(1)}, bf16[2,128,128]{2,1,0:T(8,128)(2,1)S(1)}, u32[]{:S(2)}, u32[]{:S(2)}) collective-permute-start(bf16[2,128,128]{2,1,0:T(8,128)(2,1)S(1)} %fusion.41), channel_id=1, source_target_pairs={{0,4},{2,6},{4,0},{6,2},{8,12},{10,14},{12,8},{14,10},{1,5},{3,7},... | collective-permute-start | bytes 196616 | tf_op jit(solution)/shard_map/ppermute | solution.py:216
  31.9 1.3 %collective-permute-start.14 = (bf16[2,128,128]{2,1,0:T(8,128)(2,1)S(1)}, bf16[2,128,128]{2,1,0:T(8,128)(2,1)S(1)}, u32[]{:S(2)}, u32[]{:S(2)}) collective-permute-start(bf16[2,128,128]{2,1,0:T(8,128)(2,1)S(1)} %get-tuple-element.216), channel_id=1, source_target_pairs={{0,2},{2,0},{4,6},{6,4},{8,10},{10,8},{12,14},{14,12},{1,3},{3,1},... | collective-permute-start | bytes 196616 | tf_op jit(solution)/shard_map/ppermute | solution.py:216
  33.2 2.1 %shard_map.82 = (f32[8,128,128]{2,1,0:T(8,128)S(1)}, f32[8,128,128]{2,1,0:T(8,128)S(1)}, bf16[128,2048]{1,0:T(8,128)(2,1)}, bf16[128,2048]{1,0:T(8,128)(2,1)}) custom-call(bf16[128,2048]{1,0:T(8,128)(2,1)S(1)} %copy-done, bf16[128,2048]{1,0:T(8,128)(2,1)S(1)} %get-tuple-element.173.k_ref, bf16[128,2048]{1,0:T(8,128)(2,1)S(1)} %get-tuple-element.174.v_ref, ...), custom_call_target="tpu_custom_call" | custom-call | flops 167772160 | bytes 5242880 | tf_op jit(solution)/shard_map/pallas_call | solution.py:202
  36.2 3.2 %collective-permute-start.16 = (bf16[2,128,128]{2,1,0:T(8,128)(2,1)S(1)}, bf16[2,128,128]{2,1,0:T(8,128)(2,1)S(1)}, u32[]{:S(2)}, u32[]{:S(2)}) collective-permute-start(bf16[2,128,128]{2,1,0:T(8,128)(2,1)S(1)} %fusion.53), channel_id=1, source_target_pairs={{0,8},{2,10},{4,12},{6,14},{8,0},{10,2},{12,4},{14,6},{1,9},{3,11}... | collective-permute-start | bytes 196616 | tf_op jit(solution)/shard_map/ppermute | solution.py:216
  39.5 2.1 %shard_map.83 = (f32[8,128,128]{2,1,0:T(8,128)S(1)}, f32[8,128,128]{2,1,0:T(8,128)S(1)}, bf16[128,2048]{1,0:T(8,128)(2,1)}, bf16[128,2048]{1,0:T(8,128)(2,1)}) custom-call(bf16[128,2048]{1,0:T(8,128)(2,1)S(1)} %copy-done, bf16[128,2048]{1,0:T(8,128)(2,1)S(1)} %get-tuple-element.173.k_ref, ...), custom_call_target="tpu_custom_call", output_to_operand_aliasing={{2}: (10, {}), {3}: (11, {})} | custom-call | flops 167772160 | bytes 5242880 | tf_op jit(solution)/shard_map/pallas_call | solution.py:202
  41.9 1.6 %collective-permute-start.19 = (bf16[2,128,128]{2,1,0:T(8,128)(2,1)S(1)}, bf16[2,128,128]{2,1,0:T(8,128)(2,1)S(1)}, u32[]{:S(2)}, u32[]{:S(2)}) collective-permute-start(bf16[2,128,128]{2,1,0:T(8,128)(2,1)S(1)} %get-tuple-element.206), channel_id=1, source_target_pairs={{0,4},{2,6},{4,0},{6,2},{8,12},{10,14},{12,8},{14,10},{1,5},{3,7},... | collective-permute-start | bytes 196616 | tf_op jit(solution)/shard_map/ppermute | solution.py:216
  43.4 1.7 %collective-permute-start.17 = (bf16[2,128,128]{2,1,0:T(8,128)(2,1)S(1)}, bf16[2,128,128]{2,1,0:T(8,128)(2,1)S(1)}, u32[]{:S(2)}, u32[]{:S(2)}) collective-permute-start(bf16[2,128,128]{2,1,0:T(8,128)(2,1)S(1)} %get-tuple-element.207), channel_id=1, source_target_pairs={{0,6},{2,4},{4,2},{6,0},{8,14},{10,12},{12,10},{14,8},{1,7},{3,5},... | collective-permute-start | bytes 196616 | tf_op jit(solution)/shard_map/ppermute | solution.py:216
  45.4 0.8 %collective-permute-done.19 = bf16[2,128,128]{2,1,0:T(8,128)(2,1)S(1)} collective-permute-done((bf16[2,128,128]{2,1,0:T(8,128)(2,1)S(1)}, bf16[2,128,128]{2,1,0:T(8,128)(2,1)S(1)}, u32[]{:S(2)}, u32[]{:S(2)}) %collective-permute-start.19) | collective-permute-done | bytes 65568 | tf_op jit(solution)/shard_map/ppermute | solution.py:216
  46.2 3.2 %collective-permute-done.18 = bf16[2,128,128]{2,1,0:T(8,128)(2,1)S(1)} collective-permute-done((bf16[2,128,128]{2,1,0:T(8,128)(2,1)S(1)}, bf16[2,128,128]{2,1,0:T(8,128)(2,1)S(1)}, u32[]{:S(2)}, u32[]{:S(2)}) %collective-permute-start.18) | collective-permute-done | bytes 65568 | tf_op jit(solution)/shard_map/ppermute | solution.py:216
  51.2 1.2 %shard_map.85 = (bf16[128,2048]{1,0:T(8,128)(2,1)}, bf16[128,2048]{1,0:T(8,128)(2,1)}) custom-call(bf16[128,2048]{1,0:T(8,128)(2,1)S(1)} %get-tuple-element.173.k_ref, bf16[128,2048]{1,0:T(8,128)(2,1)S(1)} %get-tuple-element.174.v_ref, f32[8,128,128]{2,1,0:T(8,128)S(1)} %get-tuple-element.189.gk_ref, f32[8,128,128]{2,1,0:T(8,128)S(1)} %get-tuple-element.190.gv_ref, ...), custom_call_target="tpu_custom_call" | custom-call | flops 67108864 | bytes 5767168 | tf_op jit(solution)/shard_map/pallas_call | solution.py:202
  (59 shorter events, 9.6 us)
Async XLA Ops:
  0.6 8.0 %copy-start.1 = (bf16[128,2048]{1,0:T(8,128)(2,1)S(1)}, bf16[128,2048]{1,0:T(8,128)(2,1)}, u32[]{:S(2)}) copy-start(bf16[128,2048]{1,0:T(8,128)(2,1)} %g_ref.7) | copy-start | bytes 1572868
  2.4 6.2 %copy-start = (bf16[128,2048]{1,0:T(8,128)(2,1)S(1)}, bf16[128,2048]{1,0:T(8,128)(2,1)}, u32[]{:S(2)}) copy-start(bf16[128,2048]{1,0:T(8,128)(2,1)} %q_ref.11) | copy-start | bytes 1572868
  2.4 1.5 %collective-permute-start.2 = (bf16[4,128,128]{2,1,0:T(8,128)(2,1)S(1)}, bf16[4,128,128]{2,1,0:T(8,128)(2,1)S(1)}, u32[]{:S(2)}, u32[]{:S(2)}) collective-permute-start(bf16[4,128,128]{2,1,0:T(8,128)(2,1)S(1)} %get-tuple-element.109), channel_id=1, source_target_pairs={{0,1},{1,0},{2,3},{3,2},{4,5},{5,4},{6,7},{7,6},{8,9},{9,8},{10,11... | collective-permute-start | bytes 393224 | tf_op jit(solution)/shard_map/ppermute | solution.py:216
  2.9 4.9 %collective-permute-start = (bf16[4,128,128]{2,1,0:T(8,128)(2,1)S(1)}, bf16[4,128,128]{2,1,0:T(8,128)(2,1)S(1)}, u32[]{:S(2)}, u32[]{:S(2)}) collective-permute-start(bf16[4,128,128]{2,1,0:T(8,128)(2,1)S(1)} %get-tuple-element.107), channel_id=1, source_target_pairs={{0,1},{1,0},{2,3},{3,2},{4,5},{5,4},{6,7},{7,6},{8,9},{9,8},{10,11... | collective-permute-start | bytes 393224 | tf_op jit(solution)/shard_map/ppermute | solution.py:216
  3.9 6.3 %collective-permute-start.4 = (bf16[2,128,128]{2,1,0:T(8,128)(2,1)S(1)}, bf16[2,128,128]{2,1,0:T(8,128)(2,1)S(1)}, u32[]{:S(2)}, u32[]{:S(2)}) collective-permute-start(bf16[2,128,128]{2,1,0:T(8,128)(2,1)S(1)} %get-tuple-element.112), channel_id=1, source_target_pairs={{0,6},{2,4},{4,2},{6,0},{8,14},{10,12},{12,10},{14,8},{1,7},{3,5},... | collective-permute-start | bytes 196616 | tf_op jit(solution)/shard_map/ppermute | solution.py:216
  7.9 4.3 %collective-permute-start.1 = (bf16[2,128,128]{2,1,0:T(8,128)(2,1)S(1)}, bf16[2,128,128]{2,1,0:T(8,128)(2,1)S(1)}, u32[]{:S(2)}, u32[]{:S(2)}) collective-permute-start(bf16[2,128,128]{2,1,0:T(8,128)(2,1)S(1)} %fusion.30), channel_id=1, source_target_pairs={{0,4},{2,6},{4,0},{6,2},{8,12},{10,14},{12,8},{14,10},{1,5},{3,7},... | collective-permute-start | bytes 196616 | tf_op jit(solution)/shard_map/ppermute | solution.py:216
  8.4 4.3 %collective-permute-start.3 = (bf16[2,128,128]{2,1,0:T(8,128)(2,1)S(1)}, bf16[2,128,128]{2,1,0:T(8,128)(2,1)S(1)}, u32[]{:S(2)}, u32[]{:S(2)}) collective-permute-start(bf16[2,128,128]{2,1,0:T(8,128)(2,1)S(1)} %get-tuple-element.218), channel_id=1, source_target_pairs={{0,2},{2,0},{4,6},{6,4},{8,10},{10,8},{12,14},{14,12},{1,3},{3,1},... | collective-permute-start | bytes 196616 | tf_op jit(solution)/shard_map/ppermute | solution.py:216
  12.7 5.2 %collective-permute-start.5 = (bf16[2,128,128]{2,1,0:T(8,128)(2,1)S(1)}, bf16[2,128,128]{2,1,0:T(8,128)(2,1)S(1)}, u32[]{:S(2)}, u32[]{:S(2)}) collective-permute-start(bf16[2,128,128]{2,1,0:T(8,128)(2,1)S(1)} %fusion.51), channel_id=1, source_target_pairs={{0,8},{2,10},{4,12},{6,14},{8,0},{10,2},{12,4},{14,6},{1,9},{3,11}... | collective-permute-start | bytes 196616 | tf_op jit(solution)/shard_map/ppermute | solution.py:216
  18.1 4.3 %collective-permute-start.8 = (bf16[2,128,128]{2,1,0:T(8,128)(2,1)S(1)}, bf16[2,128,128]{2,1,0:T(8,128)(2,1)S(1)}, u32[]{:S(2)}, u32[]{:S(2)}) collective-permute-start(bf16[2,128,128]{2,1,0:T(8,128)(2,1)S(1)} %get-tuple-element.210), channel_id=1, source_target_pairs={{0,4},{2,6},{4,0},{6,2},{8,12},{10,14},{12,8},{14,10},{1,5},{3,7},... | collective-permute-start | bytes 196616 | tf_op jit(solution)/shard_map/ppermute | solution.py:216
  19.7 5.9 %collective-permute-start.6 = (bf16[2,128,128]{2,1,0:T(8,128)(2,1)S(1)}, bf16[2,128,128]{2,1,0:T(8,128)(2,1)S(1)}, u32[]{:S(2)}, u32[]{:S(2)}) collective-permute-start(bf16[2,128,128]{2,1,0:T(8,128)(2,1)S(1)} %get-tuple-element.211), channel_id=1, source_target_pairs={{0,6},{2,4},{4,2},{6,0},{8,14},{10,12},{12,10},{14,8},{1,7},{3,5},... | collective-permute-start | bytes 196616 | tf_op jit(solution)/shard_map/ppermute | solution.py:216
  20.6 5.0 %collective-permute-start.7 = (bf16[2,128,128]{2,1,0:T(8,128)(2,1)S(1)}, bf16[2,128,128]{2,1,0:T(8,128)(2,1)S(1)}, u32[]{:S(2)}, u32[]{:S(2)}) collective-permute-start(bf16[2,128,128]{2,1,0:T(8,128)(2,1)S(1)} %get-tuple-element.212), channel_id=1, source_target_pairs={{0,2},{2,0},{4,6},{6,4},{8,10},{10,8},{12,14},{14,12},{1,3},{3,1},... | collective-permute-start | bytes 196616 | tf_op jit(solution)/shard_map/ppermute | solution.py:216
  25.7 1.4 %collective-permute-start.9 = (bf16[4,128,128]{2,1,0:T(8,128)(2,1)S(1)}, bf16[4,128,128]{2,1,0:T(8,128)(2,1)S(1)}, u32[]{:S(2)}, u32[]{:S(2)}) collective-permute-start(bf16[4,128,128]{2,1,0:T(8,128)(2,1)S(1)} %get-tuple-element.128), channel_id=1, source_target_pairs={{0,1},{1,0},{2,3},{3,2},{4,5},{5,4},{6,7},{7,6},{8,9},{9,8},{10,11... | collective-permute-start | bytes 393224 | tf_op jit(solution)/shard_map/ppermute | solution.py:216
  25.8 1.8 %collective-permute-start.10 = (bf16[4,128,128]{2,1,0:T(8,128)(2,1)S(1)}, bf16[4,128,128]{2,1,0:T(8,128)(2,1)S(1)}, u32[]{:S(2)}, u32[]{:S(2)}) collective-permute-start(bf16[4,128,128]{2,1,0:T(8,128)(2,1)S(1)} %pad_maximum_fusion.3), channel_id=1, source_target_pairs={{0,1},{1,0},{2,3},{3,2},{4,5},{5,4},{6,7},{7,6},{8,9},{9,8},{10,11... | collective-permute-start | bytes 393224 | tf_op jit(solution)/shard_map/ppermute | solution.py:216
  28.2 1.4 %collective-permute-start.13 = (bf16[4,128,128]{2,1,0:T(8,128)(2,1)S(1)}, bf16[4,128,128]{2,1,0:T(8,128)(2,1)S(1)}, u32[]{:S(2)}, u32[]{:S(2)}) collective-permute-start(bf16[4,128,128]{2,1,0:T(8,128)(2,1)S(1)} %get-tuple-element.147), channel_id=1, source_target_pairs={{0,1},{1,0},{2,3},{3,2},{4,5},{5,4},{6,7},{7,6},{8,9},{9,8},{10,11... | collective-permute-start | bytes 393224 | tf_op jit(solution)/shard_map/ppermute | solution.py:216
  28.4 2.7 %collective-permute-start.11 = (bf16[4,128,128]{2,1,0:T(8,128)(2,1)S(1)}, bf16[4,128,128]{2,1,0:T(8,128)(2,1)S(1)}, u32[]{:S(2)}, u32[]{:S(2)}) collective-permute-start(bf16[4,128,128]{2,1,0:T(8,128)(2,1)S(1)} %get-tuple-element.144), channel_id=1, source_target_pairs={{0,1},{1,0},{2,3},{3,2},{4,5},{5,4},{6,7},{7,6},{8,9},{9,8},{10,11... | collective-permute-start | bytes 393224 | tf_op jit(solution)/shard_map/ppermute | solution.py:216
  29.6 5.8 %collective-permute-start.15 = (bf16[2,128,128]{2,1,0:T(8,128)(2,1)S(1)}, bf16[2,128,128]{2,1,0:T(8,128)(2,1)S(1)}, u32[]{:S(2)}, u32[]{:S(2)}) collective-permute-start(bf16[2,128,128]{2,1,0:T(8,128)(2,1)S(1)} %get-tuple-element.153), channel_id=1, source_target_pairs={{0,6},{2,4},{4,2},{6,0},{8,14},{10,12},{12,10},{14,8},{1,7},{3,5},... | collective-permute-start | bytes 196616 | tf_op jit(solution)/shard_map/ppermute | solution.py:216
  31.0 4.4 %collective-permute-start.12 = (bf16[2,128,128]{2,1,0:T(8,128)(2,1)S(1)}, bf16[2,128,128]{2,1,0:T(8,128)(2,1)S(1)}, u32[]{:S(2)}, u32[]{:S(2)}) collective-permute-start(bf16[2,128,128]{2,1,0:T(8,128)(2,1)S(1)} %fusion.41), channel_id=1, source_target_pairs={{0,4},{2,6},{4,0},{6,2},{8,12},{10,14},{12,8},{14,10},{1,5},{3,7},... | collective-permute-start | bytes 196616 | tf_op jit(solution)/shard_map/ppermute | solution.py:216
  31.9 4.3 %collective-permute-start.14 = (bf16[2,128,128]{2,1,0:T(8,128)(2,1)S(1)}, bf16[2,128,128]{2,1,0:T(8,128)(2,1)S(1)}, u32[]{:S(2)}, u32[]{:S(2)}) collective-permute-start(bf16[2,128,128]{2,1,0:T(8,128)(2,1)S(1)} %get-tuple-element.216), channel_id=1, source_target_pairs={{0,2},{2,0},{4,6},{6,4},{8,10},{10,8},{12,14},{14,12},{1,3},{3,1},... | collective-permute-start | bytes 196616 | tf_op jit(solution)/shard_map/ppermute | solution.py:216
  36.2 5.5 %collective-permute-start.16 = (bf16[2,128,128]{2,1,0:T(8,128)(2,1)S(1)}, bf16[2,128,128]{2,1,0:T(8,128)(2,1)S(1)}, u32[]{:S(2)}, u32[]{:S(2)}) collective-permute-start(bf16[2,128,128]{2,1,0:T(8,128)(2,1)S(1)} %fusion.53), channel_id=1, source_target_pairs={{0,8},{2,10},{4,12},{6,14},{8,0},{10,2},{12,4},{14,6},{1,9},{3,11}... | collective-permute-start | bytes 196616 | tf_op jit(solution)/shard_map/ppermute | solution.py:216
  41.9 4.3 %collective-permute-start.19 = (bf16[2,128,128]{2,1,0:T(8,128)(2,1)S(1)}, bf16[2,128,128]{2,1,0:T(8,128)(2,1)S(1)}, u32[]{:S(2)}, u32[]{:S(2)}) collective-permute-start(bf16[2,128,128]{2,1,0:T(8,128)(2,1)S(1)} %get-tuple-element.206), channel_id=1, source_target_pairs={{0,4},{2,6},{4,0},{6,2},{8,12},{10,14},{12,8},{14,10},{1,5},{3,7},... | collective-permute-start | bytes 196616 | tf_op jit(solution)/shard_map/ppermute | solution.py:216
  43.4 6.0 %collective-permute-start.17 = (bf16[2,128,128]{2,1,0:T(8,128)(2,1)S(1)}, bf16[2,128,128]{2,1,0:T(8,128)(2,1)S(1)}, u32[]{:S(2)}, u32[]{:S(2)}) collective-permute-start(bf16[2,128,128]{2,1,0:T(8,128)(2,1)S(1)} %get-tuple-element.207), channel_id=1, source_target_pairs={{0,6},{2,4},{4,2},{6,0},{8,14},{10,12},{12,10},{14,8},{1,7},{3,5},... | collective-permute-start | bytes 196616 | tf_op jit(solution)/shard_map/ppermute | solution.py:216
  45.2 4.3 %collective-permute-start.18 = (bf16[2,128,128]{2,1,0:T(8,128)(2,1)S(1)}, bf16[2,128,128]{2,1,0:T(8,128)(2,1)S(1)}, u32[]{:S(2)}, u32[]{:S(2)}) collective-permute-start(bf16[2,128,128]{2,1,0:T(8,128)(2,1)S(1)} %get-tuple-element.208), channel_id=1, source_target_pairs={{0,2},{2,0},{4,6},{6,4},{8,10},{10,8},{12,14},{14,12},{1,3},{3,1},... | collective-permute-start | bytes 196616 | tf_op jit(solution)/shard_map/ppermute | solution.py:216
  49.6 1.4 %collective-permute-start.21 = (bf16[4,128,128]{2,1,0:T(8,128)(2,1)S(1)}, bf16[4,128,128]{2,1,0:T(8,128)(2,1)S(1)}, u32[]{:S(2)}, u32[]{:S(2)}) collective-permute-start(bf16[4,128,128]{2,1,0:T(8,128)(2,1)S(1)} %pad_maximum_fusion.5), channel_id=1, source_target_pairs={{0,1},{1,0},{2,3},{3,2},{4,5},{5,4},{6,7},{7,6},{8,9},{9,8},{10,11... | collective-permute-start | bytes 393224 | tf_op jit(solution)/shard_map/ppermute | solution.py:216
  49.7 1.5 %collective-permute-start.20 = (bf16[4,128,128]{2,1,0:T(8,128)(2,1)S(1)}, bf16[4,128,128]{2,1,0:T(8,128)(2,1)S(1)}, u32[]{:S(2)}, u32[]{:S(2)}) collective-permute-start(bf16[4,128,128]{2,1,0:T(8,128)(2,1)S(1)} %pad_maximum_fusion.4), channel_id=1, source_target_pairs={{0,1},{1,0},{2,3},{3,2},{4,5},{5,4},{6,7},{7,6},{8,9},{9,8},{10,11... | collective-permute-start | bytes 393224 | tf_op jit(solution)/shard_map/ppermute | solution.py:216

commit v6 on v5

--- a/solution.py
+++ b/solution.py
@@ -16,6 +16,7 @@
 NT = (((1,), (1,)), ((), ()))
 TN = (((0,), (0,)), ((), ()))
 AXES = ("seq", "head", "sub")
+BACK = (1, 0)
 
 
 def dot(left, right, form):
@@ -272,17 +273,17 @@
     for group in order:
         message = carried + before(pair[0], others, plan.mask(group), bits, reverse)
         sums[group] = swap(message.astype(BF), chips, plan.mask(group)).astype(F32)
-    near, far, message = [], [], None
-    for part in members:
+    near, far, message = [None, None], [None, None], None
+    for part in BACK:
         if message is not None:
-            for group in part:
+            for group in members[part]:
                 sums[group], message = lax.optimization_barrier((sums[group], message))
-            far.append(swap(message, "sub", 1))
-        message = [sums[group] + gated(own[group], bits, 0, lower) for group in part]
-        known = [sums[group] + gated(near_got[group], bits, 0, upper) for group in part]
+            far[1 - part] = swap(message, "sub", 1)
+        message = [sums[group] + gated(own[group], bits, 0, lower) for group in members[part]]
+        known = [sums[group] + gated(near_got[group], bits, 0, upper) for group in members[part]]
         message = jnp.concatenate(message).astype(BF)
-        near.append(jnp.concatenate(known).astype(BF))
-    far.append(swap(message, "sub", 1))
+        near[part] = jnp.concatenate(known).astype(BF)
+    far[BACK[1]] = swap(message, "sub", 1)
     return near, far, given
 
 
@@ -326,13 +327,14 @@
             [vm(part_state, BF), vm(part_state, BF), vm(part_state, BF if is_far else F32)], unit,
         )
 
-    normed = [[None, None], []]
-    normed[0][0] = norm(0, 0, near[0])
-    far[0], normed[0][0] = lax.optimization_barrier((far[0], normed[0][0]))
-    for part in range(2):
-        normed[1].append(norm(part, 1, far[part]))
-    near[1], normed[1] = lax.optimization_barrier((near[1], normed[1]))
-    normed[0][1] = norm(1, 0, near[1])
+    normed = [[None, None], [None, None]]
+    early, late = BACK
+    normed[0][early] = norm(early, 0, near[early])
+    far[early], normed[0][early] = lax.optimization_barrier((far[early], normed[0][early]))
+    for part in BACK:
+        normed[1][part] = norm(part, 1, far[part])
+    near[late], normed[1] = lax.optimization_barrier((near[late], normed[1]))
+    normed[0][late] = norm(late, 0, near[late])
     partials = ()
 
     def local_grads(is_far, operands):

time: 52.6 us -> 52.2 us (level)
  starting transfers between devices: 23.6 us -> 22.4 us
  waiting for transfers between devices: 14.8 us -> 15.5 us
    ppermute x22, starting transfers between devices: 23.6 us -> 22.4 us  [swap(): return lax.ppermute(value, axes, pairs)]
    ppermute x22, waiting for transfers between devices: 14.8 us -> 15.5 us  [swap(): return lax.ppermute(value, axes, pairs)]
  transfers between devices with their start and end apart: 22 -> 22, of which waited for: 16 -> 18; matrix products, arithmetic and copies ran while one was open for 1% -> 1% of each run, Pallas kernels for 17% -> 17%
where the time goes in v6:
time: 52.2 us; the launch traced here: 52 us
  starting transfers between devices  22.4 us (43%)
  waiting for transfers between devices  15.5 us (30%)
  Pallas kernels  12.3 us (24%)
  other arithmetic  0.88 us (2%)
  between operations  0.88 us (2%)
    ppermute x22, starting transfers between devices, swap(): return lax.ppermute(value, axes, pairs)  22.4 us
    ppermute x22, waiting for transfers between devices, swap(): return lax.ppermute(value, axes, pairs)  15.5 us
    pallas_call x11, Pallas kernels, call(): pl.pallas_call(body, out_shape=outs, in_specs=in_specs, out_specs=[anywhe...  12.3 us
  transfers between devices with their start and end apart: 22, of which 18 were waited for; matrix products, arithmetic and copies ran while one was open for 1% of the time, Pallas kernels for 17%

profile of v6, /device:TPU:0, one launch (start us, length us, event | category | flops | bytes accessed | tf_op | source)
XLA Modules:
  0.0 52.0 jit_solution(15524109054269706238)
XLA Ops:
  0.6 1.7 %shard_map.75 = (bf16[4,128,128]{2,1,0:T(8,128)(2,1)S(1)}, bf16[4,128,128]{2,1,0:T(8,128)(2,1)S(1)}, f32[4,128,128]{2,1,0:T(8,128)S(1)}, f32[4,128,128]{2,1,0:T(...) custom-call(bf16[128,2048]{1,0:T(8,128)(2,1)} %k_ref.1, ...), custom_call_target="tpu_custom_call" | custom-call | flops 67108864 | bytes 2097152 | tf_op jit(solution)/shard_map/pallas_call | solution.py:203
  3.0 0.9 %collective-permute-done = bf16[4,128,128]{2,1,0:T(8,128)(2,1)S(1)} collective-permute-done((bf16[4,128,128]{2,1,0:T(8,128)(2,1)S(1)}, bf16[4,128,128]{2,1,0:T(8,128)(2,1)S(1)}, u32[]{:S(2)}, u32[]{:S(2)}) %collective-permute-start) | collective-permute-done | bytes 131104 | tf_op jit(solution)/shard_map/ppermute | solution.py:217
  3.9 3.9 %collective-permute-start.1 = (bf16[2,128,128]{2,1,0:T(8,128)(2,1)S(1)}, bf16[2,128,128]{2,1,0:T(8,128)(2,1)S(1)}, u32[]{:S(2)}, u32[]{:S(2)}) collective-permute-start(bf16[2,128,128]{2,1,0:T(8,128)(2,1)S(1)} %get-tuple-element.109), channel_id=1, source_target_pairs={{0,6},{2,4},{4,2},{6,0},{8,14},{10,12},{12,10},{14,8},{1,7},{3,5},... | collective-permute-start | bytes 196616 | tf_op jit(solution)/shard_map/ppermute | solution.py:217
  8.6 1.4 %shard_map.76 = (bf16[8,128,128]{2,1,0:T(8,128)(2,1)S(1)}, f32[8,128,128]{2,1,0:T(8,128)S(1)}) custom-call(bf16[128,2048]{1,0:T(8,128)(2,1)S(1)} %copy-done, bf16[128,2048]{1,0:T(8,128)(2,1)S(1)} %get-tuple-element.173.k_ref, bf16[128,2048]{1,0:T(8,128)(2,1)S(1)} %get-tuple-element.174.v_ref, bf16[128,2048]{1,0:T(8,128)(2,1)S(1)} %copy-done.1), custom_call_target="tpu_custom_call" | custom-call | flops 67108864 | bytes 4194304 | tf_op jit(solution)/shard_map/pallas_call | solution.py:203
  10.3 1.9 %collective-permute-done.4 = bf16[2,128,128]{2,1,0:T(8,128)(2,1)S(1)} collective-permute-done((bf16[2,128,128]{2,1,0:T(8,128)(2,1)S(1)}, bf16[2,128,128]{2,1,0:T(8,128)(2,1)S(1)}, u32[]{:S(2)}, u32[]{:S(2)}) %collective-permute-start.4) | collective-permute-done | bytes 65568 | tf_op jit(solution)/shard_map/ppermute | solution.py:217
  12.8 2.7 %collective-permute-start.5 = (bf16[2,128,128]{2,1,0:T(8,128)(2,1)S(1)}, bf16[2,128,128]{2,1,0:T(8,128)(2,1)S(1)}, u32[]{:S(2)}, u32[]{:S(2)}) collective-permute-start(bf16[2,128,128]{2,1,0:T(8,128)(2,1)S(1)} %fusion.51), channel_id=1, source_target_pairs={{0,8},{2,10},{4,12},{6,14},{8,0},{10,2},{12,4},{14,6},{1,9},{3,11}... | collective-permute-start | bytes 196616 | tf_op jit(solution)/shard_map/ppermute | solution.py:217
  15.5 1.4 %shard_map.77 = (bf16[8,128,128]{2,1,0:T(8,128)(2,1)S(1)}, f32[8,128,128]{2,1,0:T(8,128)S(1)}) custom-call(bf16[128,2048]{1,0:T(8,128)(2,1)S(1)} %copy-done, bf16[128,2048]{1,0:T(8,128)(2,1)S(1)} %get-tuple-element.173.k_ref, bf16[128,2048]{1,0:T(8,128)(2,1)S(1)} %get-tuple-element.174.v_ref), custom_call_target="tpu_custom_call" | custom-call | flops 67108864 | bytes 3145728 | tf_op jit(solution)/shard_map/pallas_call | solution.py:203
  16.8 1.9 %collective-permute-done.5 = bf16[2,128,128]{2,1,0:T(8,128)(2,1)S(1)} collective-permute-done((bf16[2,128,128]{2,1,0:T(8,128)(2,1)S(1)}, bf16[2,128,128]{2,1,0:T(8,128)(2,1)S(1)}, u32[]{:S(2)}, u32[]{:S(2)}) %collective-permute-start.5) | collective-permute-done | bytes 65568 | tf_op jit(solution)/shard_map/ppermute | solution.py:217
  18.9 1.4 %collective-permute-start.6 = (bf16[2,128,128]{2,1,0:T(8,128)(2,1)S(1)}, bf16[2,128,128]{2,1,0:T(8,128)(2,1)S(1)}, u32[]{:S(2)}, u32[]{:S(2)}) collective-permute-start(bf16[2,128,128]{2,1,0:T(8,128)(2,1)S(1)} %get-tuple-element.209), channel_id=1, source_target_pairs={{0,2},{2,0},{4,6},{6,4},{8,10},{10,8},{12,14},{14,12},{1,3},{3,1},... | collective-permute-start | bytes 196616 | tf_op jit(solution)/shard_map/ppermute | solution.py:217
  20.4 2.0 %collective-permute-start.8 = (bf16[2,128,128]{2,1,0:T(8,128)(2,1)S(1)}, bf16[2,128,128]{2,1,0:T(8,128)(2,1)S(1)}, u32[]{:S(2)}, u32[]{:S(2)}) collective-permute-start(bf16[2,128,128]{2,1,0:T(8,128)(2,1)S(1)} %get-tuple-element.211), channel_id=1, source_target_pairs={{0,4},{2,6},{4,0},{6,2},{8,12},{10,14},{12,8},{14,10},{1,5},{3,7},... | collective-permute-start | bytes 196616 | tf_op jit(solution)/shard_map/ppermute | solution.py:217
  22.4 0.8 %collective-permute-done.6 = bf16[2,128,128]{2,1,0:T(8,128)(2,1)S(1)} collective-permute-done((bf16[2,128,128]{2,1,0:T(8,128)(2,1)S(1)}, bf16[2,128,128]{2,1,0:T(8,128)(2,1)S(1)}, u32[]{:S(2)}, u32[]{:S(2)}) %collective-permute-start.6) | collective-permute-done | bytes 65568 | tf_op jit(solution)/shard_map/ppermute | solution.py:217
  23.2 2.3 %collective-permute-done.7 = bf16[2,128,128]{2,1,0:T(8,128)(2,1)S(1)} collective-permute-done((bf16[2,128,128]{2,1,0:T(8,128)(2,1)S(1)}, bf16[2,128,128]{2,1,0:T(8,128)(2,1)S(1)}, u32[]{:S(2)}, u32[]{:S(2)}) %collective-permute-start.7) | collective-permute-done | bytes 65568 | tf_op jit(solution)/shard_map/ppermute | solution.py:217
  29.6 2.0 %collective-permute-start.15 = (bf16[2,128,128]{2,1,0:T(8,128)(2,1)S(1)}, bf16[2,128,128]{2,1,0:T(8,128)(2,1)S(1)}, u32[]{:S(2)}, u32[]{:S(2)}) collective-permute-start(bf16[2,128,128]{2,1,0:T(8,128)(2,1)S(1)} %get-tuple-element.153), channel_id=1, source_target_pairs={{0,6},{2,4},{4,2},{6,0},{8,14},{10,12},{12,10},{14,8},{1,7},{3,5},... | collective-permute-start | bytes 196616 | tf_op jit(solution)/shard_map/ppermute | solution.py:217
  31.5 0.8 %collective-permute-start.12 = (bf16[2,128,128]{2,1,0:T(8,128)(2,1)S(1)}, bf16[2,128,128]{2,1,0:T(8,128)(2,1)S(1)}, u32[]{:S(2)}, u32[]{:S(2)}) collective-permute-start(bf16[2,128,128]{2,1,0:T(8,128)(2,1)S(1)} %fusion.41), channel_id=1, source_target_pairs={{0,4},{2,6},{4,0},{6,2},{8,12},{10,14},{12,8},{14,10},{1,5},{3,7},... | collective-permute-start | bytes 196616 | tf_op jit(solution)/shard_map/ppermute | solution.py:217
  32.3 0.9 %collective-permute-start.14 = (bf16[2,128,128]{2,1,0:T(8,128)(2,1)S(1)}, bf16[2,128,128]{2,1,0:T(8,128)(2,1)S(1)}, u32[]{:S(2)}, u32[]{:S(2)}) collective-permute-start(bf16[2,128,128]{2,1,0:T(8,128)(2,1)S(1)} %get-tuple-element.212), channel_id=1, source_target_pairs={{0,2},{2,0},{4,6},{6,4},{8,10},{10,8},{12,14},{14,12},{1,3},{3,1},... | collective-permute-start | bytes 196616 | tf_op jit(solution)/shard_map/ppermute | solution.py:217
  33.2 2.1 %shard_map.82 = (f32[8,128,128]{2,1,0:T(8,128)S(1)}, f32[8,128,128]{2,1,0:T(8,128)S(1)}, bf16[128,2048]{1,0:T(8,128)(2,1)}, bf16[128,2048]{1,0:T(8,128)(2,1)}) custom-call(bf16[128,2048]{1,0:T(8,128)(2,1)S(1)} %copy-done, bf16[128,2048]{1,0:T(8,128)(2,1)S(1)} %get-tuple-element.173.k_ref, bf16[128,2048]{1,0:T(8,128)(2,1)S(1)} %get-tuple-element.174.v_ref, ...), custom_call_target="tpu_custom_call" | custom-call | flops 167772160 | bytes 5242880 | tf_op jit(solution)/shard_map/pallas_call | solution.py:203
  36.6 2.1 %collective-permute-start.16 = (bf16[2,128,128]{2,1,0:T(8,128)(2,1)S(1)}, bf16[2,128,128]{2,1,0:T(8,128)(2,1)S(1)}, u32[]{:S(2)}, u32[]{:S(2)}) collective-permute-start(bf16[2,128,128]{2,1,0:T(8,128)(2,1)S(1)} %fusion.53), channel_id=1, source_target_pairs={{0,8},{2,10},{4,12},{6,14},{8,0},{10,2},{12,4},{14,6},{1,9},{3,11}... | collective-permute-start | bytes 196616 | tf_op jit(solution)/shard_map/ppermute | solution.py:217
  38.7 2.1 %shard_map.83 = (f32[8,128,128]{2,1,0:T(8,128)S(1)}, f32[8,128,128]{2,1,0:T(8,128)S(1)}, bf16[128,2048]{1,0:T(8,128)(2,1)}, bf16[128,2048]{1,0:T(8,128)(2,1)}) custom-call(bf16[128,2048]{1,0:T(8,128)(2,1)S(1)} %copy-done, bf16[128,2048]{1,0:T(8,128)(2,1)S(1)} %get-tuple-element.173.k_ref, ...), custom_call_target="tpu_custom_call", output_to_operand_aliasing={{2}: (10, {}), {3}: (11, {})} | custom-call | flops 167772160 | bytes 5242880 | tf_op jit(solution)/shard_map/pallas_call | solution.py:203
  40.8 1.1 %collective-permute-done.16 = bf16[2,128,128]{2,1,0:T(8,128)(2,1)S(1)} collective-permute-done((bf16[2,128,128]{2,1,0:T(8,128)(2,1)S(1)}, bf16[2,128,128]{2,1,0:T(8,128)(2,1)S(1)}, u32[]{:S(2)}, u32[]{:S(2)}) %collective-permute-start.16) | collective-permute-done | bytes 65568 | tf_op jit(solution)/shard_map/ppermute | solution.py:217
  42.0 1.7 %collective-permute-start.17 = (bf16[2,128,128]{2,1,0:T(8,128)(2,1)S(1)}, bf16[2,128,128]{2,1,0:T(8,128)(2,1)S(1)}, u32[]{:S(2)}, u32[]{:S(2)}) collective-permute-start(bf16[2,128,128]{2,1,0:T(8,128)(2,1)S(1)} %get-tuple-element.206), channel_id=1, source_target_pairs={{0,2},{2,0},{4,6},{6,4},{8,10},{10,8},{12,14},{14,12},{1,3},{3,1},... | collective-permute-start | bytes 196616 | tf_op jit(solution)/shard_map/ppermute | solution.py:217
  43.6 1.2 %collective-permute-start.18 = (bf16[2,128,128]{2,1,0:T(8,128)(2,1)S(1)}, bf16[2,128,128]{2,1,0:T(8,128)(2,1)S(1)}, u32[]{:S(2)}, u32[]{:S(2)}) collective-permute-start(bf16[2,128,128]{2,1,0:T(8,128)(2,1)S(1)} %get-tuple-element.207), channel_id=1, source_target_pairs={{0,6},{2,4},{4,2},{6,0},{8,14},{10,12},{12,10},{14,8},{1,7},{3,5},... | collective-permute-start | bytes 196616 | tf_op jit(solution)/shard_map/ppermute | solution.py:217
  45.5 0.8 %collective-permute-done.17 = bf16[2,128,128]{2,1,0:T(8,128)(2,1)S(1)} collective-permute-done((bf16[2,128,128]{2,1,0:T(8,128)(2,1)S(1)}, bf16[2,128,128]{2,1,0:T(8,128)(2,1)S(1)}, u32[]{:S(2)}, u32[]{:S(2)}) %collective-permute-start.17) | collective-permute-done | bytes 65568 | tf_op jit(solution)/shard_map/ppermute | solution.py:217
  46.3 2.5 %collective-permute-done.18 = bf16[2,128,128]{2,1,0:T(8,128)(2,1)S(1)} collective-permute-done((bf16[2,128,128]{2,1,0:T(8,128)(2,1)S(1)}, bf16[2,128,128]{2,1,0:T(8,128)(2,1)S(1)}, u32[]{:S(2)}, u32[]{:S(2)}) %collective-permute-start.18) | collective-permute-done | bytes 65568 | tf_op jit(solution)/shard_map/ppermute | solution.py:217
  50.8 1.2 %shard_map.85 = (bf16[128,2048]{1,0:T(8,128)(2,1)}, bf16[128,2048]{1,0:T(8,128)(2,1)}) custom-call(bf16[128,2048]{1,0:T(8,128)(2,1)S(1)} %get-tuple-element.173.k_ref, bf16[128,2048]{1,0:T(8,128)(2,1)S(1)} %get-tuple-element.174.v_ref, f32[8,128,128]{2,1,0:T(8,128)S(1)} %get-tuple-element.189.gk_ref, f32[8,128,128]{2,1,0:T(8,128)S(1)} %get-tuple-element.190.gv_ref, ...), custom_call_target="tpu_custom_call" | custom-call | flops 67108864 | bytes 5767168 | tf_op jit(solution)/shard_map/pallas_call | solution.py:203
  (57 shorter events, 10.8 us)
Async XLA Ops:
  0.6 8.0 %copy-start.1 = (bf16[128,2048]{1,0:T(8,128)(2,1)S(1)}, bf16[128,2048]{1,0:T(8,128)(2,1)}, u32[]{:S(2)}) copy-start(bf16[128,2048]{1,0:T(8,128)(2,1)} %g_ref.7) | copy-start | bytes 1572868
  2.4 6.2 %copy-start = (bf16[128,2048]{1,0:T(8,128)(2,1)S(1)}, bf16[128,2048]{1,0:T(8,128)(2,1)}, u32[]{:S(2)}) copy-start(bf16[128,2048]{1,0:T(8,128)(2,1)} %q_ref.11) | copy-start | bytes 1572868
  2.4 1.5 %collective-permute-start = (bf16[4,128,128]{2,1,0:T(8,128)(2,1)S(1)}, bf16[4,128,128]{2,1,0:T(8,128)(2,1)S(1)}, u32[]{:S(2)}, u32[]{:S(2)}) collective-permute-start(bf16[4,128,128]{2,1,0:T(8,128)(2,1)S(1)} %get-tuple-element.106), channel_id=1, source_target_pairs={{0,1},{1,0},{2,3},{3,2},{4,5},{5,4},{6,7},{7,6},{8,9},{9,8},{10,11... | collective-permute-start | bytes 393224 | tf_op jit(solution)/shard_map/ppermute | solution.py:217
  2.9 5.5 %collective-permute-start.2 = (bf16[4,128,128]{2,1,0:T(8,128)(2,1)S(1)}, bf16[4,128,128]{2,1,0:T(8,128)(2,1)S(1)}, u32[]{:S(2)}, u32[]{:S(2)}) collective-permute-start(bf16[4,128,128]{2,1,0:T(8,128)(2,1)S(1)} %get-tuple-element.119), channel_id=1, source_target_pairs={{0,1},{1,0},{2,3},{3,2},{4,5},{5,4},{6,7},{7,6},{8,9},{9,8},{10,11... | collective-permute-start | bytes 393224 | tf_op jit(solution)/shard_map/ppermute | solution.py:217
  3.9 6.3 %collective-permute-start.1 = (bf16[2,128,128]{2,1,0:T(8,128)(2,1)S(1)}, bf16[2,128,128]{2,1,0:T(8,128)(2,1)S(1)}, u32[]{:S(2)}, u32[]{:S(2)}) collective-permute-start(bf16[2,128,128]{2,1,0:T(8,128)(2,1)S(1)} %get-tuple-element.109), channel_id=1, source_target_pairs={{0,6},{2,4},{4,2},{6,0},{8,14},{10,12},{12,10},{14,8},{1,7},{3,5},... | collective-permute-start | bytes 196616 | tf_op jit(solution)/shard_map/ppermute | solution.py:217
  7.9 4.3 %collective-permute-start.4 = (bf16[2,128,128]{2,1,0:T(8,128)(2,1)S(1)}, bf16[2,128,128]{2,1,0:T(8,128)(2,1)S(1)}, u32[]{:S(2)}, u32[]{:S(2)}) collective-permute-start(bf16[2,128,128]{2,1,0:T(8,128)(2,1)S(1)} %get-tuple-element.215), channel_id=1, source_target_pairs={{0,2},{2,0},{4,6},{6,4},{8,10},{10,8},{12,14},{14,12},{1,3},{3,1},... | collective-permute-start | bytes 196616 | tf_op jit(solution)/shard_map/ppermute | solution.py:217
  8.4 4.3 %collective-permute-start.3 = (bf16[2,128,128]{2,1,0:T(8,128)(2,1)S(1)}, bf16[2,128,128]{2,1,0:T(8,128)(2,1)S(1)}, u32[]{:S(2)}, u32[]{:S(2)}) collective-permute-start(bf16[2,128,128]{2,1,0:T(8,128)(2,1)S(1)} %fusion.31), channel_id=1, source_target_pairs={{0,4},{2,6},{4,0},{6,2},{8,12},{10,14},{12,8},{14,10},{1,5},{3,7},... | collective-permute-start | bytes 196616 | tf_op jit(solution)/shard_map/ppermute | solution.py:217
  12.8 5.9 %collective-permute-start.5 = (bf16[2,128,128]{2,1,0:T(8,128)(2,1)S(1)}, bf16[2,128,128]{2,1,0:T(8,128)(2,1)S(1)}, u32[]{:S(2)}, u32[]{:S(2)}) collective-permute-start(bf16[2,128,128]{2,1,0:T(8,128)(2,1)S(1)} %fusion.51), channel_id=1, source_target_pairs={{0,8},{2,10},{4,12},{6,14},{8,0},{10,2},{12,4},{14,6},{1,9},{3,11}... | collective-permute-start | bytes 196616 | tf_op jit(solution)/shard_map/ppermute | solution.py:217
  18.9 4.3 %collective-permute-start.6 = (bf16[2,128,128]{2,1,0:T(8,128)(2,1)S(1)}, bf16[2,128,128]{2,1,0:T(8,128)(2,1)S(1)}, u32[]{:S(2)}, u32[]{:S(2)}) collective-permute-start(bf16[2,128,128]{2,1,0:T(8,128)(2,1)S(1)} %get-tuple-element.209), channel_id=1, source_target_pairs={{0,2},{2,0},{4,6},{6,4},{8,10},{10,8},{12,14},{14,12},{1,3},{3,1},... | collective-permute-start | bytes 196616 | tf_op jit(solution)/shard_map/ppermute | solution.py:217
  20.3 5.2 %collective-permute-start.7 = (bf16[2,128,128]{2,1,0:T(8,128)(2,1)S(1)}, bf16[2,128,128]{2,1,0:T(8,128)(2,1)S(1)}, u32[]{:S(2)}, u32[]{:S(2)}) collective-permute-start(bf16[2,128,128]{2,1,0:T(8,128)(2,1)S(1)} %get-tuple-element.210), channel_id=1, source_target_pairs={{0,6},{2,4},{4,2},{6,0},{8,14},{10,12},{12,10},{14,8},{1,7},{3,5},... | collective-permute-start | bytes 196616 | tf_op jit(solution)/shard_map/ppermute | solution.py:217
  20.4 5.1 %collective-permute-start.8 = (bf16[2,128,128]{2,1,0:T(8,128)(2,1)S(1)}, bf16[2,128,128]{2,1,0:T(8,128)(2,1)S(1)}, u32[]{:S(2)}, u32[]{:S(2)}) collective-permute-start(bf16[2,128,128]{2,1,0:T(8,128)(2,1)S(1)} %get-tuple-element.211), channel_id=1, source_target_pairs={{0,4},{2,6},{4,0},{6,2},{8,12},{10,14},{12,8},{14,10},{1,5},{3,7},... | collective-permute-start | bytes 196616 | tf_op jit(solution)/shard_map/ppermute | solution.py:217
  25.6 1.4 %collective-permute-start.10 = (bf16[4,128,128]{2,1,0:T(8,128)(2,1)S(1)}, bf16[4,128,128]{2,1,0:T(8,128)(2,1)S(1)}, u32[]{:S(2)}, u32[]{:S(2)}) collective-permute-start(bf16[4,128,128]{2,1,0:T(8,128)(2,1)S(1)} %get-tuple-element.135), channel_id=1, source_target_pairs={{0,1},{1,0},{2,3},{3,2},{4,5},{5,4},{6,7},{7,6},{8,9},{9,8},{10,11... | collective-permute-start | bytes 393224 | tf_op jit(solution)/shard_map/ppermute | solution.py:217
  25.8 1.8 %collective-permute-start.9 = (bf16[4,128,128]{2,1,0:T(8,128)(2,1)S(1)}, bf16[4,128,128]{2,1,0:T(8,128)(2,1)S(1)}, u32[]{:S(2)}, u32[]{:S(2)}) collective-permute-start(bf16[4,128,128]{2,1,0:T(8,128)(2,1)S(1)} %pad_maximum_fusion.2), channel_id=1, source_target_pairs={{0,1},{1,0},{2,3},{3,2},{4,5},{5,4},{6,7},{7,6},{8,9},{9,8},{10,11... | collective-permute-start | bytes 393224 | tf_op jit(solution)/shard_map/ppermute | solution.py:217
  28.1 1.4 %collective-permute-start.13 = (bf16[4,128,128]{2,1,0:T(8,128)(2,1)S(1)}, bf16[4,128,128]{2,1,0:T(8,128)(2,1)S(1)}, u32[]{:S(2)}, u32[]{:S(2)}) collective-permute-start(bf16[4,128,128]{2,1,0:T(8,128)(2,1)S(1)} %get-tuple-element.147), channel_id=1, source_target_pairs={{0,1},{1,0},{2,3},{3,2},{4,5},{5,4},{6,7},{7,6},{8,9},{9,8},{10,11... | collective-permute-start | bytes 393224 | tf_op jit(solution)/shard_map/ppermute | solution.py:217
  28.3 3.2 %collective-permute-start.11 = (bf16[4,128,128]{2,1,0:T(8,128)(2,1)S(1)}, bf16[4,128,128]{2,1,0:T(8,128)(2,1)S(1)}, u32[]{:S(2)}, u32[]{:S(2)}) collective-permute-start(bf16[4,128,128]{2,1,0:T(8,128)(2,1)S(1)} %get-tuple-element.145), channel_id=1, source_target_pairs={{0,1},{1,0},{2,3},{3,2},{4,5},{5,4},{6,7},{7,6},{8,9},{9,8},{10,11... | collective-permute-start | bytes 393224 | tf_op jit(solution)/shard_map/ppermute | solution.py:217
  29.6 5.9 %collective-permute-start.15 = (bf16[2,128,128]{2,1,0:T(8,128)(2,1)S(1)}, bf16[2,128,128]{2,1,0:T(8,128)(2,1)S(1)}, u32[]{:S(2)}, u32[]{:S(2)}) collective-permute-start(bf16[2,128,128]{2,1,0:T(8,128)(2,1)S(1)} %get-tuple-element.153), channel_id=1, source_target_pairs={{0,6},{2,4},{4,2},{6,0},{8,14},{10,12},{12,10},{14,8},{1,7},{3,5},... | collective-permute-start | bytes 196616 | tf_op jit(solution)/shard_map/ppermute | solution.py:217
  31.5 4.3 %collective-permute-start.12 = (bf16[2,128,128]{2,1,0:T(8,128)(2,1)S(1)}, bf16[2,128,128]{2,1,0:T(8,128)(2,1)S(1)}, u32[]{:S(2)}, u32[]{:S(2)}) collective-permute-start(bf16[2,128,128]{2,1,0:T(8,128)(2,1)S(1)} %fusion.41), channel_id=1, source_target_pairs={{0,4},{2,6},{4,0},{6,2},{8,12},{10,14},{12,8},{14,10},{1,5},{3,7},... | collective-permute-start | bytes 196616 | tf_op jit(solution)/shard_map/ppermute | solution.py:217
  32.3 4.3 %collective-permute-start.14 = (bf16[2,128,128]{2,1,0:T(8,128)(2,1)S(1)}, bf16[2,128,128]{2,1,0:T(8,128)(2,1)S(1)}, u32[]{:S(2)}, u32[]{:S(2)}) collective-permute-start(bf16[2,128,128]{2,1,0:T(8,128)(2,1)S(1)} %get-tuple-element.212), channel_id=1, source_target_pairs={{0,2},{2,0},{4,6},{6,4},{8,10},{10,8},{12,14},{14,12},{1,3},{3,1},... | collective-permute-start | bytes 196616 | tf_op jit(solution)/shard_map/ppermute | solution.py:217
  36.6 5.2 %collective-permute-start.16 = (bf16[2,128,128]{2,1,0:T(8,128)(2,1)S(1)}, bf16[2,128,128]{2,1,0:T(8,128)(2,1)S(1)}, u32[]{:S(2)}, u32[]{:S(2)}) collective-permute-start(bf16[2,128,128]{2,1,0:T(8,128)(2,1)S(1)} %fusion.53), channel_id=1, source_target_pairs={{0,8},{2,10},{4,12},{6,14},{8,0},{10,2},{12,4},{14,6},{1,9},{3,11}... | collective-permute-start | bytes 196616 | tf_op jit(solution)/shard_map/ppermute | solution.py:217
  42.0 4.3 %collective-permute-start.17 = (bf16[2,128,128]{2,1,0:T(8,128)(2,1)S(1)}, bf16[2,128,128]{2,1,0:T(8,128)(2,1)S(1)}, u32[]{:S(2)}, u32[]{:S(2)}) collective-permute-start(bf16[2,128,128]{2,1,0:T(8,128)(2,1)S(1)} %get-tuple-element.206), channel_id=1, source_target_pairs={{0,2},{2,0},{4,6},{6,4},{8,10},{10,8},{12,14},{14,12},{1,3},{3,1},... | collective-permute-start | bytes 196616 | tf_op jit(solution)/shard_map/ppermute | solution.py:217
  43.6 5.2 %collective-permute-start.18 = (bf16[2,128,128]{2,1,0:T(8,128)(2,1)S(1)}, bf16[2,128,128]{2,1,0:T(8,128)(2,1)S(1)}, u32[]{:S(2)}, u32[]{:S(2)}) collective-permute-start(bf16[2,128,128]{2,1,0:T(8,128)(2,1)S(1)} %get-tuple-element.207), channel_id=1, source_target_pairs={{0,6},{2,4},{4,2},{6,0},{8,14},{10,12},{12,10},{14,8},{1,7},{3,5},... | collective-permute-start | bytes 196616 | tf_op jit(solution)/shard_map/ppermute | solution.py:217
  44.8 4.3 %collective-permute-start.19 = (bf16[2,128,128]{2,1,0:T(8,128)(2,1)S(1)}, bf16[2,128,128]{2,1,0:T(8,128)(2,1)S(1)}, u32[]{:S(2)}, u32[]{:S(2)}) collective-permute-start(bf16[2,128,128]{2,1,0:T(8,128)(2,1)S(1)} %get-tuple-element.208), channel_id=1, source_target_pairs={{0,4},{2,6},{4,0},{6,2},{8,12},{10,14},{12,8},{14,10},{1,5},{3,7},... | collective-permute-start | bytes 196616 | tf_op jit(solution)/shard_map/ppermute | solution.py:217
  49.2 1.4 %collective-permute-start.20 = (bf16[4,128,128]{2,1,0:T(8,128)(2,1)S(1)}, bf16[4,128,128]{2,1,0:T(8,128)(2,1)S(1)}, u32[]{:S(2)}, u32[]{:S(2)}) collective-permute-start(bf16[4,128,128]{2,1,0:T(8,128)(2,1)S(1)} %pad_maximum_fusion.5), channel_id=1, source_target_pairs={{0,1},{1,0},{2,3},{3,2},{4,5},{5,4},{6,7},{7,6},{8,9},{9,8},{10,11... | collective-permute-start | bytes 393224 | tf_op jit(solution)/shard_map/ppermute | solution.py:217
  49.3 1.5 %collective-permute-start.21 = (bf16[4,128,128]{2,1,0:T(8,128)(2,1)S(1)}, bf16[4,128,128]{2,1,0:T(8,128)(2,1)S(1)}, u32[]{:S(2)}, u32[]{:S(2)}) collective-permute-start(bf16[4,128,128]{2,1,0:T(8,128)(2,1)S(1)} %pad_maximum_fusion.4), channel_id=1, source_target_pairs={{0,1},{1,0},{2,3},{3,2},{4,5},{5,4},{6,7},{7,6},{8,9},{9,8},{10,11... | collective-permute-start | bytes 393224 | tf_op jit(solution)/shard_map/ppermute | solution.py:217

commit v7 on v6

--- a/solution.py
+++ b/solution.py
@@ -179,7 +179,8 @@
 
     for part in range(2):
         leave(part, 0, (gk_near, gv_near))
-    for part, state_ref in enumerate(states):
+    for part in range(2):
+        state_ref = states[0].at[pl.ds(part * plan.part, plan.part)]
         last_grads(plan, part, 1, k_ref, v_ref, gk_ref, gv_ref, state_ref, gk_buf, gv_buf)
         leave(part, 1, (gk_buf, gv_buf))
     for copy in copies:
@@ -278,11 +279,16 @@
         if message is not None:
             for group in members[part]:
                 sums[group], message = lax.optimization_barrier((sums[group], message))
-            far[1 - part] = swap(message, "sub", 1)
+            if not reverse:
+                far[1 - part] = swap(message, "sub", 1)
+            first = message
         message = [sums[group] + gated(own[group], bits, 0, lower) for group in members[part]]
         known = [sums[group] + gated(near_got[group], bits, 0, upper) for group in members[part]]
         message = jnp.concatenate(message).astype(BF)
         near[part] = jnp.concatenate(known).astype(BF)
+    if reverse:
+        both = swap(jnp.concatenate([message, first]), "sub", 1)
+        return near, [both], given
     far[BACK[1]] = swap(message, "sub", 1)
     return near, far, given
 

time: 52.2 us -> 52.2 us (level)
    ppermute x22 -> x21, starting transfers between devices: 22.4 us -> 21.9 us  [swap(): return lax.ppermute(value, axes, pairs)]
    ppermute x22 -> x21, waiting for transfers between devices: 15.5 us -> 16 us  [swap(): return lax.ppermute(value, axes, pairs)]
  transfers between devices with their start and end apart: 22 -> 21, of which waited for: 18 -> 17; matrix products, arithmetic and copies ran while one was open for 1% -> 1% of each run, Pallas kernels for 17% -> 17%
where the time goes in v7:
time: 52.2 us; the launch traced here: 52.1 us
  starting transfers between devices  21.9 us (42%)
  waiting for transfers between devices  16 us (31%)
  Pallas kernels  12.3 us (24%)
  other arithmetic  0.9 us (2%)
  between operations  0.88 us (2%)
    ppermute x21, starting transfers between devices, swap(): return lax.ppermute(value, axes, pairs)  21.9 us
    ppermute x21, waiting for transfers between devices, swap(): return lax.ppermute(value, axes, pairs)  16 us
    pallas_call x11, Pallas kernels, call(): pl.pallas_call(body, out_shape=outs, in_specs=in_specs, out_specs=[anywhe...  12.3 us
  transfers between devices with their start and end apart: 21, of which 17 were waited for; matrix products, arithmetic and copies ran while one was open for 1% of the time, Pallas kernels for 17%

profile of v7, /device:TPU:0, one launch (start us, length us, event | category | flops | bytes accessed | tf_op | source)
XLA Modules:
  0.0 52.1 jit_solution(2598863584363615503)
XLA Ops:
  0.6 1.7 %shard_map.75 = (bf16[4,128,128]{2,1,0:T(8,128)(2,1)S(1)}, bf16[4,128,128]{2,1,0:T(8,128)(2,1)S(1)}, f32[4,128,128]{2,1,0:T(8,128)S(1)}, f32[4,128,128]{2,1,0:T(...) custom-call(bf16[128,2048]{1,0:T(8,128)(2,1)} %k_ref.1, ...), custom_call_target="tpu_custom_call" | custom-call | flops 67108864 | bytes 2097152 | tf_op jit(solution)/shard_map/pallas_call | solution.py:204
  3.0 0.9 %collective-permute-done = bf16[4,128,128]{2,1,0:T(8,128)(2,1)S(1)} collective-permute-done((bf16[4,128,128]{2,1,0:T(8,128)(2,1)S(1)}, bf16[4,128,128]{2,1,0:T(8,128)(2,1)S(1)}, u32[]{:S(2)}, u32[]{:S(2)}) %collective-permute-start) | collective-permute-done | bytes 131104 | tf_op jit(solution)/shard_map/ppermute | solution.py:218
  3.9 3.9 %collective-permute-start.1 = (bf16[2,128,128]{2,1,0:T(8,128)(2,1)S(1)}, bf16[2,128,128]{2,1,0:T(8,128)(2,1)S(1)}, u32[]{:S(2)}, u32[]{:S(2)}) collective-permute-start(bf16[2,128,128]{2,1,0:T(8,128)(2,1)S(1)} %get-tuple-element.108), channel_id=1, source_target_pairs={{0,6},{2,4},{4,2},{6,0},{8,14},{10,12},{12,10},{14,8},{1,7},{3,5},... | collective-permute-start | bytes 196616 | tf_op jit(solution)/shard_map/ppermute | solution.py:218
  8.6 1.4 %shard_map.76 = (bf16[8,128,128]{2,1,0:T(8,128)(2,1)S(1)}, f32[8,128,128]{2,1,0:T(8,128)S(1)}) custom-call(bf16[128,2048]{1,0:T(8,128)(2,1)S(1)} %copy-done, bf16[128,2048]{1,0:T(8,128)(2,1)S(1)} %get-tuple-element.172.k_ref, bf16[128,2048]{1,0:T(8,128)(2,1)S(1)} %get-tuple-element.173.v_ref, bf16[128,2048]{1,0:T(8,128)(2,1)S(1)} %copy-done.1), custom_call_target="tpu_custom_call" | custom-call | flops 67108864 | bytes 4194304 | tf_op jit(solution)/shard_map/pallas_call | solution.py:204
  10.3 1.9 %collective-permute-done.4 = bf16[2,128,128]{2,1,0:T(8,128)(2,1)S(1)} collective-permute-done((bf16[2,128,128]{2,1,0:T(8,128)(2,1)S(1)}, bf16[2,128,128]{2,1,0:T(8,128)(2,1)S(1)}, u32[]{:S(2)}, u32[]{:S(2)}) %collective-permute-start.4) | collective-permute-done | bytes 65568 | tf_op jit(solution)/shard_map/ppermute | solution.py:218
  12.8 2.7 %collective-permute-start.5 = (bf16[2,128,128]{2,1,0:T(8,128)(2,1)S(1)}, bf16[2,128,128]{2,1,0:T(8,128)(2,1)S(1)}, u32[]{:S(2)}, u32[]{:S(2)}) collective-permute-start(bf16[2,128,128]{2,1,0:T(8,128)(2,1)S(1)} %fusion.51), channel_id=1, source_target_pairs={{0,8},{2,10},{4,12},{6,14},{8,0},{10,2},{12,4},{14,6},{1,9},{3,11}... | collective-permute-start | bytes 196616 | tf_op jit(solution)/shard_map/ppermute | solution.py:218
  15.5 1.4 %shard_map.77 = (bf16[8,128,128]{2,1,0:T(8,128)(2,1)S(1)}, f32[8,128,128]{2,1,0:T(8,128)S(1)}) custom-call(bf16[128,2048]{1,0:T(8,128)(2,1)S(1)} %copy-done, bf16[128,2048]{1,0:T(8,128)(2,1)S(1)} %get-tuple-element.172.k_ref, bf16[128,2048]{1,0:T(8,128)(2,1)S(1)} %get-tuple-element.173.v_ref), custom_call_target="tpu_custom_call" | custom-call | flops 67108864 | bytes 3145728 | tf_op jit(solution)/shard_map/pallas_call | solution.py:204
  16.8 1.9 %collective-permute-done.5 = bf16[2,128,128]{2,1,0:T(8,128)(2,1)S(1)} collective-permute-done((bf16[2,128,128]{2,1,0:T(8,128)(2,1)S(1)}, bf16[2,128,128]{2,1,0:T(8,128)(2,1)S(1)}, u32[]{:S(2)}, u32[]{:S(2)}) %collective-permute-start.5) | collective-permute-done | bytes 65568 | tf_op jit(solution)/shard_map/ppermute | solution.py:218
  18.9 1.4 %collective-permute-start.6 = (bf16[2,128,128]{2,1,0:T(8,128)(2,1)S(1)}, bf16[2,128,128]{2,1,0:T(8,128)(2,1)S(1)}, u32[]{:S(2)}, u32[]{:S(2)}) collective-permute-start(bf16[2,128,128]{2,1,0:T(8,128)(2,1)S(1)} %get-tuple-element.207), channel_id=1, source_target_pairs={{0,2},{2,0},{4,6},{6,4},{8,10},{10,8},{12,14},{14,12},{1,3},{3,1},... | collective-permute-start | bytes 196616 | tf_op jit(solution)/shard_map/ppermute | solution.py:218
  20.4 2.0 %collective-permute-start.8 = (bf16[2,128,128]{2,1,0:T(8,128)(2,1)S(1)}, bf16[2,128,128]{2,1,0:T(8,128)(2,1)S(1)}, u32[]{:S(2)}, u32[]{:S(2)}) collective-permute-start(bf16[2,128,128]{2,1,0:T(8,128)(2,1)S(1)} %get-tuple-element.209), channel_id=1, source_target_pairs={{0,4},{2,6},{4,0},{6,2},{8,12},{10,14},{12,8},{14,10},{1,5},{3,7},... | collective-permute-start | bytes 196616 | tf_op jit(solution)/shard_map/ppermute | solution.py:218
  22.4 0.8 %collective-permute-done.6 = bf16[2,128,128]{2,1,0:T(8,128)(2,1)S(1)} collective-permute-done((bf16[2,128,128]{2,1,0:T(8,128)(2,1)S(1)}, bf16[2,128,128]{2,1,0:T(8,128)(2,1)S(1)}, u32[]{:S(2)}, u32[]{:S(2)}) %collective-permute-start.6) | collective-permute-done | bytes 65568 | tf_op jit(solution)/shard_map/ppermute | solution.py:218
  23.2 2.3 %collective-permute-done.7 = bf16[2,128,128]{2,1,0:T(8,128)(2,1)S(1)} collective-permute-done((bf16[2,128,128]{2,1,0:T(8,128)(2,1)S(1)}, bf16[2,128,128]{2,1,0:T(8,128)(2,1)S(1)}, u32[]{:S(2)}, u32[]{:S(2)}) %collective-permute-start.7) | collective-permute-done | bytes 65568 | tf_op jit(solution)/shard_map/ppermute | solution.py:218
  29.6 2.0 %collective-permute-start.15 = (bf16[2,128,128]{2,1,0:T(8,128)(2,1)S(1)}, bf16[2,128,128]{2,1,0:T(8,128)(2,1)S(1)}, u32[]{:S(2)}, u32[]{:S(2)}) collective-permute-start(bf16[2,128,128]{2,1,0:T(8,128)(2,1)S(1)} %get-tuple-element.152), channel_id=1, source_target_pairs={{0,6},{2,4},{4,2},{6,0},{8,14},{10,12},{12,10},{14,8},{1,7},{3,5},... | collective-permute-start | bytes 196616 | tf_op jit(solution)/shard_map/ppermute | solution.py:218
  32.3 0.9 %collective-permute-start.14 = (bf16[2,128,128]{2,1,0:T(8,128)(2,1)S(1)}, bf16[2,128,128]{2,1,0:T(8,128)(2,1)S(1)}, u32[]{:S(2)}, u32[]{:S(2)}) collective-permute-start(bf16[2,128,128]{2,1,0:T(8,128)(2,1)S(1)} %get-tuple-element.210), channel_id=1, source_target_pairs={{0,2},{2,0},{4,6},{6,4},{8,10},{10,8},{12,14},{14,12},{1,3},{3,1},... | collective-permute-start | bytes 196616 | tf_op jit(solution)/shard_map/ppermute | solution.py:218
  33.2 2.1 %shard_map.82 = (f32[8,128,128]{2,1,0:T(8,128)S(1)}, f32[8,128,128]{2,1,0:T(8,128)S(1)}, bf16[128,2048]{1,0:T(8,128)(2,1)}, bf16[128,2048]{1,0:T(8,128)(2,1)}) custom-call(bf16[128,2048]{1,0:T(8,128)(2,1)S(1)} %copy-done, bf16[128,2048]{1,0:T(8,128)(2,1)S(1)} %get-tuple-element.172.k_ref, bf16[128,2048]{1,0:T(8,128)(2,1)S(1)} %get-tuple-element.173.v_ref, ...), custom_call_target="tpu_custom_call" | custom-call | flops 167772160 | bytes 5242880 | tf_op jit(solution)/shard_map/pallas_call | solution.py:204
  36.6 2.1 %collective-permute-start.16 = (bf16[2,128,128]{2,1,0:T(8,128)(2,1)S(1)}, bf16[2,128,128]{2,1,0:T(8,128)(2,1)S(1)}, u32[]{:S(2)}, u32[]{:S(2)}) collective-permute-start(bf16[2,128,128]{2,1,0:T(8,128)(2,1)S(1)} %fusion.53), channel_id=1, source_target_pairs={{0,8},{2,10},{4,12},{6,14},{8,0},{10,2},{12,4},{14,6},{1,9},{3,11}... | collective-permute-start | bytes 196616 | tf_op jit(solution)/shard_map/ppermute | solution.py:218
  38.7 2.1 %shard_map.83 = (f32[8,128,128]{2,1,0:T(8,128)S(1)}, f32[8,128,128]{2,1,0:T(8,128)S(1)}, bf16[128,2048]{1,0:T(8,128)(2,1)}, bf16[128,2048]{1,0:T(8,128)(2,1)}) custom-call(bf16[128,2048]{1,0:T(8,128)(2,1)S(1)} %copy-done, bf16[128,2048]{1,0:T(8,128)(2,1)S(1)} %get-tuple-element.172.k_ref, ...), custom_call_target="tpu_custom_call", output_to_operand_aliasing={{2}: (10, {}), {3}: (11, {})} | custom-call | flops 167772160 | bytes 5242880 | tf_op jit(solution)/shard_map/pallas_call | solution.py:204
  40.8 1.1 %collective-permute-done.16 = bf16[2,128,128]{2,1,0:T(8,128)(2,1)S(1)} collective-permute-done((bf16[2,128,128]{2,1,0:T(8,128)(2,1)S(1)}, bf16[2,128,128]{2,1,0:T(8,128)(2,1)S(1)}, u32[]{:S(2)}, u32[]{:S(2)}) %collective-permute-start.16) | collective-permute-done | bytes 65568 | tf_op jit(solution)/shard_map/ppermute | solution.py:218
  42.0 1.7 %collective-permute-start.17 = (bf16[2,128,128]{2,1,0:T(8,128)(2,1)S(1)}, bf16[2,128,128]{2,1,0:T(8,128)(2,1)S(1)}, u32[]{:S(2)}, u32[]{:S(2)}) collective-permute-start(bf16[2,128,128]{2,1,0:T(8,128)(2,1)S(1)} %get-tuple-element.204), channel_id=1, source_target_pairs={{0,2},{2,0},{4,6},{6,4},{8,10},{10,8},{12,14},{14,12},{1,3},{3,1},... | collective-permute-start | bytes 196616 | tf_op jit(solution)/shard_map/ppermute | solution.py:218
  43.6 1.2 %collective-permute-start.18 = (bf16[2,128,128]{2,1,0:T(8,128)(2,1)S(1)}, bf16[2,128,128]{2,1,0:T(8,128)(2,1)S(1)}, u32[]{:S(2)}, u32[]{:S(2)}) collective-permute-start(bf16[2,128,128]{2,1,0:T(8,128)(2,1)S(1)} %get-tuple-element.205), channel_id=1, source_target_pairs={{0,6},{2,4},{4,2},{6,0},{8,14},{10,12},{12,10},{14,8},{1,7},{3,5},... | collective-permute-start | bytes 196616 | tf_op jit(solution)/shard_map/ppermute | solution.py:218
  45.5 0.8 %collective-permute-done.17 = bf16[2,128,128]{2,1,0:T(8,128)(2,1)S(1)} collective-permute-done((bf16[2,128,128]{2,1,0:T(8,128)(2,1)S(1)}, bf16[2,128,128]{2,1,0:T(8,128)(2,1)S(1)}, u32[]{:S(2)}, u32[]{:S(2)}) %collective-permute-start.17) | collective-permute-done | bytes 65568 | tf_op jit(solution)/shard_map/ppermute | solution.py:218
  46.3 2.5 %collective-permute-done.18 = bf16[2,128,128]{2,1,0:T(8,128)(2,1)S(1)} collective-permute-done((bf16[2,128,128]{2,1,0:T(8,128)(2,1)S(1)}, bf16[2,128,128]{2,1,0:T(8,128)(2,1)S(1)}, u32[]{:S(2)}, u32[]{:S(2)}) %collective-permute-start.18) | collective-permute-done | bytes 65568 | tf_op jit(solution)/shard_map/ppermute | solution.py:218
  49.7 1.1 %collective-permute-done.20.rest_0_ = bf16[8,128,128]{2,1,0:T(8,128)(2,1)S(1)} collective-permute-done((bf16[8,128,128]{2,1,0:T(8,128)(2,1)S(1)}, bf16[8,128,128]{2,1,0:T(8,128)(2,1)S(1)}, u32[]{:S(2)}, u32[]{:S(2)}) %collective-permute-start.20) | collective-permute-done | bytes 262176 | tf_op jit(solution)/shard_map/ppermute | solution.py:218
  50.8 1.2 %shard_map.85 = (bf16[128,2048]{1,0:T(8,128)(2,1)}, bf16[128,2048]{1,0:T(8,128)(2,1)}) custom-call(bf16[128,2048]{1,0:T(8,128)(2,1)S(1)} %get-tuple-element.172.k_ref, bf16[128,2048]{1,0:T(8,128)(2,1)S(1)} %get-tuple-element.173.v_ref, f32[8,128,128]{2,1,0:T(8,128)S(1)} %get-tuple-element.188.gk_ref, f32[8,128,128]{2,1,0:T(8,128)S(1)} %get-tuple-element.189.gv_ref, ...), custom_call_target="tpu_custom_call" | custom-call | flops 67108864 | bytes 5767168 | tf_op jit(solution)/shard_map/pallas_call | solution.py:204
  (55 shorter events, 10.5 us)
Async XLA Ops:
  0.6 8.0 %copy-start.1 = (bf16[128,2048]{1,0:T(8,128)(2,1)S(1)}, bf16[128,2048]{1,0:T(8,128)(2,1)}, u32[]{:S(2)}) copy-start(bf16[128,2048]{1,0:T(8,128)(2,1)} %g_ref.7) | copy-start | bytes 1572868
  2.4 6.2 %copy-start = (bf16[128,2048]{1,0:T(8,128)(2,1)S(1)}, bf16[128,2048]{1,0:T(8,128)(2,1)}, u32[]{:S(2)}) copy-start(bf16[128,2048]{1,0:T(8,128)(2,1)} %q_ref.11) | copy-start | bytes 1572868
  2.4 1.5 %collective-permute-start = (bf16[4,128,128]{2,1,0:T(8,128)(2,1)S(1)}, bf16[4,128,128]{2,1,0:T(8,128)(2,1)S(1)}, u32[]{:S(2)}, u32[]{:S(2)}) collective-permute-start(bf16[4,128,128]{2,1,0:T(8,128)(2,1)S(1)} %get-tuple-element.105), channel_id=1, source_target_pairs={{0,1},{1,0},{2,3},{3,2},{4,5},{5,4},{6,7},{7,6},{8,9},{9,8},{10,11... | collective-permute-start | bytes 393224 | tf_op jit(solution)/shard_map/ppermute | solution.py:218
  2.9 5.5 %collective-permute-start.2 = (bf16[4,128,128]{2,1,0:T(8,128)(2,1)S(1)}, bf16[4,128,128]{2,1,0:T(8,128)(2,1)S(1)}, u32[]{:S(2)}, u32[]{:S(2)}) collective-permute-start(bf16[4,128,128]{2,1,0:T(8,128)(2,1)S(1)} %get-tuple-element.118), channel_id=1, source_target_pairs={{0,1},{1,0},{2,3},{3,2},{4,5},{5,4},{6,7},{7,6},{8,9},{9,8},{10,11... | collective-permute-start | bytes 393224 | tf_op jit(solution)/shard_map/ppermute | solution.py:218
  3.9 6.3 %collective-permute-start.1 = (bf16[2,128,128]{2,1,0:T(8,128)(2,1)S(1)}, bf16[2,128,128]{2,1,0:T(8,128)(2,1)S(1)}, u32[]{:S(2)}, u32[]{:S(2)}) collective-permute-start(bf16[2,128,128]{2,1,0:T(8,128)(2,1)S(1)} %get-tuple-element.108), channel_id=1, source_target_pairs={{0,6},{2,4},{4,2},{6,0},{8,14},{10,12},{12,10},{14,8},{1,7},{3,5},... | collective-permute-start | bytes 196616 | tf_op jit(solution)/shard_map/ppermute | solution.py:218
  7.9 4.3 %collective-permute-start.4 = (bf16[2,128,128]{2,1,0:T(8,128)(2,1)S(1)}, bf16[2,128,128]{2,1,0:T(8,128)(2,1)S(1)}, u32[]{:S(2)}, u32[]{:S(2)}) collective-permute-start(bf16[2,128,128]{2,1,0:T(8,128)(2,1)S(1)} %get-tuple-element.213), channel_id=1, source_target_pairs={{0,2},{2,0},{4,6},{6,4},{8,10},{10,8},{12,14},{14,12},{1,3},{3,1},... | collective-permute-start | bytes 196616 | tf_op jit(solution)/shard_map/ppermute | solution.py:218
  8.4 4.3 %collective-permute-start.3 = (bf16[2,128,128]{2,1,0:T(8,128)(2,1)S(1)}, bf16[2,128,128]{2,1,0:T(8,128)(2,1)S(1)}, u32[]{:S(2)}, u32[]{:S(2)}) collective-permute-start(bf16[2,128,128]{2,1,0:T(8,128)(2,1)S(1)} %fusion.31), channel_id=1, source_target_pairs={{0,4},{2,6},{4,0},{6,2},{8,12},{10,14},{12,8},{14,10},{1,5},{3,7},... | collective-permute-start | bytes 196616 | tf_op jit(solution)/shard_map/ppermute | solution.py:218
  12.8 5.9 %collective-permute-start.5 = (bf16[2,128,128]{2,1,0:T(8,128)(2,1)S(1)}, bf16[2,128,128]{2,1,0:T(8,128)(2,1)S(1)}, u32[]{:S(2)}, u32[]{:S(2)}) collective-permute-start(bf16[2,128,128]{2,1,0:T(8,128)(2,1)S(1)} %fusion.51), channel_id=1, source_target_pairs={{0,8},{2,10},{4,12},{6,14},{8,0},{10,2},{12,4},{14,6},{1,9},{3,11}... | collective-permute-start | bytes 196616 | tf_op jit(solution)/shard_map/ppermute | solution.py:218
  18.9 4.3 %collective-permute-start.6 = (bf16[2,128,128]{2,1,0:T(8,128)(2,1)S(1)}, bf16[2,128,128]{2,1,0:T(8,128)(2,1)S(1)}, u32[]{:S(2)}, u32[]{:S(2)}) collective-permute-start(bf16[2,128,128]{2,1,0:T(8,128)(2,1)S(1)} %get-tuple-element.207), channel_id=1, source_target_pairs={{0,2},{2,0},{4,6},{6,4},{8,10},{10,8},{12,14},{14,12},{1,3},{3,1},... | collective-permute-start | bytes 196616 | tf_op jit(solution)/shard_map/ppermute | solution.py:218
  20.3 5.2 %collective-permute-start.7 = (bf16[2,128,128]{2,1,0:T(8,128)(2,1)S(1)}, bf16[2,128,128]{2,1,0:T(8,128)(2,1)S(1)}, u32[]{:S(2)}, u32[]{:S(2)}) collective-permute-start(bf16[2,128,128]{2,1,0:T(8,128)(2,1)S(1)} %get-tuple-element.208), channel_id=1, source_target_pairs={{0,6},{2,4},{4,2},{6,0},{8,14},{10,12},{12,10},{14,8},{1,7},{3,5},... | collective-permute-start | bytes 196616 | tf_op jit(solution)/shard_map/ppermute | solution.py:218
  20.4 5.1 %collective-permute-start.8 = (bf16[2,128,128]{2,1,0:T(8,128)(2,1)S(1)}, bf16[2,128,128]{2,1,0:T(8,128)(2,1)S(1)}, u32[]{:S(2)}, u32[]{:S(2)}) collective-permute-start(bf16[2,128,128]{2,1,0:T(8,128)(2,1)S(1)} %get-tuple-element.209), channel_id=1, source_target_pairs={{0,4},{2,6},{4,0},{6,2},{8,12},{10,14},{12,8},{14,10},{1,5},{3,7},... | collective-permute-start | bytes 196616 | tf_op jit(solution)/shard_map/ppermute | solution.py:218
  25.6 1.4 %collective-permute-start.10 = (bf16[4,128,128]{2,1,0:T(8,128)(2,1)S(1)}, bf16[4,128,128]{2,1,0:T(8,128)(2,1)S(1)}, u32[]{:S(2)}, u32[]{:S(2)}) collective-permute-start(bf16[4,128,128]{2,1,0:T(8,128)(2,1)S(1)} %get-tuple-element.134), channel_id=1, source_target_pairs={{0,1},{1,0},{2,3},{3,2},{4,5},{5,4},{6,7},{7,6},{8,9},{9,8},{10,11... | collective-permute-start | bytes 393224 | tf_op jit(solution)/shard_map/ppermute | solution.py:218
  25.8 1.8 %collective-permute-start.9 = (bf16[4,128,128]{2,1,0:T(8,128)(2,1)S(1)}, bf16[4,128,128]{2,1,0:T(8,128)(2,1)S(1)}, u32[]{:S(2)}, u32[]{:S(2)}) collective-permute-start(bf16[4,128,128]{2,1,0:T(8,128)(2,1)S(1)} %pad_maximum_fusion.3), channel_id=1, source_target_pairs={{0,1},{1,0},{2,3},{3,2},{4,5},{5,4},{6,7},{7,6},{8,9},{9,8},{10,11... | collective-permute-start | bytes 393224 | tf_op jit(solution)/shard_map/ppermute | solution.py:218
  28.1 1.4 %collective-permute-start.13 = (bf16[4,128,128]{2,1,0:T(8,128)(2,1)S(1)}, bf16[4,128,128]{2,1,0:T(8,128)(2,1)S(1)}, u32[]{:S(2)}, u32[]{:S(2)}) collective-permute-start(bf16[4,128,128]{2,1,0:T(8,128)(2,1)S(1)} %get-tuple-element.146), channel_id=1, source_target_pairs={{0,1},{1,0},{2,3},{3,2},{4,5},{5,4},{6,7},{7,6},{8,9},{9,8},{10,11... | collective-permute-start | bytes 393224 | tf_op jit(solution)/shard_map/ppermute | solution.py:218
  28.3 3.2 %collective-permute-start.11 = (bf16[4,128,128]{2,1,0:T(8,128)(2,1)S(1)}, bf16[4,128,128]{2,1,0:T(8,128)(2,1)S(1)}, u32[]{:S(2)}, u32[]{:S(2)}) collective-permute-start(bf16[4,128,128]{2,1,0:T(8,128)(2,1)S(1)} %get-tuple-element.144), channel_id=1, source_target_pairs={{0,1},{1,0},{2,3},{3,2},{4,5},{5,4},{6,7},{7,6},{8,9},{9,8},{10,11... | collective-permute-start | bytes 393224 | tf_op jit(solution)/shard_map/ppermute | solution.py:218
  29.6 5.9 %collective-permute-start.15 = (bf16[2,128,128]{2,1,0:T(8,128)(2,1)S(1)}, bf16[2,128,128]{2,1,0:T(8,128)(2,1)S(1)}, u32[]{:S(2)}, u32[]{:S(2)}) collective-permute-start(bf16[2,128,128]{2,1,0:T(8,128)(2,1)S(1)} %get-tuple-element.152), channel_id=1, source_target_pairs={{0,6},{2,4},{4,2},{6,0},{8,14},{10,12},{12,10},{14,8},{1,7},{3,5},... | collective-permute-start | bytes 196616 | tf_op jit(solution)/shard_map/ppermute | solution.py:218
  31.5 4.3 %collective-permute-start.12 = (bf16[2,128,128]{2,1,0:T(8,128)(2,1)S(1)}, bf16[2,128,128]{2,1,0:T(8,128)(2,1)S(1)}, u32[]{:S(2)}, u32[]{:S(2)}) collective-permute-start(bf16[2,128,128]{2,1,0:T(8,128)(2,1)S(1)} %fusion.41), channel_id=1, source_target_pairs={{0,4},{2,6},{4,0},{6,2},{8,12},{10,14},{12,8},{14,10},{1,5},{3,7},... | collective-permute-start | bytes 196616 | tf_op jit(solution)/shard_map/ppermute | solution.py:218
  32.3 4.3 %collective-permute-start.14 = (bf16[2,128,128]{2,1,0:T(8,128)(2,1)S(1)}, bf16[2,128,128]{2,1,0:T(8,128)(2,1)S(1)}, u32[]{:S(2)}, u32[]{:S(2)}) collective-permute-start(bf16[2,128,128]{2,1,0:T(8,128)(2,1)S(1)} %get-tuple-element.210), channel_id=1, source_target_pairs={{0,2},{2,0},{4,6},{6,4},{8,10},{10,8},{12,14},{14,12},{1,3},{3,1},... | collective-permute-start | bytes 196616 | tf_op jit(solution)/shard_map/ppermute | solution.py:218
  36.6 5.2 %collective-permute-start.16 = (bf16[2,128,128]{2,1,0:T(8,128)(2,1)S(1)}, bf16[2,128,128]{2,1,0:T(8,128)(2,1)S(1)}, u32[]{:S(2)}, u32[]{:S(2)}) collective-permute-start(bf16[2,128,128]{2,1,0:T(8,128)(2,1)S(1)} %fusion.53), channel_id=1, source_target_pairs={{0,8},{2,10},{4,12},{6,14},{8,0},{10,2},{12,4},{14,6},{1,9},{3,11}... | collective-permute-start | bytes 196616 | tf_op jit(solution)/shard_map/ppermute | solution.py:218
  42.0 4.3 %collective-permute-start.17 = (bf16[2,128,128]{2,1,0:T(8,128)(2,1)S(1)}, bf16[2,128,128]{2,1,0:T(8,128)(2,1)S(1)}, u32[]{:S(2)}, u32[]{:S(2)}) collective-permute-start(bf16[2,128,128]{2,1,0:T(8,128)(2,1)S(1)} %get-tuple-element.204), channel_id=1, source_target_pairs={{0,2},{2,0},{4,6},{6,4},{8,10},{10,8},{12,14},{14,12},{1,3},{3,1},... | collective-permute-start | bytes 196616 | tf_op jit(solution)/shard_map/ppermute | solution.py:218
  43.6 5.2 %collective-permute-start.18 = (bf16[2,128,128]{2,1,0:T(8,128)(2,1)S(1)}, bf16[2,128,128]{2,1,0:T(8,128)(2,1)S(1)}, u32[]{:S(2)}, u32[]{:S(2)}) collective-permute-start(bf16[2,128,128]{2,1,0:T(8,128)(2,1)S(1)} %get-tuple-element.205), channel_id=1, source_target_pairs={{0,6},{2,4},{4,2},{6,0},{8,14},{10,12},{12,10},{14,8},{1,7},{3,5},... | collective-permute-start | bytes 196616 | tf_op jit(solution)/shard_map/ppermute | solution.py:218
  44.8 4.3 %collective-permute-start.19 = (bf16[2,128,128]{2,1,0:T(8,128)(2,1)S(1)}, bf16[2,128,128]{2,1,0:T(8,128)(2,1)S(1)}, u32[]{:S(2)}, u32[]{:S(2)}) collective-permute-start(bf16[2,128,128]{2,1,0:T(8,128)(2,1)S(1)} %get-tuple-element.206), channel_id=1, source_target_pairs={{0,4},{2,6},{4,0},{6,2},{8,12},{10,14},{12,8},{14,10},{1,5},{3,7},... | collective-permute-start | bytes 196616 | tf_op jit(solution)/shard_map/ppermute | solution.py:218
  49.2 1.6 %collective-permute-start.20 = (bf16[8,128,128]{2,1,0:T(8,128)(2,1)S(1)}, bf16[8,128,128]{2,1,0:T(8,128)(2,1)S(1)}, u32[]{:S(2)}, u32[]{:S(2)}) collective-permute-start(bf16[8,128,128]{2,1,0:T(8,128)(2,1)S(1)} %pad_maximum_fusion), channel_id=1, source_target_pairs={{0,1},{1,0},{2,3},{3,2},{4,5},{5,4},{6,7},{7,6},{8,9},{9,8},{10,11... | collective-permute-start | bytes 786440 | tf_op jit(solution)/shard_map/ppermute | solution.py:218

commit v8 on v7

--- a/solution.py
+++ b/solution.py
@@ -336,9 +336,11 @@
     normed = [[None, None], [None, None]]
     early, late = BACK
     normed[0][early] = norm(early, 0, near[early])
-    far[early], normed[0][early] = lax.optimization_barrier((far[early], normed[0][early]))
+    far, normed[0][early] = lax.optimization_barrier((far, normed[0][early]))
     for part in BACK:
         normed[1][part] = norm(part, 1, far[part])
+        if part == early:
+            far[late], normed[1][part] = lax.optimization_barrier((far[late], normed[1][part]))
     near[late], normed[1] = lax.optimization_barrier((near[late], normed[1]))
     normed[0][late] = norm(late, 0, near[late])
     partials = ()

time: 52.2 us -> 52.5 us (level)
  transfers between devices with their start and end apart: 21 -> 21, of which waited for: 17 -> 18; matrix products, arithmetic and copies ran while one was open for 1% -> 1% of each run, Pallas kernels for 17% -> 16%
where the time goes in v8:
time: 52.5 us; the launch traced here: 52.3 us
  starting transfers between devices  21.9 us (42%)
  waiting for transfers between devices  16.4 us (31%)
  Pallas kernels  12.3 us (23%)
  other arithmetic  0.9 us (2%)
  between operations  0.87 us (2%)
    ppermute x21, starting transfers between devices, swap(): return lax.ppermute(value, axes, pairs)  21.9 us
    ppermute x21, waiting for transfers between devices, swap(): return lax.ppermute(value, axes, pairs)  16.4 us
    pallas_call x11, Pallas kernels, call(): pl.pallas_call(body, out_shape=outs, in_specs=in_specs, out_specs=[anywhe...  12.3 us
  transfers between devices with their start and end apart: 21, of which 18 were waited for; matrix products, arithmetic and copies ran while one was open for 1% of the time, Pallas kernels for 16%

profile of v8, /device:TPU:0, one launch (start us, length us, event | category | flops | bytes accessed | tf_op | source)
XLA Modules:
  0.0 52.3 jit_solution(10247917580437919393)
XLA Ops:
  0.6 1.7 %shard_map.75 = (bf16[4,128,128]{2,1,0:T(8,128)(2,1)S(1)}, bf16[4,128,128]{2,1,0:T(8,128)(2,1)S(1)}, f32[4,128,128]{2,1,0:T(8,128)S(1)}, f32[4,128,128]{2,1,0:T(...) custom-call(bf16[128,2048]{1,0:T(8,128)(2,1)} %k_ref.1, ...), custom_call_target="tpu_custom_call" | custom-call | flops 67108864 | bytes 2097152 | tf_op jit(solution)/shard_map/pallas_call | solution.py:204
  3.0 0.9 %collective-permute-done = bf16[4,128,128]{2,1,0:T(8,128)(2,1)S(1)} collective-permute-done((bf16[4,128,128]{2,1,0:T(8,128)(2,1)S(1)}, bf16[4,128,128]{2,1,0:T(8,128)(2,1)S(1)}, u32[]{:S(2)}, u32[]{:S(2)}) %collective-permute-start) | collective-permute-done | bytes 131104 | tf_op jit(solution)/shard_map/ppermute | solution.py:218
  3.9 3.9 %collective-permute-start.1 = (bf16[2,128,128]{2,1,0:T(8,128)(2,1)S(1)}, bf16[2,128,128]{2,1,0:T(8,128)(2,1)S(1)}, u32[]{:S(2)}, u32[]{:S(2)}) collective-permute-start(bf16[2,128,128]{2,1,0:T(8,128)(2,1)S(1)} %get-tuple-element.113), channel_id=1, source_target_pairs={{0,6},{2,4},{4,2},{6,0},{8,14},{10,12},{12,10},{14,8},{1,7},{3,5},... | collective-permute-start | bytes 196616 | tf_op jit(solution)/shard_map/ppermute | solution.py:218
  8.6 1.4 %shard_map.76 = (bf16[8,128,128]{2,1,0:T(8,128)(2,1)S(1)}, f32[8,128,128]{2,1,0:T(8,128)S(1)}) custom-call(bf16[128,2048]{1,0:T(8,128)(2,1)S(1)} %copy-done, bf16[128,2048]{1,0:T(8,128)(2,1)S(1)} %get-tuple-element.182.k_ref, bf16[128,2048]{1,0:T(8,128)(2,1)S(1)} %get-tuple-element.183.v_ref, bf16[128,2048]{1,0:T(8,128)(2,1)S(1)} %copy-done.1), custom_call_target="tpu_custom_call" | custom-call | flops 67108864 | bytes 4194304 | tf_op jit(solution)/shard_map/pallas_call | solution.py:204
  10.3 1.9 %collective-permute-done.4 = bf16[2,128,128]{2,1,0:T(8,128)(2,1)S(1)} collective-permute-done((bf16[2,128,128]{2,1,0:T(8,128)(2,1)S(1)}, bf16[2,128,128]{2,1,0:T(8,128)(2,1)S(1)}, u32[]{:S(2)}, u32[]{:S(2)}) %collective-permute-start.4) | collective-permute-done | bytes 65568 | tf_op jit(solution)/shard_map/ppermute | solution.py:218
  12.8 2.7 %collective-permute-start.5 = (bf16[2,128,128]{2,1,0:T(8,128)(2,1)S(1)}, bf16[2,128,128]{2,1,0:T(8,128)(2,1)S(1)}, u32[]{:S(2)}, u32[]{:S(2)}) collective-permute-start(bf16[2,128,128]{2,1,0:T(8,128)(2,1)S(1)} %fusion.51), channel_id=1, source_target_pairs={{0,8},{2,10},{4,12},{6,14},{8,0},{10,2},{12,4},{14,6},{1,9},{3,11}... | collective-permute-start | bytes 196616 | tf_op jit(solution)/shard_map/ppermute | solution.py:218
  15.5 1.4 %shard_map.77 = (bf16[8,128,128]{2,1,0:T(8,128)(2,1)S(1)}, f32[8,128,128]{2,1,0:T(8,128)S(1)}) custom-call(bf16[128,2048]{1,0:T(8,128)(2,1)S(1)} %copy-done, bf16[128,2048]{1,0:T(8,128)(2,1)S(1)} %get-tuple-element.182.k_ref, bf16[128,2048]{1,0:T(8,128)(2,1)S(1)} %get-tuple-element.183.v_ref), custom_call_target="tpu_custom_call" | custom-call | flops 67108864 | bytes 3145728 | tf_op jit(solution)/shard_map/pallas_call | solution.py:204
  16.8 1.9 %collective-permute-done.5 = bf16[2,128,128]{2,1,0:T(8,128)(2,1)S(1)} collective-permute-done((bf16[2,128,128]{2,1,0:T(8,128)(2,1)S(1)}, bf16[2,128,128]{2,1,0:T(8,128)(2,1)S(1)}, u32[]{:S(2)}, u32[]{:S(2)}) %collective-permute-start.5) | collective-permute-done | bytes 65568 | tf_op jit(solution)/shard_map/ppermute | solution.py:218
  18.9 1.4 %collective-permute-start.6 = (bf16[2,128,128]{2,1,0:T(8,128)(2,1)S(1)}, bf16[2,128,128]{2,1,0:T(8,128)(2,1)S(1)}, u32[]{:S(2)}, u32[]{:S(2)}) collective-permute-start(bf16[2,128,128]{2,1,0:T(8,128)(2,1)S(1)} %get-tuple-element.217), channel_id=1, source_target_pairs={{0,2},{2,0},{4,6},{6,4},{8,10},{10,8},{12,14},{14,12},{1,3},{3,1},... | collective-permute-start | bytes 196616 | tf_op jit(solution)/shard_map/ppermute | solution.py:218
  20.4 2.0 %collective-permute-start.8 = (bf16[2,128,128]{2,1,0:T(8,128)(2,1)S(1)}, bf16[2,128,128]{2,1,0:T(8,128)(2,1)S(1)}, u32[]{:S(2)}, u32[]{:S(2)}) collective-permute-start(bf16[2,128,128]{2,1,0:T(8,128)(2,1)S(1)} %get-tuple-element.219), channel_id=1, source_target_pairs={{0,4},{2,6},{4,0},{6,2},{8,12},{10,14},{12,8},{14,10},{1,5},{3,7},... | collective-permute-start | bytes 196616 | tf_op jit(solution)/shard_map/ppermute | solution.py:218
  22.4 0.8 %collective-permute-done.6 = bf16[2,128,128]{2,1,0:T(8,128)(2,1)S(1)} collective-permute-done((bf16[2,128,128]{2,1,0:T(8,128)(2,1)S(1)}, bf16[2,128,128]{2,1,0:T(8,128)(2,1)S(1)}, u32[]{:S(2)}, u32[]{:S(2)}) %collective-permute-start.6) | collective-permute-done | bytes 65568 | tf_op jit(solution)/shard_map/ppermute | solution.py:218
  23.2 2.3 %collective-permute-done.7 = bf16[2,128,128]{2,1,0:T(8,128)(2,1)S(1)} collective-permute-done((bf16[2,128,128]{2,1,0:T(8,128)(2,1)S(1)}, bf16[2,128,128]{2,1,0:T(8,128)(2,1)S(1)}, u32[]{:S(2)}, u32[]{:S(2)}) %collective-permute-start.7) | collective-permute-done | bytes 65568 | tf_op jit(solution)/shard_map/ppermute | solution.py:218
  29.8 2.0 %collective-permute-start.15 = (bf16[2,128,128]{2,1,0:T(8,128)(2,1)S(1)}, bf16[2,128,128]{2,1,0:T(8,128)(2,1)S(1)}, u32[]{:S(2)}, u32[]{:S(2)}) collective-permute-start(bf16[2,128,128]{2,1,0:T(8,128)(2,1)S(1)} %get-tuple-element.162), channel_id=1, source_target_pairs={{0,6},{2,4},{4,2},{6,0},{8,14},{10,12},{12,10},{14,8},{1,7},{3,5},... | collective-permute-start | bytes 196616 | tf_op jit(solution)/shard_map/ppermute | solution.py:218
  32.6 0.9 %collective-permute-start.14 = (bf16[2,128,128]{2,1,0:T(8,128)(2,1)S(1)}, bf16[2,128,128]{2,1,0:T(8,128)(2,1)S(1)}, u32[]{:S(2)}, u32[]{:S(2)}) collective-permute-start(bf16[2,128,128]{2,1,0:T(8,128)(2,1)S(1)} %get-tuple-element.220), channel_id=1, source_target_pairs={{0,2},{2,0},{4,6},{6,4},{8,10},{10,8},{12,14},{14,12},{1,3},{3,1},... | collective-permute-start | bytes 196616 | tf_op jit(solution)/shard_map/ppermute | solution.py:218
  33.5 2.1 %shard_map.82 = (f32[8,128,128]{2,1,0:T(8,128)S(1)}, f32[8,128,128]{2,1,0:T(8,128)S(1)}, bf16[128,2048]{1,0:T(8,128)(2,1)}, bf16[128,2048]{1,0:T(8,128)(2,1)}) custom-call(bf16[128,2048]{1,0:T(8,128)(2,1)S(1)} %copy-done, bf16[128,2048]{1,0:T(8,128)(2,1)S(1)} %get-tuple-element.182.k_ref, bf16[128,2048]{1,0:T(8,128)(2,1)S(1)} %get-tuple-element.183.v_ref, ...), custom_call_target="tpu_custom_call" | custom-call | flops 167772160 | bytes 5242880 | tf_op jit(solution)/shard_map/pallas_call | solution.py:204
  36.9 2.1 %collective-permute-start.16 = (bf16[2,128,128]{2,1,0:T(8,128)(2,1)S(1)}, bf16[2,128,128]{2,1,0:T(8,128)(2,1)S(1)}, u32[]{:S(2)}, u32[]{:S(2)}) collective-permute-start(bf16[2,128,128]{2,1,0:T(8,128)(2,1)S(1)} %fusion.53), channel_id=1, source_target_pairs={{0,8},{2,10},{4,12},{6,14},{8,0},{10,2},{12,4},{14,6},{1,9},{3,11}... | collective-permute-start | bytes 196616 | tf_op jit(solution)/shard_map/ppermute | solution.py:218
  39.0 2.1 %shard_map.83 = (f32[8,128,128]{2,1,0:T(8,128)S(1)}, f32[8,128,128]{2,1,0:T(8,128)S(1)}, bf16[128,2048]{1,0:T(8,128)(2,1)}, bf16[128,2048]{1,0:T(8,128)(2,1)}) custom-call(bf16[128,2048]{1,0:T(8,128)(2,1)S(1)} %copy-done, bf16[128,2048]{1,0:T(8,128)(2,1)S(1)} %get-tuple-element.182.k_ref, ...), custom_call_target="tpu_custom_call", output_to_operand_aliasing={{2}: (10, {}), {3}: (11, {})} | custom-call | flops 167772160 | bytes 5242880 | tf_op jit(solution)/shard_map/pallas_call | solution.py:204
  41.0 1.1 %collective-permute-done.16 = bf16[2,128,128]{2,1,0:T(8,128)(2,1)S(1)} collective-permute-done((bf16[2,128,128]{2,1,0:T(8,128)(2,1)S(1)}, bf16[2,128,128]{2,1,0:T(8,128)(2,1)S(1)}, u32[]{:S(2)}, u32[]{:S(2)}) %collective-permute-start.16) | collective-permute-done | bytes 65568 | tf_op jit(solution)/shard_map/ppermute | solution.py:218
  42.3 1.0 %collective-permute-start.17 = (bf16[2,128,128]{2,1,0:T(8,128)(2,1)S(1)}, bf16[2,128,128]{2,1,0:T(8,128)(2,1)S(1)}, u32[]{:S(2)}, u32[]{:S(2)}) collective-permute-start(bf16[2,128,128]{2,1,0:T(8,128)(2,1)S(1)} %get-tuple-element.214), channel_id=1, source_target_pairs={{0,2},{2,0},{4,6},{6,4},{8,10},{10,8},{12,14},{14,12},{1,3},{3,1},... | collective-permute-start | bytes 196616 | tf_op jit(solution)/shard_map/ppermute | solution.py:218
  43.2 1.9 %collective-permute-start.18 = (bf16[2,128,128]{2,1,0:T(8,128)(2,1)S(1)}, bf16[2,128,128]{2,1,0:T(8,128)(2,1)S(1)}, u32[]{:S(2)}, u32[]{:S(2)}) collective-permute-start(bf16[2,128,128]{2,1,0:T(8,128)(2,1)S(1)} %get-tuple-element.215), channel_id=1, source_target_pairs={{0,6},{2,4},{4,2},{6,0},{8,14},{10,12},{12,10},{14,8},{1,7},{3,5},... | collective-permute-start | bytes 196616 | tf_op jit(solution)/shard_map/ppermute | solution.py:218
  46.6 1.8 %collective-permute-done.18 = bf16[2,128,128]{2,1,0:T(8,128)(2,1)S(1)} collective-permute-done((bf16[2,128,128]{2,1,0:T(8,128)(2,1)S(1)}, bf16[2,128,128]{2,1,0:T(8,128)(2,1)S(1)}, u32[]{:S(2)}, u32[]{:S(2)}) %collective-permute-start.18) | collective-permute-done | bytes 65568 | tf_op jit(solution)/shard_map/ppermute | solution.py:218
  48.5 0.9 %collective-permute-done.19 = bf16[2,128,128]{2,1,0:T(8,128)(2,1)S(1)} collective-permute-done((bf16[2,128,128]{2,1,0:T(8,128)(2,1)S(1)}, bf16[2,128,128]{2,1,0:T(8,128)(2,1)S(1)}, u32[]{:S(2)}, u32[]{:S(2)}) %collective-permute-start.19) | collective-permute-done | bytes 65568 | tf_op jit(solution)/shard_map/ppermute | solution.py:218
  50.0 1.1 %collective-permute-done.20.rest_0_ = bf16[8,128,128]{2,1,0:T(8,128)(2,1)S(1)} collective-permute-done((bf16[8,128,128]{2,1,0:T(8,128)(2,1)S(1)}, bf16[8,128,128]{2,1,0:T(8,128)(2,1)S(1)}, u32[]{:S(2)}, u32[]{:S(2)}) %collective-permute-start.20) | collective-permute-done | bytes 262176 | tf_op jit(solution)/shard_map/ppermute | solution.py:218
  51.1 1.2 %shard_map.85 = (bf16[128,2048]{1,0:T(8,128)(2,1)}, bf16[128,2048]{1,0:T(8,128)(2,1)}) custom-call(bf16[128,2048]{1,0:T(8,128)(2,1)S(1)} %get-tuple-element.182.k_ref, bf16[128,2048]{1,0:T(8,128)(2,1)S(1)} %get-tuple-element.183.v_ref, f32[8,128,128]{2,1,0:T(8,128)S(1)} %get-tuple-element.198.gk_ref, f32[8,128,128]{2,1,0:T(8,128)S(1)} %get-tuple-element.199.gv_ref, ...), custom_call_target="tpu_custom_call" | custom-call | flops 67108864 | bytes 5767168 | tf_op jit(solution)/shard_map/pallas_call | solution.py:204
  (55 shorter events, 11.3 us)
Async XLA Ops:
  0.6 8.0 %copy-start.1 = (bf16[128,2048]{1,0:T(8,128)(2,1)S(1)}, bf16[128,2048]{1,0:T(8,128)(2,1)}, u32[]{:S(2)}) copy-start(bf16[128,2048]{1,0:T(8,128)(2,1)} %g_ref.7) | copy-start | bytes 1572868
  2.4 6.2 %copy-start = (bf16[128,2048]{1,0:T(8,128)(2,1)S(1)}, bf16[128,2048]{1,0:T(8,128)(2,1)}, u32[]{:S(2)}) copy-start(bf16[128,2048]{1,0:T(8,128)(2,1)} %q_ref.11) | copy-start | bytes 1572868
  2.4 1.5 %collective-permute-start = (bf16[4,128,128]{2,1,0:T(8,128)(2,1)S(1)}, bf16[4,128,128]{2,1,0:T(8,128)(2,1)S(1)}, u32[]{:S(2)}, u32[]{:S(2)}) collective-permute-start(bf16[4,128,128]{2,1,0:T(8,128)(2,1)S(1)} %get-tuple-element.110), channel_id=1, source_target_pairs={{0,1},{1,0},{2,3},{3,2},{4,5},{5,4},{6,7},{7,6},{8,9},{9,8},{10,11... | collective-permute-start | bytes 393224 | tf_op jit(solution)/shard_map/ppermute | solution.py:218
  2.9 5.5 %collective-permute-start.2 = (bf16[4,128,128]{2,1,0:T(8,128)(2,1)S(1)}, bf16[4,128,128]{2,1,0:T(8,128)(2,1)S(1)}, u32[]{:S(2)}, u32[]{:S(2)}) collective-permute-start(bf16[4,128,128]{2,1,0:T(8,128)(2,1)S(1)} %get-tuple-element.123), channel_id=1, source_target_pairs={{0,1},{1,0},{2,3},{3,2},{4,5},{5,4},{6,7},{7,6},{8,9},{9,8},{10,11... | collective-permute-start | bytes 393224 | tf_op jit(solution)/shard_map/ppermute | solution.py:218
  3.9 6.3 %collective-permute-start.1 = (bf16[2,128,128]{2,1,0:T(8,128)(2,1)S(1)}, bf16[2,128,128]{2,1,0:T(8,128)(2,1)S(1)}, u32[]{:S(2)}, u32[]{:S(2)}) collective-permute-start(bf16[2,128,128]{2,1,0:T(8,128)(2,1)S(1)} %get-tuple-element.113), channel_id=1, source_target_pairs={{0,6},{2,4},{4,2},{6,0},{8,14},{10,12},{12,10},{14,8},{1,7},{3,5},... | collective-permute-start | bytes 196616 | tf_op jit(solution)/shard_map/ppermute | solution.py:218
  7.9 4.3 %collective-permute-start.4 = (bf16[2,128,128]{2,1,0:T(8,128)(2,1)S(1)}, bf16[2,128,128]{2,1,0:T(8,128)(2,1)S(1)}, u32[]{:S(2)}, u32[]{:S(2)}) collective-permute-start(bf16[2,128,128]{2,1,0:T(8,128)(2,1)S(1)} %get-tuple-element.223), channel_id=1, source_target_pairs={{0,2},{2,0},{4,6},{6,4},{8,10},{10,8},{12,14},{14,12},{1,3},{3,1},... | collective-permute-start | bytes 196616 | tf_op jit(solution)/shard_map/ppermute | solution.py:218
  8.4 4.3 %collective-permute-start.3 = (bf16[2,128,128]{2,1,0:T(8,128)(2,1)S(1)}, bf16[2,128,128]{2,1,0:T(8,128)(2,1)S(1)}, u32[]{:S(2)}, u32[]{:S(2)}) collective-permute-start(bf16[2,128,128]{2,1,0:T(8,128)(2,1)S(1)} %fusion.31), channel_id=1, source_target_pairs={{0,4},{2,6},{4,0},{6,2},{8,12},{10,14},{12,8},{14,10},{1,5},{3,7},... | collective-permute-start | bytes 196616 | tf_op jit(solution)/shard_map/ppermute | solution.py:218
  12.8 5.9 %collective-permute-start.5 = (bf16[2,128,128]{2,1,0:T(8,128)(2,1)S(1)}, bf16[2,128,128]{2,1,0:T(8,128)(2,1)S(1)}, u32[]{:S(2)}, u32[]{:S(2)}) collective-permute-start(bf16[2,128,128]{2,1,0:T(8,128)(2,1)S(1)} %fusion.51), channel_id=1, source_target_pairs={{0,8},{2,10},{4,12},{6,14},{8,0},{10,2},{12,4},{14,6},{1,9},{3,11}... | collective-permute-start | bytes 196616 | tf_op jit(solution)/shard_map/ppermute | solution.py:218
  18.9 4.3 %collective-permute-start.6 = (bf16[2,128,128]{2,1,0:T(8,128)(2,1)S(1)}, bf16[2,128,128]{2,1,0:T(8,128)(2,1)S(1)}, u32[]{:S(2)}, u32[]{:S(2)}) collective-permute-start(bf16[2,128,128]{2,1,0:T(8,128)(2,1)S(1)} %get-tuple-element.217), channel_id=1, source_target_pairs={{0,2},{2,0},{4,6},{6,4},{8,10},{10,8},{12,14},{14,12},{1,3},{3,1},... | collective-permute-start | bytes 196616 | tf_op jit(solution)/shard_map/ppermute | solution.py:218
  20.3 5.2 %collective-permute-start.7 = (bf16[2,128,128]{2,1,0:T(8,128)(2,1)S(1)}, bf16[2,128,128]{2,1,0:T(8,128)(2,1)S(1)}, u32[]{:S(2)}, u32[]{:S(2)}) collective-permute-start(bf16[2,128,128]{2,1,0:T(8,128)(2,1)S(1)} %get-tuple-element.218), channel_id=1, source_target_pairs={{0,6},{2,4},{4,2},{6,0},{8,14},{10,12},{12,10},{14,8},{1,7},{3,5},... | collective-permute-start | bytes 196616 | tf_op jit(solution)/shard_map/ppermute | solution.py:218
  20.4 5.1 %collective-permute-start.8 = (bf16[2,128,128]{2,1,0:T(8,128)(2,1)S(1)}, bf16[2,128,128]{2,1,0:T(8,128)(2,1)S(1)}, u32[]{:S(2)}, u32[]{:S(2)}) collective-permute-start(bf16[2,128,128]{2,1,0:T(8,128)(2,1)S(1)} %get-tuple-element.219), channel_id=1, source_target_pairs={{0,4},{2,6},{4,0},{6,2},{8,12},{10,14},{12,8},{14,10},{1,5},{3,7},... | collective-permute-start | bytes 196616 | tf_op jit(solution)/shard_map/ppermute | solution.py:218
  25.7 1.4 %collective-permute-start.9 = (bf16[4,128,128]{2,1,0:T(8,128)(2,1)S(1)}, bf16[4,128,128]{2,1,0:T(8,128)(2,1)S(1)}, u32[]{:S(2)}, u32[]{:S(2)}) collective-permute-start(bf16[4,128,128]{2,1,0:T(8,128)(2,1)S(1)} %pad_maximum_fusion.3), channel_id=1, source_target_pairs={{0,1},{1,0},{2,3},{3,2},{4,5},{5,4},{6,7},{7,6},{8,9},{9,8},{10,11... | collective-permute-start | bytes 393224 | tf_op jit(solution)/shard_map/ppermute | solution.py:218
  25.8 1.5 %collective-permute-start.10 = (bf16[4,128,128]{2,1,0:T(8,128)(2,1)S(1)}, bf16[4,128,128]{2,1,0:T(8,128)(2,1)S(1)}, u32[]{:S(2)}, u32[]{:S(2)}) collective-permute-start(bf16[4,128,128]{2,1,0:T(8,128)(2,1)S(1)} %get-tuple-element.136), channel_id=1, source_target_pairs={{0,1},{1,0},{2,3},{3,2},{4,5},{5,4},{6,7},{7,6},{8,9},{9,8},{10,11... | collective-permute-start | bytes 393224 | tf_op jit(solution)/shard_map/ppermute | solution.py:218
  28.4 1.4 %collective-permute-start.13 = (bf16[4,128,128]{2,1,0:T(8,128)(2,1)S(1)}, bf16[4,128,128]{2,1,0:T(8,128)(2,1)S(1)}, u32[]{:S(2)}, u32[]{:S(2)}) collective-permute-start(bf16[4,128,128]{2,1,0:T(8,128)(2,1)S(1)} %get-tuple-element.156), channel_id=1, source_target_pairs={{0,1},{1,0},{2,3},{3,2},{4,5},{5,4},{6,7},{7,6},{8,9},{9,8},{10,11... | collective-permute-start | bytes 393224 | tf_op jit(solution)/shard_map/ppermute | solution.py:218
  28.8 3.0 %collective-permute-start.11 = (bf16[4,128,128]{2,1,0:T(8,128)(2,1)S(1)}, bf16[4,128,128]{2,1,0:T(8,128)(2,1)S(1)}, u32[]{:S(2)}, u32[]{:S(2)}) collective-permute-start(bf16[4,128,128]{2,1,0:T(8,128)(2,1)S(1)} %get-tuple-element.154), channel_id=1, source_target_pairs={{0,1},{1,0},{2,3},{3,2},{4,5},{5,4},{6,7},{7,6},{8,9},{9,8},{10,11... | collective-permute-start | bytes 393224 | tf_op jit(solution)/shard_map/ppermute | solution.py:218
  29.8 5.8 %collective-permute-start.15 = (bf16[2,128,128]{2,1,0:T(8,128)(2,1)S(1)}, bf16[2,128,128]{2,1,0:T(8,128)(2,1)S(1)}, u32[]{:S(2)}, u32[]{:S(2)}) collective-permute-start(bf16[2,128,128]{2,1,0:T(8,128)(2,1)S(1)} %get-tuple-element.162), channel_id=1, source_target_pairs={{0,6},{2,4},{4,2},{6,0},{8,14},{10,12},{12,10},{14,8},{1,7},{3,5},... | collective-permute-start | bytes 196616 | tf_op jit(solution)/shard_map/ppermute | solution.py:218
  31.8 4.4 %collective-permute-start.12 = (bf16[2,128,128]{2,1,0:T(8,128)(2,1)S(1)}, bf16[2,128,128]{2,1,0:T(8,128)(2,1)S(1)}, u32[]{:S(2)}, u32[]{:S(2)}) collective-permute-start(bf16[2,128,128]{2,1,0:T(8,128)(2,1)S(1)} %fusion.41), channel_id=1, source_target_pairs={{0,4},{2,6},{4,0},{6,2},{8,12},{10,14},{12,8},{14,10},{1,5},{3,7},... | collective-permute-start | bytes 196616 | tf_op jit(solution)/shard_map/ppermute | solution.py:218
  32.6 4.3 %collective-permute-start.14 = (bf16[2,128,128]{2,1,0:T(8,128)(2,1)S(1)}, bf16[2,128,128]{2,1,0:T(8,128)(2,1)S(1)}, u32[]{:S(2)}, u32[]{:S(2)}) collective-permute-start(bf16[2,128,128]{2,1,0:T(8,128)(2,1)S(1)} %get-tuple-element.220), channel_id=1, source_target_pairs={{0,2},{2,0},{4,6},{6,4},{8,10},{10,8},{12,14},{14,12},{1,3},{3,1},... | collective-permute-start | bytes 196616 | tf_op jit(solution)/shard_map/ppermute | solution.py:218
  36.9 5.2 %collective-permute-start.16 = (bf16[2,128,128]{2,1,0:T(8,128)(2,1)S(1)}, bf16[2,128,128]{2,1,0:T(8,128)(2,1)S(1)}, u32[]{:S(2)}, u32[]{:S(2)}) collective-permute-start(bf16[2,128,128]{2,1,0:T(8,128)(2,1)S(1)} %fusion.53), channel_id=1, source_target_pairs={{0,8},{2,10},{4,12},{6,14},{8,0},{10,2},{12,4},{14,6},{1,9},{3,11}... | collective-permute-start | bytes 196616 | tf_op jit(solution)/shard_map/ppermute | solution.py:218
  42.3 4.3 %collective-permute-start.17 = (bf16[2,128,128]{2,1,0:T(8,128)(2,1)S(1)}, bf16[2,128,128]{2,1,0:T(8,128)(2,1)S(1)}, u32[]{:S(2)}, u32[]{:S(2)}) collective-permute-start(bf16[2,128,128]{2,1,0:T(8,128)(2,1)S(1)} %get-tuple-element.214), channel_id=1, source_target_pairs={{0,2},{2,0},{4,6},{6,4},{8,10},{10,8},{12,14},{14,12},{1,3},{3,1},... | collective-permute-start | bytes 196616 | tf_op jit(solution)/shard_map/ppermute | solution.py:218
  43.2 5.2 %collective-permute-start.18 = (bf16[2,128,128]{2,1,0:T(8,128)(2,1)S(1)}, bf16[2,128,128]{2,1,0:T(8,128)(2,1)S(1)}, u32[]{:S(2)}, u32[]{:S(2)}) collective-permute-start(bf16[2,128,128]{2,1,0:T(8,128)(2,1)S(1)} %get-tuple-element.215), channel_id=1, source_target_pairs={{0,6},{2,4},{4,2},{6,0},{8,14},{10,12},{12,10},{14,8},{1,7},{3,5},... | collective-permute-start | bytes 196616 | tf_op jit(solution)/shard_map/ppermute | solution.py:218
  45.1 4.3 %collective-permute-start.19 = (bf16[2,128,128]{2,1,0:T(8,128)(2,1)S(1)}, bf16[2,128,128]{2,1,0:T(8,128)(2,1)S(1)}, u32[]{:S(2)}, u32[]{:S(2)}) collective-permute-start(bf16[2,128,128]{2,1,0:T(8,128)(2,1)S(1)} %get-tuple-element.216), channel_id=1, source_target_pairs={{0,4},{2,6},{4,0},{6,2},{8,12},{10,14},{12,8},{14,10},{1,5},{3,7},... | collective-permute-start | bytes 196616 | tf_op jit(solution)/shard_map/ppermute | solution.py:218
  49.5 1.6 %collective-permute-start.20 = (bf16[8,128,128]{2,1,0:T(8,128)(2,1)S(1)}, bf16[8,128,128]{2,1,0:T(8,128)(2,1)S(1)}, u32[]{:S(2)}, u32[]{:S(2)}) collective-permute-start(bf16[8,128,128]{2,1,0:T(8,128)(2,1)S(1)} %pad_maximum_fusion), channel_id=1, source_target_pairs={{0,1},{1,0},{2,3},{3,2},{4,5},{5,4},{6,7},{7,6},{8,9},{9,8},{10,11... | collective-permute-start | bytes 786440 | tf_op jit(solution)/shard_map/ppermute | solution.py:218
